TPU v7x, 32 devices: a whole 2x2x4 slice. The times are simulated.
32 devices in a mesh: dp: 4 (over y, x), fsdp: 8 (over z, core).
Axes of the slice: x: 2, y: 2, z: 4, core: 2. Of those that a mesh axis runs over, the one named last changes fastest.
Arguments:
- layer_input: bfloat16 [64, 256, 768], P(('dp', 'fsdp')), may hold values from -6 to 6
- encoder_states: bfloat16 [64, 256, 768], P(('dp', 'fsdp')), may hold values from -6 to 6
- output_grad: bfloat16 [64, 256, 768], P(('dp', 'fsdp')), may hold values from -6 to 6
- span_start: int32 [64], P(('dp', 'fsdp')), may hold values from 0 to 128, as said below
- span_length: int32 [64], P(('dp', 'fsdp')), may hold values from 128 to 256, as said below
- self_project: bfloat16 [3, 768, 768], P(None, ('dp', 'fsdp')), may hold values from -0.21875 to 0.21875
- self_output: bfloat16 [768, 768], P(('dp', 'fsdp')), may hold values from -1.75 to 1.75
- cross_project: bfloat16 [3, 768, 768], P(None, ('dp', 'fsdp')), may hold values from -0.21875 to 0.21875
- cross_output: bfloat16 [768, 768], P(('dp', 'fsdp')), may hold values from -1.75 to 1.75
- attend_bias: bfloat16 [6, 768], P(None, ('dp', 'fsdp')), may hold values from -1.796875 to 1.796875
- expand_weight: bfloat16 [768, 3072], P(('dp', 'fsdp')), may hold values from -0.21875 to 0.21875
- expand_bias: bfloat16 [3072], P(('dp', 'fsdp')), may hold values from -1.796875 to 1.796875
- contract_weight: bfloat16 [3072, 768], P(('dp', 'fsdp')), may hold values from -0.109375 to 0.109375
- contract_bias: bfloat16 [768], P(('dp', 'fsdp')), may hold values from -1.796875 to 1.796875
- norm_gain: bfloat16 [3, 768], P(None, ('dp', 'fsdp')), may hold values from 0.25 to 1.75
- norm_shift: bfloat16 [3, 768], P(None, ('dp', 'fsdp')), may hold values from -1.796875 to 1.796875
Outputs:
- layer_output: bfloat16 [64, 256, 768], P(('dp', 'fsdp'))
- input_grad: float32 [64, 256, 768], P(('dp', 'fsdp'))
- encoder_grad: float32 [64, 256, 768], P(('dp', 'fsdp'))
- self_project_grad: float32 [3, 768, 768], P(None, ('dp', 'fsdp'))
- self_output_grad: float32 [768, 768], P(('dp', 'fsdp'))
- cross_project_grad: float32 [3, 768, 768], P(None, ('dp', 'fsdp'))
- cross_output_grad: float32 [768, 768], P(('dp', 'fsdp'))
- attend_bias_grad: float32 [6, 768], P(None, ('dp', 'fsdp'))
- expand_weight_grad: float32 [768, 3072], P(('dp', 'fsdp'))
- expand_bias_grad: float32 [3072], P(('dp', 'fsdp'))
- contract_weight_grad: float32 [3072, 768], P(('dp', 'fsdp'))
- contract_bias_grad: float32 [768], P(('dp', 'fsdp'))
- norm_gain_grad: float32 [3, 768], P(None, ('dp', 'fsdp'))
- norm_shift_grad: float32 [3, 768], P(None, ('dp', 'fsdp'))
Inputs may be any that keep to these rules, and one draw needn't show every extreme that they name: span_start + span_length <= 256 for every sequence; some sequence has its span start at 0, some at 128. `span_length`: some sequence has a span of exactly 256 tokens and some of exactly 128.
All inputs are finite; a program needn't handle non-finite values.
Results may differ from a plain program's by a relative error of at most 0.025.
Values may be sent and summed in bfloat16 or wider, within the bound.
No kernel may reach another device: no remote copies, remote signals or barrier semaphores. Data moves between devices by JAX's collectives and lax.ppermute only.
A program may use at most 256 MiB of HBM per device.

v0:
```python
import functools

import jax
import jax.numpy as jnp
import numpy as np
from jax import lax
from jax.experimental import pallas as pl
from jax.experimental.pallas import tpu as pltpu
from jax.sharding import PartitionSpec as P

D = 768
H = 12
HD = 64
FF = 3072
AXES = ("dp", "fsdp")

EPS = 1e-05
BIG_NEGATIVE = -1000000000.0
BF = jnp.bfloat16
F32 = jnp.float32
QUICK = pl.CostEstimate(flops=1000, bytes_accessed=1000, transcendentals=0)


class Place:
    def __init__(self):
        self.dp_count = lax.axis_size("dp")
        self.inner = lax.axis_size("fsdp")
        self.chips = self.inner // 2
        self.bits = int(np.log2(self.dp_count))
        self.dp = lax.axis_index("dp")
        inner = lax.axis_index("fsdp")
        self.chip = inner // 2
        self.core = inner % 2
        table = []
        for dp in range(self.dp_count):
            for chip in range(self.chips):
                for core in range(2):
                    table.append(
                        [dp ^ self.mask(core, m) for m in range(self.dp_count)]
                        + [dp ^ self.mask(1 - core, m) for m in range(self.dp_count)]
                        + [(chip + k) % self.chips for k in range(self.chips)]
                        + [(chip - k) % self.chips for k in range(self.chips)]
                        + [core, 1 - core]
                    )
        index = self.dp * self.inner + inner
        self.spots = lax.dynamic_index_in_dim(
            jnp.asarray(np.array(table, np.int32)), index, 0, keepdims=False
        )
        self.theirs_at = self.dp_count
        self.up_at = 2 * self.dp_count
        self.down_at = self.up_at + self.chips
        self.core_at = self.down_at + self.chips

    def bit(self, core, step):
        return 1 << (self.bits - 1 - step if core == 0 else step)

    def mask(self, core, relative):
        return sum(self.bit(core, s) for s in range(self.bits) if relative >> s & 1)

    def permute(self, value, target):
        pairs = []
        for dp in range(self.dp_count):
            for chip in range(self.chips):
                for core in range(2):
                    to = target(dp, chip, core)
                    pairs.append(
                        (
                            dp * self.inner + chip * 2 + core,
                            to[0] * self.inner + to[1] * 2 + to[2],
                        )
                    )
        return lax.ppermute(value, AXES, pairs)

    def across_cores(self, value):
        return self.permute(value, lambda d, z, c: (d, z, 1 - c))

    def across_step(self, value, step):
        return self.permute(value, lambda d, z, c: (d ^ self.bit(c, step), z, c))

    def along_chips(self, value, shift):
        return self.permute(value, lambda d, z, c: (d, (z + shift) % self.chips, c))


def after(values, *earlier):
    return lax.optimization_barrier((values, earlier))[0]


def copy_kernel(plan, n_in, spots_ref, *refs):
    ins, outs, sems = refs[:n_in], refs[n_in:-1], refs[-1]
    copies = []
    for i, (source, source_at, target, target_at) in enumerate(plan):
        copies.append(
            pltpu.make_async_copy(
                ins[source].at[source_at(spots_ref)],
                outs[target].at[target_at(spots_ref)],
                sems.at[i],
            )
        )
    for c in copies:
        c.start()
    for c in copies:
        c.wait()


def copy_call(place, plan, ins, outs, name):
    anywhere = pl.BlockSpec(memory_space=pl.ANY)
    return pl.pallas_call(
        functools.partial(copy_kernel, plan, len(ins)),
        grid_spec=pltpu.PrefetchScalarGridSpec(
            num_scalar_prefetch=1,
            grid=(1,),
            in_specs=[anywhere] * len(ins),
            out_specs=[anywhere] * len(outs),
            scratch_shapes=[pltpu.SemaphoreType.DMA((len(plan),))],
        ),
        out_shape=outs,
        compiler_params=pltpu.CompilerParams(vmem_limit_bytes=1 << 20),
        cost_estimate=QUICK,
        name=name,
    )(place.spots, *ins)


class Gather:
    def __init__(self, place, local):
        self.place = place
        self.local = local
        self.got = [local] + [
            place.along_chips(local, k) for k in range(1, place.chips)
        ]

    def column(self, *earlier):
        place = self.place
        self.got = after(self.got, *earlier)
        plan = [
            (
                k,
                lambda s: (slice(None),),
                0,
                lambda s, k=k: (s[place.down_at + k],),
            )
            for k in range(place.chips)
        ]
        shape = jax.ShapeDtypeStruct((place.chips,) + self.local.shape, BF)
        self.blocks = {0: copy_call(place, plan, self.got, [shape], "column")[0]}
        return self.blocks[0]

    def meet(self, later):
        self.blocks, later.got = lax.optimization_barrier((self.blocks, later.got))

    def hop(self, step, held, *earlier):
        self.blocks[held] = after(self.blocks[held], *earlier)
        self.blocks[held | 1 << step] = self.place.across_step(self.blocks[held], step)

    def share(self, held):
        return self.place.across_cores(self.blocks[held])

    def spread(self, parts, *earlier):
        place = self.place
        others = [self.share(m) for m in range(place.dp_count)]
        ins = [self.blocks[m] for m in range(place.dp_count)] + others
        ins = after(ins, *earlier)
        cols = self.local.shape[1]
        plan, outs = [], []
        for out, (first, rows) in enumerate(parts):
            outs.append(
                jax.ShapeDtypeStruct((place.dp_count, place.chips, 2, rows, cols), BF)
            )
            for m in range(2 * place.dp_count):
                core = place.core_at + (m >= place.dp_count)
                plan.append(
                    (
                        m,
                        lambda s, a=first, n=rows: (slice(None), pl.ds(a, n)),
                        out,
                        lambda s, m=m, core=core: (s[m], slice(None), s[core]),
                    )
                )
        whole = copy_call(place, plan, ins, outs, "spread")
        return [w.reshape(-1, cols) for w in whole]


def sum_refs(refs, n, arrived):
    parts = []
    for mine, other in zip(refs[:n], refs[n : 2 * n]):
        shape = mine.shape[-2:]
        lead = mine.shape[1:2]
        parts.append(
            (mine[...].astype(F32) + other[...].astype(F32)).reshape(lead + shape)
        )
    value = parts[0] if n == 1 else jnp.concatenate(parts, axis=1)
    for a in refs[2 * n : 2 * n + arrived]:
        value = value + a[...].astype(F32).reshape(value.shape)
    return value


def leave_kernel(n, arrived, spots_ref, *refs):
    out = refs[-1]
    out[...] = sum_refs(refs[:-1], n, arrived).astype(BF).reshape(out.shape)


def last_kernel(n, arrived, chips, spots_ref, *refs):
    each = 2 * n + arrived
    outs = refs[chips * each :]
    for k in range(chips):
        value = sum_refs(refs[k * each : (k + 1) * each], n, arrived)
        outs[k][...] = value.astype(outs[k].dtype).reshape(outs[k].shape)


def cut_kernel(parts, count, *refs):
    total = refs[0][...].astype(F32)
    for r in refs[1:count]:
        total = total + r[...].astype(F32)
    for (shape, row, col), out in zip(parts, refs[count:]):
        piece = total[row : row + int(np.prod(shape[:-1])), col : col + shape[-1]]
        out[...] = piece.reshape(shape)


def cut_sum(terms, parts):
    return pl.pallas_call(
        functools.partial(cut_kernel, parts, len(terms)),
        out_shape=[jax.ShapeDtypeStruct(s, F32) for s, _, _ in parts],
        compiler_params=pltpu.CompilerParams(vmem_limit_bytes=8 << 20),
        cost_estimate=QUICK,
        name="cut_sum",
    )(*terms)


class Reduce:
    def __init__(self, place, blocks):
        self.place = place
        self.blocks = blocks
        self.rows = sum(b.shape[3] for b in blocks)
        self.cols = blocks[0].shape[4]
        self.others = [place.across_cores(b) for b in blocks]
        self.got = []

    def leave(self, step, *earlier):
        place = self.place
        if step == 0:
            self.others = after(self.others, *earlier)
        else:
            self.got[-1] = after(self.got[-1], *earlier)
        count = 1 << (place.bits - 1 - step)
        chips, core = place.chips, place.core_at

        def spot(i, s):
            return s[(1 << step) + i * (2 << step)]

        specs = [
            pl.BlockSpec(
                (1, chips, 1) + b.shape[3:], lambda i, s: (spot(i, s), 0, s[core], 0, 0)
            )
            for b in self.blocks
        ] * 2
        for t in range(step):
            specs.append(
                pl.BlockSpec(
                    (1, chips, self.rows, self.cols),
                    lambda i, s, t=t: ((1 << (step - t - 1)) + i * (1 << (step - t)), 0, 0, 0),
                )
            )
        sent = pl.pallas_call(
            functools.partial(leave_kernel, len(self.blocks), step),
            grid_spec=pltpu.PrefetchScalarGridSpec(
                num_scalar_prefetch=1,
                grid=(count,),
                in_specs=specs,
                out_specs=pl.BlockSpec(
                    (1, chips, self.rows, self.cols), lambda i, s: (i, 0, 0, 0)
                ),
            ),
            out_shape=jax.ShapeDtypeStruct((count, chips, self.rows, self.cols), BF),
            compiler_params=pltpu.CompilerParams(vmem_limit_bytes=24 << 20),
            cost_estimate=QUICK,
            name="leave",
        )(place.spots, *self.blocks, *self.others, *self.got)
        self.got.append(place.across_step(sent, step))
        return sent

    def last(self, *earlier):
        place = self.place
        self.got[-1] = after(self.got[-1], *earlier)
        chips, core = place.chips, place.core_at
        specs, ins = [], []
        for k in range(chips):
            up = place.up_at + k
            for b in self.blocks + self.others:
                ins.append(b)
                specs.append(
                    pl.BlockSpec(
                        (1, 1, 1) + b.shape[3:],
                        lambda i, s, up=up: (s[0], s[up], s[core], 0, 0),
                    )
                )
            for g in self.got:
                ins.append(g)
                specs.append(
                    pl.BlockSpec(
                        (1, 1, self.rows, self.cols), lambda i, s, up=up: (0, s[up], 0, 0)
                    )
                )
        flat = pl.BlockSpec((self.rows, self.cols), lambda i, s: (0, 0))
        own, *sent = pl.pallas_call(
            functools.partial(last_kernel, len(self.blocks), place.bits, chips),
            grid_spec=pltpu.PrefetchScalarGridSpec(
                num_scalar_prefetch=1, grid=(1,), in_specs=specs, out_specs=[flat] * chips
            ),
            out_shape=[
                jax.ShapeDtypeStruct((self.rows, self.cols), F32 if k == 0 else BF)
                for k in range(chips)
            ],
            compiler_params=pltpu.CompilerParams(vmem_limit_bytes=24 << 20),
            cost_estimate=QUICK,
            name="last",
        )(place.spots, *ins)
        self.own = own
        self.came = [place.along_chips(v, k + 1) for k, v in enumerate(sent)]
        return own

    def result(self, parts, *earlier):
        self.came = after(self.came, *earlier)
        return cut_sum([self.own] + self.came, parts)


def owner_blocks(place, gradient):
    rows = gradient.shape[0] // (place.dp_count * place.inner)
    return gradient.reshape(
        place.dp_count, place.chips, 2, rows, gradient.shape[-1]
    )


class PlainReduce:
    def __init__(self, place, blocks):
        devices = place.dp_count * place.inner
        flat = [b.reshape((devices,) + b.shape[3:]) for b in blocks]
        self.sum = lax.psum_scatter(
            jnp.concatenate(flat, axis=1), AXES, scatter_dimension=0, tiled=False
        )

    def leave(self, step, *earlier):
        return self.sum

    def last(self, *earlier):
        return self.sum

    def result(self, parts, *earlier):
        total = self.sum.astype(F32)
        return [
            total[r : r + int(np.prod(s[:-1])), c : c + s[-1]].reshape(s)
            for s, r, c in parts
        ]


def dot_nt(a, b):
    return lax.dot_general(a, b, (((1,), (1,)), ((), ())), preferred_element_type=F32)


def dot_nn(a, b):
    return jnp.dot(a, b, preferred_element_type=F32)


def dot_tn(a, b):
    return lax.dot_general(a, b, (((0,), (0,)), ((), ())), preferred_element_type=F32)


def head(h):
    return slice(h * HD, (h + 1) * HD)


def attend_kernel(
    masked, start_ref, length_ref, q_ref, k_ref, v_ref, o_ref, p_ref, scores_ref
):
    rows = q_ref.shape[0]
    keys = k_ref.shape[0]
    if masked:
        seq = pl.program_id(0)
        start = start_ref[seq]
        stop = start + length_ref[seq]
        key_at = lax.broadcasted_iota(jnp.int32, (keys, rows), 0)
        row_at = lax.broadcasted_iota(jnp.int32, (keys, rows), 1)
        inside = (key_at >= start) & (key_at < stop) & (row_at >= start) & (row_at < stop)
        hidden = jnp.where((key_at <= row_at) | inside, 0.0, BIG_NEGATIVE).astype(F32)
    for h in range(H):
        scores_ref[h] = dot_nt(k_ref[:, head(h)], q_ref[:, head(h)])
    for h in range(H):
        scores = scores_ref[h]
        if masked:
            scores = scores + hidden
        peak = jnp.max(scores, axis=0, keepdims=True)
        weights = jnp.exp(scores - peak)
        total = jnp.sum(weights, axis=0, keepdims=True)
        p_ref[0, h] = (weights * (1.0 / total)).astype(BF)
    values_t = v_ref[...].T
    pieces = [dot_nn(values_t[head(h)], p_ref[0, h]) for h in range(H)]
    o_ref[...] = jnp.concatenate(pieces, axis=0).T.astype(BF)


def attend(queries, keys, values, start, length, masked, count):
    rows = queries.shape[0] // count
    key_rows = keys.shape[0] // count
    block = lambda n: pl.BlockSpec((n, D), lambda s, *_: (s, 0))
    return pl.pallas_call(
        functools.partial(attend_kernel, masked),
        grid_spec=pltpu.PrefetchScalarGridSpec(
            num_scalar_prefetch=2,
            grid=(count,),
            in_specs=[block(rows), block(key_rows), block(key_rows)],
            out_specs=[
                block(rows),
                pl.BlockSpec((1, H, key_rows, rows), lambda s, *_: (s, 0, 0, 0)),
            ],
            scratch_shapes=[pltpu.VMEM((H, key_rows, rows), F32)],
        ),
        out_shape=[
            jax.ShapeDtypeStruct(queries.shape, BF),
            jax.ShapeDtypeStruct((count, H, key_rows, rows), BF),
        ],
        compiler_params=pltpu.CompilerParams(vmem_limit_bytes=20 << 20),
        cost_estimate=QUICK,
        name="attend",
    )(start, length, queries, keys, values)


def attend_back_kernel(
    q_ref, k_ref, v_ref, p_ref, g_ref, dq_ref, dk_ref, dv_ref, moved_ref, ds_ref
):
    for h in range(H):
        moved_ref[h] = dot_nt(v_ref[:, head(h)], g_ref[:, head(h)])
    for h in range(H):
        weights = p_ref[0, h].astype(F32)
        moved = moved_ref[h]
        centre = jnp.sum(weights * moved, axis=0, keepdims=True)
        ds_ref[h] = (weights * (moved - centre)).astype(BF)
    keys_t = k_ref[...].T
    dq, dk, dv = [], [], []
    for h in range(H):
        dk.append(dot_nn(ds_ref[h], q_ref[:, head(h)]))
        dv.append(dot_nn(p_ref[0, h], g_ref[:, head(h)]))
        dq.append(dot_nn(keys_t[head(h)], ds_ref[h]))
    dq_ref[...] = jnp.concatenate(dq, axis=0).T.astype(BF)
    dk_ref[...] = jnp.concatenate(dk, axis=1).astype(BF)
    dv_ref[...] = jnp.concatenate(dv, axis=1).astype(BF)


def attend_back(queries, keys, values, weights, grads, count):
    rows = queries.shape[0] // count
    key_rows = keys.shape[0] // count
    block = lambda n: pl.BlockSpec((n, D), lambda s: (s, 0))
    return pl.pallas_call(
        attend_back_kernel,
        grid=(count,),
        in_specs=[
            block(rows),
            block(key_rows),
            block(key_rows),
            pl.BlockSpec((1, H, key_rows, rows), lambda s: (s, 0, 0, 0)),
            block(rows),
        ],
        out_specs=[block(rows), block(key_rows), block(key_rows)],
        out_shape=[
            jax.ShapeDtypeStruct(queries.shape, BF),
            jax.ShapeDtypeStruct(keys.shape, BF),
            jax.ShapeDtypeStruct(keys.shape, BF),
        ],
        scratch_shapes=[
            pltpu.VMEM((H, key_rows, rows), F32),
            pltpu.VMEM((H, key_rows, rows), BF),
        ],
        compiler_params=pltpu.CompilerParams(vmem_limit_bytes=24 << 20),
        cost_estimate=QUICK,
        name="attend_back",
    )(queries, keys, values, weights, grads)


def norm(summed):
    centre = summed - jnp.mean(summed, axis=-1, keepdims=True)
    scale = lax.rsqrt(jnp.mean(centre * centre, axis=-1, keepdims=True) + EPS)
    return centre * scale, scale


def norm_back(normal, scale, gain, grad):
    inner = grad * gain
    back = scale * (
        inner
        - jnp.mean(inner, axis=-1, keepdims=True)
        - normal * jnp.mean(inner * normal, axis=-1, keepdims=True)
    )
    return back, jnp.sum(grad * normal, axis=0), jnp.sum(grad, axis=0)


def column_sum(value):
    return jnp.sum(value.astype(F32), axis=0)


def gelu_and_slope(value):
    spread = 0.5 * (1.0 + lax.erf(value * np.float32(np.sqrt(0.5))))
    density = jnp.exp(-0.5 * value * value) * np.float32(1.0 / np.sqrt(2.0 * np.pi))
    return value * spread, spread + value * density


def pack_kernel(sp_ref, so_ref, ab_ref, eb_ref, cb_ref, ng_ref, ns_ref, out_ref):
    rows, n = so_ref.shape[0], ab_ref.shape[1]
    for i in range(3):
        out_ref[i * rows : (i + 1) * rows] = sp_ref[i]
    out_ref[3 * rows : 4 * rows] = so_ref[...]

    def padded(v, width):
        v = v.astype(F32)
        if v.shape[0] < 8:
            v = jnp.concatenate([v, jnp.zeros((8 - v.shape[0], v.shape[1]), F32)])
        return jnp.concatenate([v, jnp.zeros((8, width - v.shape[1]), F32)], axis=1)

    first = jnp.concatenate([ab_ref[...].astype(F32), cb_ref[...].astype(F32)])
    second = jnp.concatenate([ng_ref[...].astype(F32), ns_ref[...].astype(F32)])
    out_ref[4 * rows :] = jnp.concatenate(
        [padded(first, 128), padded(second, 128), padded(eb_ref[...], D - 256)], axis=1
    ).astype(BF)


def pack_self(sp, so, ab, eb, cb, ng, ns):
    ins = [sp, so, ab, eb.reshape(1, -1), cb.reshape(1, -1), ng, ns]
    ins = [pltpu.with_memory_space_constraint(a, pltpu.HBM) for a in ins]
    return pl.pallas_call(
        pack_kernel,
        grid=(1,),
        in_specs=[
            pl.BlockSpec(a.shape, lambda i, n=a.ndim: (0,) * n) for a in ins
        ],
        out_specs=pl.BlockSpec((4 * so.shape[0] + 8, D), lambda i: (0, 0)),
        out_shape=jax.ShapeDtypeStruct((4 * so.shape[0] + 8, D), BF),
        compiler_params=pltpu.CompilerParams(vmem_limit_bytes=4 << 20),
        cost_estimate=QUICK,
        name="pack_self",
    )(*ins)


def pack_small(ab, eb, cb, ng, ns):
    n, wide = cb.shape[0], eb.shape[0]
    return jnp.concatenate(
        [
            jnp.pad(jnp.concatenate([ab, cb[None]]), ((0, 1), (0, 128 - n))),
            jnp.pad(jnp.concatenate([ng, ns]), ((0, 2), (0, 128 - n))),
            jnp.pad(eb[None], ((0, 7), (0, D - 256 - wide))),
        ],
        axis=1,
    )


def unpack_small_kernel(n, wide, in_ref, rows_ref, eb_ref):
    for d in range(in_ref.shape[0]):
        block = in_ref[d].astype(F32)
        rows_ref[0:8, d * n : (d + 1) * n] = block[:, 0:n]
        rows_ref[8:16, d * n : (d + 1) * n] = block[:, 128 : 128 + n]
        eb_ref[:, d * wide : (d + 1) * wide] = block[0:1, 256 : 256 + wide]


def unpack_small(gathered, n, wide):
    devices = gathered.shape[0]
    return pl.pallas_call(
        functools.partial(unpack_small_kernel, n, wide),
        out_shape=[
            jax.ShapeDtypeStruct((16, devices * n), F32),
            jax.ShapeDtypeStruct((1, devices * wide), F32),
        ],
        compiler_params=pltpu.CompilerParams(vmem_limit_bytes=8 << 20),
        cost_estimate=QUICK,
        name="unpack_small",
    )(gathered)


def split_small_kernel(n, wide, *refs):
    *vectors, eb_ref, out_ref = refs
    rows = [v[...].reshape(1, D) for v in vectors]
    zero = jnp.zeros((1, D), F32)
    first = jnp.concatenate(rows[:7] + [zero], axis=0)
    second = jnp.concatenate(rows[7:] + [zero, zero], axis=0)
    tail = jnp.broadcast_to(eb_ref[...].reshape(1, FF), (8, FF))

    def padded(v, width):
        return jnp.concatenate([v, jnp.zeros((8, width - v.shape[1]), F32)], axis=1)

    for d in range(out_ref.shape[0]):
        out_ref[d] = jnp.concatenate(
            [
                padded(first[:, d * n : (d + 1) * n], 128),
                padded(second[:, d * n : (d + 1) * n], 128),
                padded(tail[:, d * wide : (d + 1) * wide], D - 256),
            ],
            axis=1,
        ).astype(BF)


def split_small(vectors, eb, n, wide):
    devices = D // n
    return pl.pallas_call(
        functools.partial(split_small_kernel, n, wide),
        out_shape=jax.ShapeDtypeStruct((devices, 8, D), BF),
        compiler_params=pltpu.CompilerParams(vmem_limit_bytes=8 << 20),
        cost_estimate=QUICK,
        name="split_small",
    )(*vectors, eb)


def body(
    layer_input,
    encoder_states,
    output_grad,
    span_start,
    span_length,
    self_project,
    self_output,
    cross_project,
    cross_output,
    attend_bias,
    expand_weight,
    expand_bias,
    contract_weight,
    contract_bias,
    norm_gain,
    norm_shift,
):
    place = Place()
    count, length = layer_input.shape[:2]
    shape = layer_input.shape
    rows = self_output.shape[0]
    wide = expand_bias.shape[0]
    fits = rows % 8 == 0
    reduce = Reduce if fits else PlainReduce
    x = layer_input.reshape(-1, D)
    memory = encoder_states.reshape(-1, D)
    grad_out = output_grad.reshape(-1, D).astype(F32)

    local_cross = jnp.concatenate([cross_project.reshape(-1, D), cross_output])
    four = [(i * rows, rows) for i in range(4)]
    if fits:
        g_self = Gather(
            place,
            pack_self(
                self_project,
                self_output,
                attend_bias,
                expand_bias,
                contract_bias,
                norm_gain,
                norm_shift,
            ),
        )
        line = g_self.column()
        g_self.hop(0, 0)
        g_self.hop(1, 0)
        g_cross = Gather(place, after(local_cross, line))
        g_self.meet(g_cross)
        g_self.hop(1, 1)
        line = g_cross.column()
        g_cross.hop(0, 0)
        g_cross.hop(1, 0)
        g_expand = Gather(place, after(expand_weight, line))
        *w_self, smalls = g_self.spread(four + [(4 * rows, 8)], line)
        smalls = smalls.reshape(-1, 8, D)
    else:
        whole = lax.all_gather(
            jnp.concatenate(
                [
                    self_project.reshape(-1, D),
                    self_output,
                    pack_small(
                        attend_bias, expand_bias, contract_bias, norm_gain, norm_shift
                    ),
                    local_cross,
                    contract_weight,
                ]
            ),
            AXES,
            axis=0,
        )
        squares = [
            whole[:, a : a + rows].reshape(D, D)
            for a in [i * rows for i in range(4)]
            + [4 * rows + 8 + i * rows for i in range(4)]
        ]
        w_self, w_cross = squares[:4], squares[4:]
        contract = whole[:, 8 * rows + 8 :].reshape(FF, D)
        smalls = whole[:, 4 * rows : 4 * rows + 8]
        expand = lax.all_gather(expand_weight, AXES, axis=0, tiled=True)
    wq, wk, wv, wo = w_self
    small_rows, expand_b = unpack_small(smalls, rows, wide)
    biases = [small_rows[i : i + 1] for i in range(6)]
    contract_b = small_rows[6:7]
    gains = [small_rows[8 + i : 9 + i] for i in range(3)]
    shifts = [small_rows[11 + i : 12 + i] for i in range(3)]

    q = ((dot_nn(x, wq) + biases[0]) * 0.125).astype(BF)
    k = dot_nn(x, wk).astype(BF)
    v = (dot_nn(x, wv) + biases[1]).astype(BF)
    o, p = attend(q, k, v, span_start, span_length, True, count)
    if fits:
        g_cross.hop(1, 1, o)
        line = g_expand.column(o)
        g_expand.hop(0, 0)
        g_expand.hop(1, 0)
        g_contract = Gather(place, after(contract_weight, line))
        o = after(o, line)
    n1, s1 = norm(x.astype(F32) + (dot_nn(o, wo) + biases[2]))
    x1 = n1 * gains[0] + shifts[0]
    x1b = x1.astype(BF)
    if fits:
        w_cross = g_cross.spread(four, x1b)
    cq, ck, cv, co = w_cross
    q2 = ((dot_nn(x1b, cq) + biases[3]) * 0.125).astype(BF)
    k2 = dot_nn(memory, ck).astype(BF)
    v2 = (dot_nn(memory, cv) + biases[4]).astype(BF)
    o2, p2 = attend(q2, k2, v2, span_start, span_length, False, count)
    if fits:
        g_expand.hop(1, 1, o2)
        line = g_contract.column(o2)
        g_contract.hop(0, 0)
        g_contract.hop(1, 0)
        o2 = after(o2, line)
    n2, s2 = norm(x1 + (dot_nn(o2, co) + biases[5]))
    x2 = n2 * gains[1] + shifts[1]
    x2b = x2.astype(BF)
    if fits:
        (expand,) = g_expand.spread([(0, rows)], x2b)
    act, slope = gelu_and_slope(dot_nn(x2b, expand) + expand_b)
    act = act.astype(BF)
    slope = slope.astype(BF)
    if fits:
        g_contract.hop(1, 1, act)
        (contract,) = g_contract.spread([(0, 4 * rows)], act)
    n3, s3 = norm(x2 + (dot_nn(act, contract) + contract_b))
    output = (n3 * gains[2] + shifts[2]).astype(BF)

    dr3, gain3, shift3 = norm_back(n3, s3, gains[2], grad_out)
    df = dr3.astype(BF)
    d_contract = dot_tn(act, df).astype(BF)
    r_contract = reduce(place, [owner_blocks(place, d_contract)])
    d_contract_b = column_sum(df)
    df2 = after(df, d_contract)
    du = (dot_nt(df2, contract) * slope.astype(F32)).astype(BF)
    d_expand_b = column_sum(du)

    hop = r_contract.leave(0, du)
    d_expand = dot_tn(x2b, after(du, hop)).astype(BF)
    r_expand = reduce(place, [owner_blocks(place, d_expand)])
    dr2, gain2, shift2 = norm_back(
        n2, s2, gains[1], dr3 + dot_nt(after(du, d_expand), expand)
    )
    dc = dr2.astype(BF)
    hop = r_contract.leave(1, dc)
    hop2 = r_expand.leave(0, dc)
    dc2 = after(dc, hop, hop2)
    d_co = dot_tn(o2, dc2).astype(BF)
    do2 = dot_nt(dc2, co).astype(BF)
    dq2, dk2, dv2 = attend_back(q2, k2, v2, p2, after(do2, d_co), count)
    dq2 = dq2 * BF(0.125)

    sent = r_contract.last(dq2)
    hop2 = r_expand.leave(1, dq2)
    dq2, dk2, dv2 = after((dq2, dk2, dv2), sent, hop2)
    d_cross = [dot_tn(x1b, dq2), dot_tn(memory, dk2), dot_tn(memory, dv2)]
    d_cross = [d.astype(BF) for d in d_cross]
    r_cross = reduce(place, [owner_blocks(place, d) for d in d_cross + [d_co]])
    dq2, dk2, dv2 = after((dq2, dk2, dv2), d_cross)

    dr1, gain1, shift1 = norm_back(n1, s1, gains[0], dr2 + dot_nt(dq2, cq))
    da = dr1.astype(BF)
    hop = r_cross.leave(0, da)
    (own_contract,) = r_contract.result([((4 * rows, D), 0, 0)], da)
    sent = r_expand.last(da)
    da2 = after(da, hop, own_contract, sent)
    d_so = dot_tn(o, da2).astype(BF)
    do = dot_nt(da2, wo).astype(BF)
    dq, dk, dv = attend_back(q, k, v, p, after(do, d_so), count)
    dq = dq * BF(0.125)

    hop = r_cross.leave(1, dq)
    dq, dk, dv = after((dq, dk, dv), hop)
    d_self = [dot_tn(x, dq), dot_tn(x, dk), dot_tn(x, dv)]
    d_self = [d.astype(BF) for d in d_self]
    small_blocks = split_small(
        [column_sum(t) for t in (dq, dv, da, dq2, dv2, dc)]
        + [d_contract_b, gain1, gain2, gain3, shift1, shift2, shift3],
        d_expand_b,
        rows,
        wide,
    )
    small_blocks = small_blocks.reshape(place.dp_count, place.chips, 2, 8, D)
    r_self = reduce(
        place, [owner_blocks(place, d) for d in d_self + [d_so]] + [small_blocks]
    )
    (own_expand,) = r_expand.result([((rows, FF), 0, 0)], d_self, small_blocks)
    dk2, dv2 = after((dk2, dv2), own_expand)
    encoder_grad = dot_nt(dk2, ck) + dot_nt(dv2, cv)
    sent = r_cross.last(encoder_grad)
    hop = r_self.leave(0, sent)
    dq, dk, dv = after((dq, dk, dv), hop)
    input_grad = dr1 + dot_nt(dq, wq) + dot_nt(dk, wk) + dot_nt(dv, wv)
    projects = [((3, rows, D), 0, 0), ((rows, D), 3 * rows, 0)]
    own_cross = r_cross.result(projects, input_grad)
    r_self.leave(1, own_cross)
    r_self.last()
    at = 4 * rows
    own_self = r_self.result(
        projects
        + [
            ((6, rows), at, 0),
            ((1, wide), at, 256),
            ((1, rows), at + 6, 0),
            ((3, rows), at, 128),
            ((3, rows), at + 3, 128),
        ]
    )
    return (
        output.reshape(shape),
        input_grad.reshape(shape),
        encoder_grad.reshape(encoder_states.shape),
        own_self[0],
        own_self[1],
        own_cross[0],
        own_cross[1],
        own_self[2],
        own_expand,
        own_self[3].reshape(-1),
        own_contract,
        own_self[4].reshape(-1),
        own_self[5],
        own_self[6],
    )


def solution(mesh):
    rows = P(AXES)
    return jax.shard_map(
        body,
        mesh=mesh,
        in_specs=(
            P(AXES, None, None),
            P(AXES, None, None),
            P(AXES, None, None),
            P(AXES),
            P(AXES),
            P(None, AXES, None),
            P(AXES, None),
            P(None, AXES, None),
            P(AXES, None),
            P(None, AXES),
            P(AXES, None),
            P(AXES),
            P(AXES, None),
            P(AXES),
            P(None, AXES),
            P(None, AXES),
        ),
        out_specs=(
            P(AXES, None, None),
            P(AXES, None, None),
            P(AXES, None, None),
            P(None, AXES, None),
            P(AXES, None),
            P(None, AXES, None),
            P(AXES, None),
            P(None, AXES),
            P(AXES, None),
            P(AXES),
            P(AXES, None),
            P(AXES),
            P(None, AXES),
            P(None, AXES),
        ),
        check_vma=False,
    )
```

profile of v0, /device:TPU:9, one launch (start us, length us, event | category | flops | bytes accessed | tf_op | source)
XLA Modules:
  0.0 299.0 jit_solution(7782259124656764793)
XLA Ops:
  7.2 6.9 %collective-permute-done.1.refs_2_ = bf16[104,768]{1,0:T(8,128)(2,1)S(1)} collective-permute-done((bf16[104,768]{1,0:T(8,128)(2,1)S(1)}, bf16[104,768]{1,0:T(8,128)(2,1)S(1)}, u32[]{:S(2)}, u32[]{:S(2)}) %collective-permute-start.1) | collective-permute-done | bytes 159776 | tf_op jit(solution)/shard_map/ppermute | solution.py:72
  14.1 3.6 %collective-permute-done.refs_1_ = bf16[104,768]{1,0:T(8,128)(2,1)S(1)} collective-permute-done((bf16[104,768]{1,0:T(8,128)(2,1)S(1)}, bf16[104,768]{1,0:T(8,128)(2,1)S(1)}, u32[]{:S(2)}, u32[]{:S(2)}) %collective-permute-start) | collective-permute-done | bytes 159776 | tf_op jit(solution)/shard_map/ppermute | solution.py:72
  26.7 6.5 %collective-permute-done.6.refs_2_ = bf16[96,768]{1,0:T(8,128)(2,1)S(1)} collective-permute-done((bf16[96,768]{1,0:T(8,128)(2,1)S(1)}, bf16[96,768]{1,0:T(8,128)(2,1)S(1)}, u32[]{:S(2)}, u32[]{:S(2)}) %collective-permute-start.6) | collective-permute-done | bytes 147488 | tf_op jit(solution)/shard_map/ppermute | solution.py:72
  39.2 6.7 %collective-permute-done.8.refs_3_ = bf16[4,104,768]{2,1,0:T(8,128)(2,1)S(1)} collective-permute-done((bf16[4,104,768]{2,1,0:T(8,128)(2,1)S(1)}, bf16[4,104,768]{2,1,0:T(8,128)(2,1)S(1)}, u32[]{:S(2)}, u32[]{:S(2)}) %collective-permute-start.8) | collective-permute-done | bytes 639008 | tf_op jit(solution)/shard_map/ppermute | solution.py:72
  59.7 4.0 %attend.2 = (bf16[512,768]{1,0:T(8,128)(2,1)S(1)}, bf16[2,12,256,256]{3,2,1,0:T(8,128)(2,1)S(1)}) custom-call(s32[2]{0:T(128)S(1)} %copy-done.20, s32[2]{0:T(128)S(1)} %copy-done.21, bf16[512,768]{1,0:T(8,128)(2,1)S(1)} %fusion.14.q_ref, bf16[512,768]{1,0:T(8,128)(2,1)S(1)} %fusion.17.k_ref, bf16[512,768]{1,0:T(8,128)(2,1)S(1)} %fusion.15.v_ref), custom_call_target="tpu_custom_call" | custom-call | flops 1000 | bytes 1000 | tf_op jit(solution)/shard_map/attend/pallas_call | solution.py:402
  66.3 3.7 %collective-permute-start.19 = (bf16[4,96,768]{2,1,0:T(8,128)(2,1)S(1)}, bf16[4,96,768]{2,1,0:T(8,128)(2,1)S(1)}, u32[]{:S(2)}, u32[]{:S(2)}) collective-permute-start(bf16[4,96,768]{2,1,0:T(8,128)(2,1)S(1)} %column.5.refs_0_), channel_id=1, source_target_pairs={{0,1},{1,0},{2,3},{3,2},{4,5},{5,4},{6,7},{7,6},{8,9},{9,8},{10,11... | collective-permute-start | bytes 1769480 | tf_op jit(solution)/shard_map/ppermute | solution.py:72
  75.3 3.7 %collective-permute-start.22 = (bf16[4,96,768]{2,1,0:T(8,128)(2,1)S(1)}, bf16[4,96,768]{2,1,0:T(8,128)(2,1)S(1)}, u32[]{:S(2)}, u32[]{:S(2)}) collective-permute-start(bf16[4,96,768]{2,1,0:T(8,128)(2,1)S(1)} %collective-permute-done.18.refs_3_), channel_id=1, source_target_pairs={{0,1},{1,0},{2,3},{3,2},{4,5},{5,4},{6,7},{7,6},{8,9},{9,8},{10,11... | collective-permute-start | bytes 1769480 | tf_op jit(solution)/shard_map/ppermute | solution.py:72
  89.2 3.7 %attend.3 = (bf16[512,768]{1,0:T(8,128)(2,1)S(1)}, bf16[2,12,256,256]{3,2,1,0:T(8,128)(2,1)S(1)}) custom-call(s32[2]{0:T(128)S(1)} %copy-done.20, s32[2]{0:T(128)S(1)} %copy-done.21, bf16[512,768]{1,0:T(8,128)(2,1)S(1)} %multiply_convert_fusion.2.q_ref, bf16[512,768]{1,0:T(8,128)(2,1)S(1)} %fusion.18.k_ref, bf16[512,768]{1,0:T(8,128)(2,1)S(1)} %fusion.16.v_ref), custom_call_target="tpu_custom_call" | custom-call | flops 1000 | bytes 1000 | tf_op jit(solution)/shard_map/attend/pallas_call | solution.py:402
  94.2 3.7 %collective-permute-done.27.refs_2_ = bf16[4,24,3072]{2,1,0:T(8,128)(2,1)S(1)} collective-permute-done((bf16[4,24,3072]{2,1,0:T(8,128)(2,1)S(1)}, bf16[4,24,3072]{2,1,0:T(8,128)(2,1)S(1)}, u32[]{:S(2)}, u32[]{:S(2)}) %collective-permute-start.27) | collective-permute-done | bytes 589856 | tf_op jit(solution)/shard_map/ppermute | solution.py:72
  103.1 13.0 %collective-permute-done.28.refs_3_ = bf16[4,24,3072]{2,1,0:T(8,128)(2,1)S(1)} collective-permute-done((bf16[4,24,3072]{2,1,0:T(8,128)(2,1)S(1)}, bf16[4,24,3072]{2,1,0:T(8,128)(2,1)S(1)}, u32[]{:S(2)}, u32[]{:S(2)}) %collective-permute-start.28) | collective-permute-done | bytes 589856 | tf_op jit(solution)/shard_map/ppermute | solution.py:72
  119.2 5.1 %multiply_convert_fusion.1 = (bf16[512,3072]{1,0:T(8,128)(2,1)S(1)}, f32[512,3072]{1,0:T(8,128)}) fusion(f32[3072]{0:T(1024)S(1)} %bitcast.236, bf16[512,768]{1,0:T(8,128)(2,1)S(1)} %fusion.13, bf16[768,3072]{1,0:T(8,128)(2,1)S(1)} %bitcast.215), kind=kOutput, calls=%fused_computation.8 | convolution fusion | flops 2425356288 | bytes 14954496 | tf_op jit(solution)/shard_map/dot_general | solution.py:359
  127.2 6.1 %collective-permute-done.35.refs_3_ = bf16[4,96,768]{2,1,0:T(8,128)(2,1)S(1)} collective-permute-done((bf16[4,96,768]{2,1,0:T(8,128)(2,1)S(1)}, bf16[4,96,768]{2,1,0:T(8,128)(2,1)S(1)}, u32[]{:S(2)}, u32[]{:S(2)}) %collective-permute-start.35) | collective-permute-done | bytes 589856 | tf_op jit(solution)/shard_map/ppermute | solution.py:72
  147.0 6.3 %convert_reduce_fusion = (f32[3072]{0:T(1024)S(1)}, bf16[512,3072]{1,0:T(8,128)(2,1)S(1)}) fusion(f32[512,3072]{1,0:T(8,128)} %get-tuple-element.374, f32[3072]{0:T(1024)S(1)} %bitcast.237, bf16[512,768]{1,0:T(8,128)(2,1)S(1)} %get-tuple-element.250, bf16[3072,768]{1,0:T(8,128)(2,1)S(1)} %bitcast.218), kind=kOutput, calls=%fused_computation.6 | convolution fusion | flops 2439508992 | bytes 14966784 | tf_op jit(solution)/shard_map/dot_general | solution.py:355
  159.6 6.5 %multiply_reduce_fusion = (f32[768]{0:T(1024)S(1)}, f32[512]{0:T(512)S(1)}, f32[512]{0:T(512)S(1)}, f32[768]{0:T(1024)S(1)}, f32[512,768]{1,0:T(8,128)}) fusion(f32[512,768]{1,0:T(8,128)S(1)} %get-tuple-element.372, f32[512]{0:T(512)S(1)} %add_rsqrt_fusion.1, f32[512]{0:T(512)S(1)} %broadcast_multiply_fusion.8, f32[768]{0:T(1024)S(1)} %get-tuple-element.350, ...), kind=kOutput, calls=%fused_computation.24 | convolution fusion | flops 2419848704 | bytes 12600320 | tf_op jit(solution)/shard_map/dot_general | solution.py:355
  178.3 4.6 %attend_back.2 = (bf16[512,768]{1,0:T(8,128)(2,1)S(1)}, bf16[512,768]{1,0:T(8,128)(2,1)S(1)}, bf16[512,768]{1,0:T(8,128)(2,1)S(1)}) custom-call(bf16[512,768]{1,0:T(8,128)(2,1)S(1)} %copy-done.9, bf16[512,768]{1,0:T(8,128)(2,1)S(1)} %copy-done.13, bf16[512,768]{1,0:T(8,128)(2,1)S(1)} %copy-done.11, bf16[2,12,256,256]{3,2,1,0:T(8,128)(2,1)S(1)} %copy-done.5, ...), custom_call_target="tpu_custom_call" | custom-call | flops 1000 | bytes 1000 | tf_op jit(solution)/shard_map/attend_back/pallas_call | solution.py:449
  183.0 7.6 %collective-permute-done.43.refs_3_.refs_7_.refs_11_.refs_15_ = bf16[1,4,96,768]{3,2,1,0:T(8,128)(2,1)S(1)} collective-permute-done((bf16[1,4,96,768]{3,2,1,0:T(8,128)(2,1)S(1)}, bf16[1,4,96,768]{3,2,1,0:T(8,128)(2,1)S(1)}, u32[]{:S(2)}, u32[]{:S(2)}) %collective-permute-start.43) | collective-permute-done | bytes 589856 | tf_op jit(solution)/shard_map/ppermute | solution.py:72
  212.2 7.4 %collective-permute-done.50.refs_2_ = bf16[96,768]{1,0:T(8,128)(2,1)S(1)} collective-permute-done((bf16[96,768]{1,0:T(8,128)(2,1)S(1)}, bf16[96,768]{1,0:T(8,128)(2,1)S(1)}, u32[]{:S(2)}, u32[]{:S(2)}) %collective-permute-start.50) | collective-permute-done | bytes 147488 | tf_op jit(solution)/shard_map/ppermute | solution.py:72
  219.6 3.2 %collective-permute-done.51.refs_3_ = bf16[96,768]{1,0:T(8,128)(2,1)S(1)} collective-permute-done((bf16[96,768]{1,0:T(8,128)(2,1)S(1)}, bf16[96,768]{1,0:T(8,128)(2,1)S(1)}, u32[]{:S(2)}, u32[]{:S(2)}) %collective-permute-start.51) | collective-permute-done | bytes 147488 | tf_op jit(solution)/shard_map/ppermute | solution.py:72
  229.4 4.7 %attend_back.3 = (bf16[512,768]{1,0:T(8,128)(2,1)S(1)}, bf16[512,768]{1,0:T(8,128)(2,1)S(1)}, bf16[512,768]{1,0:T(8,128)(2,1)S(1)}) custom-call(bf16[512,768]{1,0:T(8,128)(2,1)S(1)} %fusion.14.q_ref, bf16[512,768]{1,0:T(8,128)(2,1)S(1)} %copy-done.7, bf16[512,768]{1,0:T(8,128)(2,1)S(1)} %fusion.15.v_ref, bf16[2,12,256,256]{3,2,1,0:T(8,128)(2,1)S(1)} %copy-done.3, ...), custom_call_target="tpu_custom_call" | custom-call | flops 1000 | bytes 1000 | tf_op jit(solution)/shard_map/attend_back/pallas_call | solution.py:449
  260.3 5.2 %collective-permute-done.65.refs_2_ = bf16[96,768]{1,0:T(8,128)(2,1)S(1)} collective-permute-done((bf16[96,768]{1,0:T(8,128)(2,1)S(1)}, bf16[96,768]{1,0:T(8,128)(2,1)S(1)}, u32[]{:S(2)}, u32[]{:S(2)}) %collective-permute-start.65) | collective-permute-done | bytes 147488 | tf_op jit(solution)/shard_map/ppermute | solution.py:72
  265.6 3.2 %collective-permute-done.66.refs_3_ = bf16[96,768]{1,0:T(8,128)(2,1)S(1)} collective-permute-done((bf16[96,768]{1,0:T(8,128)(2,1)S(1)}, bf16[96,768]{1,0:T(8,128)(2,1)S(1)}, u32[]{:S(2)}, u32[]{:S(2)}) %collective-permute-start.66) | collective-permute-done | bytes 147488 | tf_op jit(solution)/shard_map/ppermute | solution.py:72
  270.4 9.5 %collective-permute-done.67.refs_11_.refs_23_.refs_35_.refs_47_ = bf16[1,4,104,768]{3,2,1,0:T(8,128)(2,1)S(1)} collective-permute-done((bf16[1,4,104,768]{3,2,1,0:T(8,128)(2,1)S(1)}, bf16[1,4,104,768]{3,2,1,0:T(8,128)(2,1)S(1)}, u32[]{:S(2)}, u32[]{:S(2)}) %collective-permute-start.67) | collective-permute-done | bytes 639008 | tf_op jit(solution)/shard_map/ppermute | solution.py:72
  285.0 8.7 %collective-permute-done.69.refs_2_ = bf16[104,768]{1,0:T(8,128)(2,1)S(1)} collective-permute-done((bf16[104,768]{1,0:T(8,128)(2,1)S(1)}, bf16[104,768]{1,0:T(8,128)(2,1)S(1)}, u32[]{:S(2)}, u32[]{:S(2)}) %collective-permute-start.69) | collective-permute-done | bytes 159776 | tf_op jit(solution)/shard_map/ppermute | solution.py:72
  293.6 4.1 %collective-permute-done.70.refs_3_ = bf16[104,768]{1,0:T(8,128)(2,1)S(1)} collective-permute-done((bf16[104,768]{1,0:T(8,128)(2,1)S(1)}, bf16[104,768]{1,0:T(8,128)(2,1)S(1)}, u32[]{:S(2)}, u32[]{:S(2)}) %collective-permute-start.70) | collective-permute-done | bytes 159776 | tf_op jit(solution)/shard_map/ppermute | solution.py:72
  (308 shorter events, 158.9 us)
Async XLA Ops:
  19.1 17.2 %collective-permute-start.4 = (bf16[4,104,768]{2,1,0:T(8,128)(2,1)S(1)}, bf16[4,104,768]{2,1,0:T(8,128)(2,1)S(1)}, u32[]{:S(2)}, u32[]{:S(2)}) collective-permute-start(bf16[4,104,768]{2,1,0:T(8,128)(2,1)S(1)} %column.4.refs_0_), channel_id=1, source_target_pairs={{0,8},{1,17},{2,10},{3,19},{4,12},{5,21},{6,14},{7,23},{8,0},{9,25... | collective-permute-start | bytes 1916936 | tf_op jit(solution)/shard_map/ppermute | solution.py:72
  20.4 16.0 %collective-permute-start.3 = (bf16[4,104,768]{2,1,0:T(8,128)(2,1)S(1)}, bf16[4,104,768]{2,1,0:T(8,128)(2,1)S(1)}, u32[]{:S(2)}, u32[]{:S(2)}) collective-permute-start(bf16[4,104,768]{2,1,0:T(8,128)(2,1)S(1)} %column.4.refs_0_), channel_id=1, source_target_pairs={{0,16},{1,9},{2,18},{3,11},{4,20},{5,13},{6,22},{7,15},{8,24},{9,1... | collective-permute-start | bytes 1916936 | tf_op jit(solution)/shard_map/ppermute | solution.py:72
  49.0 17.3 %collective-permute-start.15 = (bf16[24,3072]{1,0:T(8,128)(2,1)S(1)}, bf16[24,3072]{1,0:T(8,128)(2,1)S(1)}, u32[]{:S(2)}, u32[]{:S(2)}) collective-permute-start(bf16[24,3072]{1,0:T(8,128)(2,1)S(1)} %copy-done.18), channel_id=1, source_target_pairs={{0,6},{1,7},{2,0},{3,1},{4,2},{5,3},{6,4},{7,5},{8,14},{9,15},{10,... | collective-permute-start | bytes 442376 | tf_op jit(solution)/shard_map/ppermute | solution.py:72
  51.2 18.9 %collective-permute-start.14 = (bf16[24,3072]{1,0:T(8,128)(2,1)S(1)}, bf16[24,3072]{1,0:T(8,128)(2,1)S(1)}, u32[]{:S(2)}, u32[]{:S(2)}) collective-permute-start(bf16[24,3072]{1,0:T(8,128)(2,1)S(1)} %copy-done.18), channel_id=1, source_target_pairs={{0,4},{1,5},{2,6},{3,7},{4,0},{5,1},{6,2},{7,3},{8,12},{9,13},{10,... | collective-permute-start | bytes 442376 | tf_op jit(solution)/shard_map/ppermute | solution.py:72
  52.4 17.7 %collective-permute-start.13 = (bf16[24,3072]{1,0:T(8,128)(2,1)S(1)}, bf16[24,3072]{1,0:T(8,128)(2,1)S(1)}, u32[]{:S(2)}, u32[]{:S(2)}) collective-permute-start(bf16[24,3072]{1,0:T(8,128)(2,1)S(1)} %copy-done.18), channel_id=1, source_target_pairs={{0,2},{1,3},{2,4},{3,5},{4,6},{5,7},{6,0},{7,1},{8,10},{9,11},{10,... | collective-permute-start | bytes 442376 | tf_op jit(solution)/shard_map/ppermute | solution.py:72
  53.7 16.3 %collective-permute-start.17 = (bf16[4,96,768]{2,1,0:T(8,128)(2,1)S(1)}, bf16[4,96,768]{2,1,0:T(8,128)(2,1)S(1)}, u32[]{:S(2)}, u32[]{:S(2)}) collective-permute-start(bf16[4,96,768]{2,1,0:T(8,128)(2,1)S(1)} %column.5.refs_0_), channel_id=1, source_target_pairs={{0,8},{1,17},{2,10},{3,19},{4,12},{5,21},{6,14},{7,23},{8,0},{9,25... | collective-permute-start | bytes 1769480 | tf_op jit(solution)/shard_map/ppermute | solution.py:72
  72.0 21.0 %collective-permute-start.25 = (bf16[96,768]{1,0:T(8,128)(2,1)S(1)}, bf16[96,768]{1,0:T(8,128)(2,1)S(1)}, u32[]{:S(2)}, u32[]{:S(2)}) collective-permute-start(bf16[96,768]{1,0:T(8,128)(2,1)S(1)} %copy-done.19), channel_id=1, source_target_pairs={{0,6},{1,7},{2,0},{3,1},{4,2},{5,3},{6,4},{7,5},{8,14},{9,15},{10,... | collective-permute-start | bytes 442376 | tf_op jit(solution)/shard_map/ppermute | solution.py:72
  79.7 19.2 %collective-permute-start.24 = (bf16[96,768]{1,0:T(8,128)(2,1)S(1)}, bf16[96,768]{1,0:T(8,128)(2,1)S(1)}, u32[]{:S(2)}, u32[]{:S(2)}) collective-permute-start(bf16[96,768]{1,0:T(8,128)(2,1)S(1)} %copy-done.19), channel_id=1, source_target_pairs={{0,4},{1,5},{2,6},{3,7},{4,0},{5,1},{6,2},{7,3},{8,12},{9,13},{10,... | collective-permute-start | bytes 442376 | tf_op jit(solution)/shard_map/ppermute | solution.py:72
  81.8 17.2 %collective-permute-start.23 = (bf16[96,768]{1,0:T(8,128)(2,1)S(1)}, bf16[96,768]{1,0:T(8,128)(2,1)S(1)}, u32[]{:S(2)}, u32[]{:S(2)}) collective-permute-start(bf16[96,768]{1,0:T(8,128)(2,1)S(1)} %copy-done.19), channel_id=1, source_target_pairs={{0,2},{1,3},{2,4},{3,5},{4,6},{5,7},{6,0},{7,1},{8,10},{9,11},{10,... | collective-permute-start | bytes 442376 | tf_op jit(solution)/shard_map/ppermute | solution.py:72
  83.2 17.7 %collective-permute-start.26 = (bf16[4,24,3072]{2,1,0:T(8,128)(2,1)S(1)}, bf16[4,24,3072]{2,1,0:T(8,128)(2,1)S(1)}, u32[]{:S(2)}, u32[]{:S(2)}) collective-permute-start(bf16[4,24,3072]{2,1,0:T(8,128)(2,1)S(1)} %column.6.refs_0_), channel_id=1, source_target_pairs={{0,16},{1,9},{2,18},{3,11},{4,20},{5,13},{6,22},{7,15},{8,24},{9,1... | collective-permute-start | bytes 1769480 | tf_op jit(solution)/shard_map/ppermute | solution.py:72
  93.0 23.7 %collective-permute-start.29 = (bf16[4,24,3072]{2,1,0:T(8,128)(2,1)S(1)}, bf16[4,24,3072]{2,1,0:T(8,128)(2,1)S(1)}, u32[]{:S(2)}, u32[]{:S(2)}) collective-permute-start(bf16[4,24,3072]{2,1,0:T(8,128)(2,1)S(1)} %column.6.refs_0_), channel_id=1, source_target_pairs={{0,1},{1,0},{2,3},{3,2},{4,5},{5,4},{6,7},{7,6},{8,9},{9,8},{10,11... | collective-permute-start | bytes 1769480 | tf_op jit(solution)/shard_map/ppermute | solution.py:72
  97.8 19.2 %collective-permute-start.31 = (bf16[4,24,3072]{2,1,0:T(8,128)(2,1)S(1)}, bf16[4,24,3072]{2,1,0:T(8,128)(2,1)S(1)}, u32[]{:S(2)}, u32[]{:S(2)}) collective-permute-start(bf16[4,24,3072]{2,1,0:T(8,128)(2,1)S(1)} %collective-permute-done.27.refs_2_), channel_id=1, source_target_pairs={{0,1},{1,0},{2,3},{3,2},{4,5},{5,4},{6,7},{7,6},{8,9},{9,8},{10,11... | collective-permute-start | bytes 1769480 | tf_op jit(solution)/shard_map/ppermute | solution.py:72
  100.3 24.0 %collective-permute-start.33 = (bf16[4,96,768]{2,1,0:T(8,128)(2,1)S(1)}, bf16[4,96,768]{2,1,0:T(8,128)(2,1)S(1)}, u32[]{:S(2)}, u32[]{:S(2)}) collective-permute-start(bf16[4,96,768]{2,1,0:T(8,128)(2,1)S(1)} %column.7.refs_0_), channel_id=1, source_target_pairs={{0,16},{1,9},{2,18},{3,11},{4,20},{5,13},{6,22},{7,15},{8,24},{9,1... | collective-permute-start | bytes 1769480 | tf_op jit(solution)/shard_map/ppermute | solution.py:72
  100.9 16.2 %collective-permute-start.30 = (bf16[4,24,3072]{2,1,0:T(8,128)(2,1)S(1)}, bf16[4,24,3072]{2,1,0:T(8,128)(2,1)S(1)}, u32[]{:S(2)}, u32[]{:S(2)}) collective-permute-start(bf16[4,24,3072]{2,1,0:T(8,128)(2,1)S(1)} %collective-permute-done.26.refs_1_), channel_id=1, source_target_pairs={{0,1},{1,0},{2,3},{3,2},{4,5},{5,4},{6,7},{7,6},{8,9},{9,8},{10,11... | collective-permute-start | bytes 1769480 | tf_op jit(solution)/shard_map/ppermute | solution.py:72
  100.9 15.2 %collective-permute-start.28 = (bf16[4,24,3072]{2,1,0:T(8,128)(2,1)S(1)}, bf16[4,24,3072]{2,1,0:T(8,128)(2,1)S(1)}, u32[]{:S(2)}, u32[]{:S(2)}) collective-permute-start(bf16[4,24,3072]{2,1,0:T(8,128)(2,1)S(1)} %collective-permute-done.26.refs_1_), channel_id=1, source_target_pairs={{0,8},{1,17},{2,10},{3,19},{4,12},{5,21},{6,14},{7,23},{8,0},{9,25... | collective-permute-start | bytes 1769480 | tf_op jit(solution)/shard_map/ppermute | solution.py:72
  158.9 15.3 %collective-permute-start.41 = (bf16[2,4,96,768]{3,2,1,0:T(8,128)(2,1)S(1)}, bf16[2,4,96,768]{3,2,1,0:T(8,128)(2,1)S(1)}, u32[]{:S(2)}, u32[]{:S(2)}) collective-permute-start(bf16[2,4,96,768]{3,2,1,0:T(8,128)(2,1)S(1)} %leave.8), channel_id=1, source_target_pairs={{0,16},{1,9},{2,18},{3,11},{4,20},{5,13},{6,22},{7,15},{8,24},{9,1... | collective-permute-start | bytes 3538952 | tf_op jit(solution)/shard_map/ppermute | solution.py:72
  170.2 23.1 %collective-permute-start.44 = (bf16[2,4,24,3072]{3,2,1,0:T(8,128)(2,1)S(1)}, bf16[2,4,24,3072]{3,2,1,0:T(8,128)(2,1)S(1)}, u32[]{:S(2)}, u32[]{:S(2)}) collective-permute-start(bf16[2,4,24,3072]{3,2,1,0:T(8,128)(2,1)S(1)} %leave.10), channel_id=1, source_target_pairs={{0,16},{1,9},{2,18},{3,11},{4,20},{5,13},{6,22},{7,15},{8,24},{9,1... | collective-permute-start | bytes 3538952 | tf_op jit(solution)/shard_map/ppermute | solution.py:72
  175.1 15.5 %collective-permute-start.43 = (bf16[1,4,96,768]{3,2,1,0:T(8,128)(2,1)S(1)}, bf16[1,4,96,768]{3,2,1,0:T(8,128)(2,1)S(1)}, u32[]{:S(2)}, u32[]{:S(2)}) collective-permute-start(bf16[1,4,96,768]{3,2,1,0:T(8,128)(2,1)S(1)} %leave.9), channel_id=1, source_target_pairs={{0,8},{1,17},{2,10},{3,19},{4,12},{5,21},{6,14},{7,23},{8,0},{9,25... | collective-permute-start | bytes 1769480 | tf_op jit(solution)/shard_map/ppermute | solution.py:72
  194.1 29.5 %collective-permute-start.52 = (bf16[1,4,24,3072]{3,2,1,0:T(8,128)(2,1)S(1)}, bf16[1,4,24,3072]{3,2,1,0:T(8,128)(2,1)S(1)}, u32[]{:S(2)}, u32[]{:S(2)}) collective-permute-start(bf16[1,4,24,3072]{3,2,1,0:T(8,128)(2,1)S(1)} %leave.11), channel_id=1, source_target_pairs={{0,8},{1,17},{2,10},{3,19},{4,12},{5,21},{6,14},{7,23},{8,0},{9,25... | collective-permute-start | bytes 1769480 | tf_op jit(solution)/shard_map/ppermute | solution.py:72
  205.7 28.5 %collective-permute-start.53 = (bf16[2,4,96,768]{3,2,1,0:T(8,128)(2,1)S(1)}, bf16[2,4,96,768]{3,2,1,0:T(8,128)(2,1)S(1)}, u32[]{:S(2)}, u32[]{:S(2)}) collective-permute-start(bf16[2,4,96,768]{3,2,1,0:T(8,128)(2,1)S(1)} %leave.12), channel_id=1, source_target_pairs={{0,16},{1,9},{2,18},{3,11},{4,20},{5,13},{6,22},{7,15},{8,24},{9,1... | collective-permute-start | bytes 3538952 | tf_op jit(solution)/shard_map/ppermute | solution.py:72
  224.5 15.0 %collective-permute-start.61 = (bf16[24,3072]{1,0:T(8,128)(2,1)S(1)}, bf16[24,3072]{1,0:T(8,128)(2,1)S(1)}, u32[]{:S(2)}, u32[]{:S(2)}) collective-permute-start(bf16[24,3072]{1,0:T(8,128)(2,1)S(1)} %get-tuple-element.294), channel_id=1, source_target_pairs={{0,4},{1,5},{2,6},{3,7},{4,0},{5,1},{6,2},{7,3},{8,12},{9,13},{10,... | collective-permute-start | bytes 442376 | tf_op jit(solution)/shard_map/ppermute | solution.py:72
  224.6 15.0 %collective-permute-start.62 = (bf16[24,3072]{1,0:T(8,128)(2,1)S(1)}, bf16[24,3072]{1,0:T(8,128)(2,1)S(1)}, u32[]{:S(2)}, u32[]{:S(2)}) collective-permute-start(bf16[24,3072]{1,0:T(8,128)(2,1)S(1)} %get-tuple-element.295), channel_id=1, source_target_pairs={{0,6},{1,7},{2,0},{3,1},{4,2},{5,3},{6,4},{7,5},{8,14},{9,15},{10,... | collective-permute-start | bytes 442376 | tf_op jit(solution)/shard_map/ppermute | solution.py:72
  227.9 21.6 %collective-permute-start.57 = (bf16[4,4,2,24,768]{4,3,2,1,0:T(8,128)(2,1)S(1)}, bf16[4,4,2,24,768]{4,3,2,1,0:T(8,128)(2,1)S(1)}, u32[]{:S(2)}, u32[]{:S(2)}) collective-permute-start(bf16[4,4,2,24,768]{4,3,2,1,0:T(8,128)(2,1)S(1)} %bitcast.152), channel_id=1, source_target_pairs={{0,1},{1,0},{2,3},{3,2},{4,5},{5,4},{6,7},{7,6},{8,9},{9,8},{10,11... | collective-permute-start | bytes 3538952 | tf_op jit(solution)/shard_map/ppermute | solution.py:72
  251.0 18.5 %collective-permute-start.63 = (bf16[2,4,104,768]{3,2,1,0:T(8,128)(2,1)S(1)}, bf16[2,4,104,768]{3,2,1,0:T(8,128)(2,1)S(1)}, u32[]{:S(2)}, u32[]{:S(2)}) collective-permute-start(bf16[2,4,104,768]{3,2,1,0:T(8,128)(2,1)S(1)} %leave.14), channel_id=1, source_target_pairs={{0,16},{1,9},{2,18},{3,11},{4,20},{5,13},{6,22},{7,15},{8,24},{9,1... | collective-permute-start | bytes 3833864 | tf_op jit(solution)/shard_map/ppermute | solution.py:72
  (96 other events, 894.7 us)
where the time goes:
time: 305 us; the launch traced here: 299 us
  waiting for transfers between devices  121 us (40%)
  starting transfers between devices  67 us (22%)
  matrix products  49.1 us (16%)
  Pallas kernels  45.4 us (15%)
  other arithmetic  9.21 us (3%)
  local copies, waits for them, and re-layouts  4.8 us (2%)
    ppermute x71, waiting for transfers between devices, permute(): return lax.ppermute(value, AXES, pairs)  121 us
    ppermute x71, starting transfers between devices, permute(): return lax.ppermute(value, AXES, pairs)  67 us
    dot_general x10, matrix products, dot_nt(): lax.dot_general(a, b, (((1,), (1,)), ((), ())), preferred_element_type=F32)  22.1 us
    dot_general x10, matrix products, dot_nn(): return jnp.dot(a, b, preferred_element_type=F32)  14.4 us
    pallas_call x8, Pallas kernels, copy_call(): pl.pallas_call(functools.partial(copy_kernel, plan, len(ins)), grid_spec=...  12.9 us
    dot_general x10, matrix products, dot_tn(): lax.dot_general(a, b, (((0,), (0,)), ((), ())), preferred_element_type=F32)  12.6 us
    pallas_call x2, Pallas kernels, attend_back(): pl.pallas_call(attend_back_kernel, grid=(count,), in_specs=[block(rows),...  9.3 us
    pallas_call x8, Pallas kernels, leave(): pl.pallas_call(functools.partial(leave_kernel, len(self.blocks), step), g...  7.82 us
  transfers between devices with their start and end apart: 71, of which 30 were waited for; matrix products, arithmetic and copies ran while one was open for 16% of the time, Pallas kernels for 12%

commit v1 on v0

--- a/solution.py
+++ b/solution.py
@@ -19,6 +19,7 @@
 BF = jnp.bfloat16
 F32 = jnp.float32
 QUICK = pl.CostEstimate(flops=1000, bytes_accessed=1000, transcendentals=0)
+LONG = pl.CostEstimate(flops=10**11, bytes_accessed=10**6, transcendentals=0)
 
 
 class Place:
@@ -154,55 +155,76 @@
     def share(self, held):
         return self.place.across_cores(self.blocks[held])
 
+    def half(self, *earlier):
+        place = self.place
+        ins = after([self.blocks[m] for m in range(place.dp_count)], *earlier)
+        plan = [
+            (m, lambda s: (slice(None),), 0, lambda s, m=m: (s[m],))
+            for m in range(place.dp_count)
+        ]
+        shape = jax.ShapeDtypeStruct((place.dp_count,) + ins[0].shape, BF)
+        self.own_half = copy_call(place, plan, ins, [shape], "half")[0]
+        self.other_half = place.across_cores(self.own_half)
+        return self.own_half
+
     def spread(self, parts, *earlier):
         place = self.place
-        others = [self.share(m) for m in range(place.dp_count)]
-        ins = [self.blocks[m] for m in range(place.dp_count)] + others
+        cols = self.local.shape[1]
+        whole = slice(None)
+        if hasattr(self, "other_half"):
+            ins = [self.own_half, self.other_half]
+            places = [lambda s: (whole,), lambda s: (whole,)]
+        else:
+            ins = [self.blocks[m] for m in range(place.dp_count)]
+            ins += [self.share(m) for m in range(place.dp_count)]
+            places = [lambda s, m=m: (s[m],) for m in range(2 * place.dp_count)]
         ins = after(ins, *earlier)
-        cols = self.local.shape[1]
         plan, outs = [], []
         for out, (first, rows) in enumerate(parts):
             outs.append(
                 jax.ShapeDtypeStruct((place.dp_count, place.chips, 2, rows, cols), BF)
             )
-            for m in range(2 * place.dp_count):
-                core = place.core_at + (m >= place.dp_count)
+            for m, where in enumerate(places):
+                core = place.core_at + (m >= len(places) // 2)
+                lead = (whole,) * (ins[m].ndim - 2)
                 plan.append(
                     (
                         m,
-                        lambda s, a=first, n=rows: (slice(None), pl.ds(a, n)),
+                        lambda s, a=first, n=rows, lead=lead: lead + (pl.ds(a, n),),
                         out,
-                        lambda s, m=m, core=core: (s[m], slice(None), s[core]),
+                        lambda s, where=where, core=core: where(s) + (whole, s[core]),
                     )
                 )
-        whole = copy_call(place, plan, ins, outs, "spread")
-        return [w.reshape(-1, cols) for w in whole]
-
-
-def sum_refs(refs, n, arrived):
-    parts = []
-    for mine, other in zip(refs[:n], refs[n : 2 * n]):
-        shape = mine.shape[-2:]
-        lead = mine.shape[1:2]
-        parts.append(
-            (mine[...].astype(F32) + other[...].astype(F32)).reshape(lead + shape)
-        )
-    value = parts[0] if n == 1 else jnp.concatenate(parts, axis=1)
-    for a in refs[2 * n : 2 * n + arrived]:
+        full = copy_call(place, plan, ins, outs, "spread")
+        return [w.reshape(-1, cols) for w in full]
+
+
+def side_by_side(refs):
+    parts = [r[...].reshape(r.shape[1:2] + r.shape[-2:]) for r in refs]
+    return parts[0] if len(parts) == 1 else jnp.concatenate(parts, axis=1)
+
+
+def exchange_kernel(spots_ref, *refs):
+    out = refs[-1]
+    out[...] = side_by_side(refs[:-1]).reshape(out.shape)
+
+
+def sum_refs(refs, n):
+    value = side_by_side(refs[:n]).astype(F32)
+    for a in refs[n:]:
         value = value + a[...].astype(F32).reshape(value.shape)
     return value
 
 
-def leave_kernel(n, arrived, spots_ref, *refs):
+def leave_kernel(n, spots_ref, *refs):
     out = refs[-1]
-    out[...] = sum_refs(refs[:-1], n, arrived).astype(BF).reshape(out.shape)
-
-
-def last_kernel(n, arrived, chips, spots_ref, *refs):
-    each = 2 * n + arrived
+    out[...] = sum_refs(refs[:-1], n).astype(BF).reshape(out.shape)
+
+
+def last_kernel(n, each, chips, spots_ref, *refs):
     outs = refs[chips * each :]
     for k in range(chips):
-        value = sum_refs(refs[k * each : (k + 1) * each], n, arrived)
+        value = sum_refs(refs[k * each : (k + 1) * each], n)
         outs[k][...] = value.astype(outs[k].dtype).reshape(outs[k].shape)
 
 
@@ -231,13 +253,40 @@
         self.blocks = blocks
         self.rows = sum(b.shape[3] for b in blocks)
         self.cols = blocks[0].shape[4]
-        self.others = [place.across_cores(b) for b in blocks]
+        shape = (place.dp_count, place.chips, self.rows, self.cols)
+        sent = self.call(
+            exchange_kernel,
+            (place.dp_count,),
+            [
+                pl.BlockSpec(
+                    (1, place.chips, 1) + b.shape[3:],
+                    lambda i, s: (i, 0, s[place.core_at + 1], 0, 0),
+                )
+                for b in blocks
+            ],
+            pl.BlockSpec((1,) + shape[1:], lambda i, s: (i, 0, 0, 0)),
+            jax.ShapeDtypeStruct(shape, BF),
+            "exchange",
+        )(place.spots, *blocks)
+        self.other = place.across_cores(sent)
         self.got = []
+
+    def call(self, kernel, grid, in_specs, out_specs, out_shape, name):
+        return pl.pallas_call(
+            kernel,
+            grid_spec=pltpu.PrefetchScalarGridSpec(
+                num_scalar_prefetch=1, grid=grid, in_specs=in_specs, out_specs=out_specs
+            ),
+            out_shape=out_shape,
+            compiler_params=pltpu.CompilerParams(vmem_limit_bytes=24 << 20),
+            cost_estimate=QUICK,
+            name=name,
+        )
 
     def leave(self, step, *earlier):
         place = self.place
         if step == 0:
-            self.others = after(self.others, *earlier)
+            self.other = after(self.other, *earlier)
         else:
             self.got[-1] = after(self.got[-1], *earlier)
         count = 1 << (place.bits - 1 - step)
@@ -246,34 +295,29 @@
         def spot(i, s):
             return s[(1 << step) + i * (2 << step)]
 
+        shape = (count, chips, self.rows, self.cols)
         specs = [
             pl.BlockSpec(
                 (1, chips, 1) + b.shape[3:], lambda i, s: (spot(i, s), 0, s[core], 0, 0)
             )
             for b in self.blocks
-        ] * 2
+        ]
+        specs.append(pl.BlockSpec((1,) + shape[1:], lambda i, s: (spot(i, s), 0, 0, 0)))
         for t in range(step):
             specs.append(
                 pl.BlockSpec(
-                    (1, chips, self.rows, self.cols),
+                    (1,) + shape[1:],
                     lambda i, s, t=t: ((1 << (step - t - 1)) + i * (1 << (step - t)), 0, 0, 0),
                 )
             )
-        sent = pl.pallas_call(
-            functools.partial(leave_kernel, len(self.blocks), step),
-            grid_spec=pltpu.PrefetchScalarGridSpec(
-                num_scalar_prefetch=1,
-                grid=(count,),
-                in_specs=specs,
-                out_specs=pl.BlockSpec(
-                    (1, chips, self.rows, self.cols), lambda i, s: (i, 0, 0, 0)
-                ),
-            ),
-            out_shape=jax.ShapeDtypeStruct((count, chips, self.rows, self.cols), BF),
-            compiler_params=pltpu.CompilerParams(vmem_limit_bytes=24 << 20),
-            cost_estimate=QUICK,
-            name="leave",
-        )(place.spots, *self.blocks, *self.others, *self.got)
+        sent = self.call(
+            functools.partial(leave_kernel, len(self.blocks)),
+            (count,),
+            specs,
+            pl.BlockSpec((1,) + shape[1:], lambda i, s: (i, 0, 0, 0)),
+            jax.ShapeDtypeStruct(shape, BF),
+            "leave",
+        )(place.spots, *self.blocks, self.other, *self.got)
         self.got.append(place.across_step(sent, step))
         return sent
 
@@ -284,7 +328,7 @@
         specs, ins = [], []
         for k in range(chips):
             up = place.up_at + k
-            for b in self.blocks + self.others:
+            for b in self.blocks:
                 ins.append(b)
                 specs.append(
                     pl.BlockSpec(
@@ -292,26 +336,24 @@
                         lambda i, s, up=up: (s[0], s[up], s[core], 0, 0),
                     )
                 )
-            for g in self.got:
+            for n, g in enumerate([self.other] + self.got):
                 ins.append(g)
                 specs.append(
                     pl.BlockSpec(
-                        (1, 1, self.rows, self.cols), lambda i, s, up=up: (0, s[up], 0, 0)
+                        (1, 1, self.rows, self.cols),
+                        lambda i, s, up=up, n=n: (s[0] if n == 0 else 0, s[up], 0, 0),
                     )
                 )
-        flat = pl.BlockSpec((self.rows, self.cols), lambda i, s: (0, 0))
-        own, *sent = pl.pallas_call(
-            functools.partial(last_kernel, len(self.blocks), place.bits, chips),
-            grid_spec=pltpu.PrefetchScalarGridSpec(
-                num_scalar_prefetch=1, grid=(1,), in_specs=specs, out_specs=[flat] * chips
-            ),
-            out_shape=[
+        own, *sent = self.call(
+            functools.partial(last_kernel, len(self.blocks), len(ins) // chips, chips),
+            (1,),
+            specs,
+            [pl.BlockSpec((self.rows, self.cols), lambda i, s: (0, 0))] * chips,
+            [
                 jax.ShapeDtypeStruct((self.rows, self.cols), F32 if k == 0 else BF)
                 for k in range(chips)
             ],
-            compiler_params=pltpu.CompilerParams(vmem_limit_bytes=24 << 20),
-            cost_estimate=QUICK,
-            name="last",
+            "last",
         )(place.spots, *ins)
         self.own = own
         self.came = [place.along_chips(v, k + 1) for k, v in enumerate(sent)]
@@ -415,61 +457,294 @@
             jax.ShapeDtypeStruct(queries.shape, BF),
             jax.ShapeDtypeStruct((count, H, key_rows, rows), BF),
         ],
-        compiler_params=pltpu.CompilerParams(vmem_limit_bytes=20 << 20),
+        compiler_params=pltpu.CompilerParams(vmem_limit_bytes=14 << 20),
         cost_estimate=QUICK,
         name="attend",
     )(start, length, queries, keys, values)
 
 
-def attend_back_kernel(
-    q_ref, k_ref, v_ref, p_ref, g_ref, dq_ref, dk_ref, dv_ref, moved_ref, ds_ref
+def norm_parts(summed):
+    centre = summed - jnp.mean(summed, axis=-1, keepdims=True)
+    scale = lax.rsqrt(jnp.mean(centre * centre, axis=-1, keepdims=True) + EPS)
+    return centre * scale, scale
+
+
+def row_sum(value):
+    return jnp.sum(value.astype(F32), axis=0, keepdims=True)
+
+
+def norm_back_sums(summed, gain, grad):
+    normal, scale = norm_parts(summed)
+    inner = grad * gain
+    back = scale * (
+        inner
+        - jnp.mean(inner, axis=-1, keepdims=True)
+        - normal * jnp.mean(inner * normal, axis=-1, keepdims=True)
+    )
+    return back, [row_sum(grad * normal), row_sum(grad)]
+
+
+def put_rows(ref, rows):
+    for i, r in enumerate(rows):
+        ref[i : i + 1] = r
+
+
+def hidden_back_kernel(df_ref, c_ref, slope_ref, du_ref, sum_ref):
+    du = (dot_nt(df_ref[...], c_ref[...]) * slope_ref[...].astype(F32)).astype(BF)
+    du_ref[...] = du
+    sum_ref[...] = row_sum(du)
+
+
+def hidden_back(df, contract, slope):
+    tokens = df.shape[0]
+    return pl.pallas_call(
+        hidden_back_kernel,
+        grid=(FF // D,),
+        in_specs=[
+            pl.BlockSpec((tokens, D), lambda j: (0, 0)),
+            pl.BlockSpec((D, D), lambda j: (j, 0)),
+            pl.BlockSpec((tokens, D), lambda j: (0, j)),
+        ],
+        out_specs=[
+            pl.BlockSpec((tokens, D), lambda j: (0, j)),
+            pl.BlockSpec((1, D), lambda j: (0, j)),
+        ],
+        out_shape=[
+            jax.ShapeDtypeStruct((tokens, FF), BF),
+            jax.ShapeDtypeStruct((1, FF), F32),
+        ],
+        compiler_params=pltpu.CompilerParams(vmem_limit_bytes=16 << 20),
+        cost_estimate=LONG,
+        name="hidden_back",
+    )(df, contract, slope)
+
+
+def expand_back_kernel(
+    x_ref, du_ref, e_ref, dr3_ref, r2_ref, gain_ref, de_ref, dr2_ref, dc_ref, sum_ref, xt_ref
 ):
-    for h in range(H):
-        moved_ref[h] = dot_nt(v_ref[:, head(h)], g_ref[:, head(h)])
-    for h in range(H):
-        weights = p_ref[0, h].astype(F32)
-        moved = moved_ref[h]
-        centre = jnp.sum(weights * moved, axis=0, keepdims=True)
-        ds_ref[h] = (weights * (moved - centre)).astype(BF)
-    keys_t = k_ref[...].T
-    dq, dk, dv = [], [], []
-    for h in range(H):
-        dk.append(dot_nn(ds_ref[h], q_ref[:, head(h)]))
-        dv.append(dot_nn(p_ref[0, h], g_ref[:, head(h)]))
-        dq.append(dot_nn(keys_t[head(h)], ds_ref[h]))
-    dq_ref[...] = jnp.concatenate(dq, axis=0).T.astype(BF)
-    dk_ref[...] = jnp.concatenate(dk, axis=1).astype(BF)
-    dv_ref[...] = jnp.concatenate(dv, axis=1).astype(BF)
-
-
-def attend_back(queries, keys, values, weights, grads, count):
-    rows = queries.shape[0] // count
-    key_rows = keys.shape[0] // count
-    block = lambda n: pl.BlockSpec((n, D), lambda s: (s, 0))
+    j = pl.program_id(0)
+
+    @pl.when(j == 0)
+    def _():
+        xt_ref[...] = x_ref[...].T
+        dr2_ref[...] = dr3_ref[...]
+
+    du = du_ref[...]
+    de_ref[...] = dot_nn(xt_ref[...], du).astype(BF)
+    dr2_ref[...] += dot_nt(du, e_ref[...])
+
+    @pl.when(j == pl.num_programs(0) - 1)
+    def _():
+        back, sums = norm_back_sums(r2_ref[...], gain_ref[...], dr2_ref[...])
+        dc = back.astype(BF)
+        dr2_ref[...] = back
+        dc_ref[...] = dc
+        put_rows(sum_ref, sums + [row_sum(dc)])
+
+
+def expand_back(x2b, du, expand, dr3, r2, gain):
+    tokens = x2b.shape[0]
+    still = pl.BlockSpec((tokens, D), lambda j: (0, 0))
+    moving = lambda n: pl.BlockSpec((n, D), lambda j: (0, j))
     return pl.pallas_call(
-        attend_back_kernel,
-        grid=(count,),
+        expand_back_kernel,
+        grid=(FF // D,),
         in_specs=[
-            block(rows),
-            block(key_rows),
-            block(key_rows),
-            pl.BlockSpec((1, H, key_rows, rows), lambda s: (s, 0, 0, 0)),
-            block(rows),
-        ],
-        out_specs=[block(rows), block(key_rows), block(key_rows)],
+            still,
+            moving(tokens),
+            moving(D),
+            still,
+            still,
+            pl.BlockSpec((1, D), lambda j: (0, 0)),
+        ],
+        out_specs=[moving(D), still, still, pl.BlockSpec((8, D), lambda j: (0, 0))],
         out_shape=[
-            jax.ShapeDtypeStruct(queries.shape, BF),
-            jax.ShapeDtypeStruct(keys.shape, BF),
-            jax.ShapeDtypeStruct(keys.shape, BF),
+            jax.ShapeDtypeStruct((D, FF), BF),
+            jax.ShapeDtypeStruct((tokens, D), F32),
+            jax.ShapeDtypeStruct((tokens, D), BF),
+            jax.ShapeDtypeStruct((8, D), F32),
+        ],
+        scratch_shapes=[pltpu.VMEM((D, tokens), BF)],
+        compiler_params=pltpu.CompilerParams(vmem_limit_bytes=24 << 20),
+        cost_estimate=LONG,
+        name="expand_back",
+    )(x2b, du, expand, dr3, r2, gain)
+
+
+def heads_back(count, q_ref, k_ref, v_ref, p_ref, g_ref, outs, moved_ref, ds_ref):
+    rows = q_ref.shape[0] // count
+    keys = k_ref.shape[0] // count
+    for s in range(count):
+        at = slice(s * rows, (s + 1) * rows)
+        key_at = slice(s * keys, (s + 1) * keys)
+        for h in range(H):
+            moved_ref[h] = dot_nt(v_ref[key_at, head(h)], g_ref[at, head(h)])
+        for h in range(H):
+            weights = p_ref[s, h].astype(F32)
+            moved = moved_ref[h]
+            centre = jnp.sum(weights * moved, axis=0, keepdims=True)
+            ds_ref[h] = (weights * (moved - centre)).astype(BF)
+        keys_t = k_ref[key_at].T
+        dq, dk, dv = [], [], []
+        for h in range(H):
+            dk.append(dot_nn(ds_ref[h], q_ref[at, head(h)]))
+            dv.append(dot_nn(p_ref[s, h], g_ref[at, head(h)]))
+            dq.append(dot_nn(keys_t[head(h)], ds_ref[h]))
+        outs[0][at] = (jnp.concatenate(dq, axis=0).T.astype(BF) * 0.125).astype(BF)
+        outs[1][key_at] = jnp.concatenate(dk, axis=1).astype(BF)
+        outs[2][key_at] = jnp.concatenate(dv, axis=1).astype(BF)
+
+
+def cross_back_kernel(
+    count,
+    dc_ref,
+    co_ref,
+    cq_ref,
+    q_ref,
+    k_ref,
+    v_ref,
+    p_ref,
+    o_ref,
+    x_ref,
+    m_ref,
+    dr2_ref,
+    r1_ref,
+    gain_ref,
+    os_ref,
+    dwq_ref,
+    dwk_ref,
+    dwv_ref,
+    dwo_ref,
+    dso_ref,
+    dk_ref,
+    dv_ref,
+    dr1_ref,
+    da_ref,
+    sum_ref,
+    g_ref,
+    dq_ref,
+    moved_ref,
+    ds_ref,
+):
+    dc = dc_ref[...]
+    g_ref[...] = dot_nt(dc, co_ref[...]).astype(BF)
+    dwo_ref[...] = dot_tn(o_ref[...], dc).astype(BF)
+    heads_back(
+        count, q_ref, k_ref, v_ref, p_ref, g_ref, (dq_ref, dk_ref, dv_ref), moved_ref, ds_ref
+    )
+    dq = dq_ref[...]
+    dr1 = dr2_ref[...] + dot_nt(dq, cq_ref[...])
+    dwq_ref[...] = dot_tn(x_ref[...], dq).astype(BF)
+    mt = m_ref[...].T
+    dwk_ref[...] = dot_nn(mt, dk_ref[...]).astype(BF)
+    dwv_ref[...] = dot_nn(mt, dv_ref[...]).astype(BF)
+    back, sums = norm_back_sums(r1_ref[...], gain_ref[...], dr1)
+    da = back.astype(BF)
+    dr1_ref[...] = back
+    da_ref[...] = da
+    dso_ref[...] = dot_tn(os_ref[...], da).astype(BF)
+    put_rows(sum_ref, sums + [row_sum(da), row_sum(dq), row_sum(dv_ref[...])])
+
+
+def cross_back(dc, co, cq, q2, k2, v2, p2, o2, x1b, memory, dr2, r1, gain, o, count):
+    tokens, rows = dc.shape[0], dc.shape[0] // count
+    keys = memory.shape[0] // count
+    square = jax.ShapeDtypeStruct((D, D), BF)
+    low = jax.ShapeDtypeStruct((tokens, D), BF)
+    return pl.pallas_call(
+        functools.partial(cross_back_kernel, count),
+        out_shape=[square] * 5
+        + [
+            jax.ShapeDtypeStruct(memory.shape, BF),
+            jax.ShapeDtypeStruct(memory.shape, BF),
+            jax.ShapeDtypeStruct((tokens, D), F32),
+            low,
+            jax.ShapeDtypeStruct((8, D), F32),
         ],
         scratch_shapes=[
-            pltpu.VMEM((H, key_rows, rows), F32),
-            pltpu.VMEM((H, key_rows, rows), BF),
-        ],
-        compiler_params=pltpu.CompilerParams(vmem_limit_bytes=24 << 20),
-        cost_estimate=QUICK,
-        name="attend_back",
-    )(queries, keys, values, weights, grads)
+            pltpu.VMEM((tokens, D), BF),
+            pltpu.VMEM((tokens, D), BF),
+            pltpu.VMEM((H, keys, rows), F32),
+            pltpu.VMEM((H, keys, rows), BF),
+        ],
+        compiler_params=pltpu.CompilerParams(vmem_limit_bytes=18 << 20),
+        cost_estimate=LONG,
+        name="cross_back",
+    )(dc, co, cq, q2, k2, v2, p2, o2, x1b, memory, dr2, r1, gain, o)
+
+
+def self_back_kernel(
+    count,
+    da_ref,
+    wo_ref,
+    q_ref,
+    k_ref,
+    v_ref,
+    p_ref,
+    x_ref,
+    dwq_ref,
+    dwk_ref,
+    dwv_ref,
+    dq_ref,
+    dk_ref,
+    dv_ref,
+    sum_ref,
+    g_ref,
+    moved_ref,
+    ds_ref,
+):
+    g_ref[...] = dot_nt(da_ref[...], wo_ref[...]).astype(BF)
+    heads_back(
+        count, q_ref, k_ref, v_ref, p_ref, g_ref, (dq_ref, dk_ref, dv_ref), moved_ref, ds_ref
+    )
+    xt = x_ref[...].T
+    dwq_ref[...] = dot_nn(xt, dq_ref[...]).astype(BF)
+    dwk_ref[...] = dot_nn(xt, dk_ref[...]).astype(BF)
+    dwv_ref[...] = dot_nn(xt, dv_ref[...]).astype(BF)
+    put_rows(sum_ref, [row_sum(dq_ref[...]), row_sum(dv_ref[...])])
+
+
+def self_back(da, wo, q, k, v, p, x, count):
+    tokens, rows = da.shape[0], da.shape[0] // count
+    square = jax.ShapeDtypeStruct((D, D), BF)
+    low = jax.ShapeDtypeStruct((tokens, D), BF)
+    return pl.pallas_call(
+        functools.partial(self_back_kernel, count),
+        out_shape=[square] * 3 + [low] * 3 + [jax.ShapeDtypeStruct((8, D), F32)],
+        scratch_shapes=[
+            pltpu.VMEM((tokens, D), BF),
+            pltpu.VMEM((H, rows, rows), F32),
+            pltpu.VMEM((H, rows, rows), BF),
+        ],
+        compiler_params=pltpu.CompilerParams(vmem_limit_bytes=14 << 20),
+        cost_estimate=LONG,
+        name="self_back",
+    )(da, wo, q, k, v, p, x)
+
+
+def inputs_back_kernel(
+    dq_ref, dk_ref, dv_ref, wq_ref, wk_ref, wv_ref, dr1_ref, dk2_ref, dv2_ref, ck_ref, cv_ref, dx_ref, de_ref
+):
+    de_ref[...] = dot_nt(dk2_ref[...], ck_ref[...]) + dot_nt(dv2_ref[...], cv_ref[...])
+    dx_ref[...] = (
+        dr1_ref[...]
+        + dot_nt(dq_ref[...], wq_ref[...])
+        + dot_nt(dk_ref[...], wk_ref[...])
+        + dot_nt(dv_ref[...], wv_ref[...])
+    )
+
+
+def inputs_back(dq, dk, dv, wq, wk, wv, dr1, dk2, dv2, ck, cv):
+    return pl.pallas_call(
+        inputs_back_kernel,
+        out_shape=[
+            jax.ShapeDtypeStruct(dr1.shape, F32),
+            jax.ShapeDtypeStruct(dk2.shape, F32),
+        ],
+        compiler_params=pltpu.CompilerParams(vmem_limit_bytes=10 << 20),
+        cost_estimate=LONG,
+        name="inputs_back",
+    )(dq, dk, dv, wq, wk, wv, dr1, dk2, dv2, ck, cv)
 
 
 def norm(summed):
@@ -568,13 +843,32 @@
     )(gathered)
 
 
-def split_small_kernel(n, wide, *refs):
-    *vectors, eb_ref, out_ref = refs
-    rows = [v[...].reshape(1, D) for v in vectors]
+def split_small_kernel(n, wide, ff_ref, cross_ref, self_ref, db_ref, g3_ref, s3_ref, eb_ref, out_ref):
     zero = jnp.zeros((1, D), F32)
-    first = jnp.concatenate(rows[:7] + [zero], axis=0)
-    second = jnp.concatenate(rows[7:] + [zero, zero], axis=0)
-    tail = jnp.broadcast_to(eb_ref[...].reshape(1, FF), (8, FF))
+    first = jnp.concatenate(
+        [
+            self_ref[0:2],
+            cross_ref[2:5],
+            ff_ref[2:3],
+            db_ref[...].reshape(1, D),
+            zero,
+        ],
+        axis=0,
+    )
+    second = jnp.concatenate(
+        [
+            cross_ref[0:1],
+            ff_ref[0:1],
+            g3_ref[...].reshape(1, D),
+            cross_ref[1:2],
+            ff_ref[1:2],
+            s3_ref[...].reshape(1, D),
+            zero,
+            zero,
+        ],
+        axis=0,
+    )
+    tail = jnp.broadcast_to(eb_ref[...], (8, FF))
 
     def padded(v, width):
         return jnp.concatenate([v, jnp.zeros((8, width - v.shape[1]), F32)], axis=1)
@@ -590,7 +884,7 @@
         ).astype(BF)
 
 
-def split_small(vectors, eb, n, wide):
+def split_small(ff_sums, cross_sums, self_sums, vectors, eb, n, wide):
     devices = D // n
     return pl.pallas_call(
         functools.partial(split_small_kernel, n, wide),
@@ -598,7 +892,7 @@
         compiler_params=pltpu.CompilerParams(vmem_limit_bytes=8 << 20),
         cost_estimate=QUICK,
         name="split_small",
-    )(*vectors, eb)
+    )(ff_sums, cross_sums, self_sums, *vectors, eb)
 
 
 def body(
@@ -654,8 +948,10 @@
         line = g_cross.column()
         g_cross.hop(0, 0)
         g_cross.hop(1, 0)
-        g_expand = Gather(place, after(expand_weight, line))
-        *w_self, smalls = g_self.spread(four + [(4 * rows, 8)], line)
+        g_self.blocks[3] = after(g_self.blocks[3], line)
+        g_expand = Gather(place, after(expand_weight, g_self.blocks[3]))
+        g_self.half(line)
+        *w_self, smalls = g_self.spread(four + [(4 * rows, 8)])
         smalls = smalls.reshape(-1, 8, D)
     else:
         whole = lax.all_gather(
@@ -698,13 +994,16 @@
         line = g_expand.column(o)
         g_expand.hop(0, 0)
         g_expand.hop(1, 0)
-        g_contract = Gather(place, after(contract_weight, line))
+        g_cross.blocks[3] = after(g_cross.blocks[3], line)
+        g_contract = Gather(place, after(contract_weight, g_cross.blocks[3]))
         o = after(o, line)
-    n1, s1 = norm(x.astype(F32) + (dot_nn(o, wo) + biases[2]))
+    r1 = x.astype(F32) + (dot_nn(o, wo) + biases[2])
+    n1, s1 = norm(r1)
     x1 = n1 * gains[0] + shifts[0]
     x1b = x1.astype(BF)
     if fits:
-        w_cross = g_cross.spread(four, x1b)
+        g_cross.half(x1b)
+        w_cross = g_cross.spread(four)
     cq, ck, cv, co = w_cross
     q2 = ((dot_nn(x1b, cq) + biases[3]) * 0.125).astype(BF)
     k2 = dot_nn(memory, ck).astype(BF)
@@ -715,12 +1014,15 @@
         line = g_contract.column(o2)
         g_contract.hop(0, 0)
         g_contract.hop(1, 0)
+        g_expand.blocks[3] = after(g_expand.blocks[3], line)
         o2 = after(o2, line)
-    n2, s2 = norm(x1 + (dot_nn(o2, co) + biases[5]))
+    r2 = x1 + (dot_nn(o2, co) + biases[5])
+    n2, s2 = norm(r2)
     x2 = n2 * gains[1] + shifts[1]
     x2b = x2.astype(BF)
     if fits:
-        (expand,) = g_expand.spread([(0, rows)], x2b)
+        g_expand.half(x2b)
+        (expand,) = g_expand.spread([(0, rows)])
     act, slope = gelu_and_slope(dot_nn(x2b, expand) + expand_b)
     act = act.astype(BF)
     slope = slope.astype(BF)
@@ -735,74 +1037,57 @@
     d_contract = dot_tn(act, df).astype(BF)
     r_contract = reduce(place, [owner_blocks(place, d_contract)])
     d_contract_b = column_sum(df)
-    df2 = after(df, d_contract)
-    du = (dot_nt(df2, contract) * slope.astype(F32)).astype(BF)
-    d_expand_b = column_sum(du)
-
-    hop = r_contract.leave(0, du)
-    d_expand = dot_tn(x2b, after(du, hop)).astype(BF)
-    r_expand = reduce(place, [owner_blocks(place, d_expand)])
-    dr2, gain2, shift2 = norm_back(
-        n2, s2, gains[1], dr3 + dot_nt(after(du, d_expand), expand)
-    )
-    dc = dr2.astype(BF)
-    hop = r_contract.leave(1, dc)
-    hop2 = r_expand.leave(0, dc)
-    dc2 = after(dc, hop, hop2)
-    d_co = dot_tn(o2, dc2).astype(BF)
-    do2 = dot_nt(dc2, co).astype(BF)
-    dq2, dk2, dv2 = attend_back(q2, k2, v2, p2, after(do2, d_co), count)
-    dq2 = dq2 * BF(0.125)
-
-    sent = r_contract.last(dq2)
-    hop2 = r_expand.leave(1, dq2)
-    dq2, dk2, dv2 = after((dq2, dk2, dv2), sent, hop2)
-    d_cross = [dot_tn(x1b, dq2), dot_tn(memory, dk2), dot_tn(memory, dv2)]
-    d_cross = [d.astype(BF) for d in d_cross]
-    r_cross = reduce(place, [owner_blocks(place, d) for d in d_cross + [d_co]])
-    dq2, dk2, dv2 = after((dq2, dk2, dv2), d_cross)
-
-    dr1, gain1, shift1 = norm_back(n1, s1, gains[0], dr2 + dot_nt(dq2, cq))
-    da = dr1.astype(BF)
-    hop = r_cross.leave(0, da)
-    (own_contract,) = r_contract.result([((4 * rows, D), 0, 0)], da)
-    sent = r_expand.last(da)
-    da2 = after(da, hop, own_contract, sent)
-    d_so = dot_tn(o, da2).astype(BF)
-    do = dot_nt(da2, wo).astype(BF)
-    dq, dk, dv = attend_back(q, k, v, p, after(do, d_so), count)
-    dq = dq * BF(0.125)
-
-    hop = r_cross.leave(1, dq)
-    dq, dk, dv = after((dq, dk, dv), hop)
-    d_self = [dot_tn(x, dq), dot_tn(x, dk), dot_tn(x, dv)]
-    d_self = [d.astype(BF) for d in d_self]
+    du, d_expand_b = hidden_back(after(df, d_contract), contract, slope)
+    sent = r_contract.leave(0, du)
+    d_expand, dr2, dc, ff_sums = expand_back(
+        x2b, after(du, sent), expand, dr3, r2, gains[1]
+    )
+    sent = r_contract.leave(1, dc)
+    r_expand = reduce(place, [owner_blocks(place, after(d_expand, sent))])
+    sent = r_expand.leave(0, dc)
+    *d_cross, dk2, dv2, dr1, da, cross_sums = cross_back(
+        after(dc, sent), co, cq, q2, k2, v2, p2, o2, x1b, memory, dr2, r1, gains[0], o, count
+    )
+    r_cross = reduce(place, [owner_blocks(place, d) for d in d_cross])
+    sent = r_contract.last(da)
+    *d_self, dq, dk, dv, self_sums = self_back(after(da, sent), wo, q, k, v, p, x, count)
+    sent = r_expand.leave(1, self_sums)
+    sent2 = r_cross.leave(0, sent)
     small_blocks = split_small(
-        [column_sum(t) for t in (dq, dv, da, dq2, dv2, dc)]
-        + [d_contract_b, gain1, gain2, gain3, shift1, shift2, shift3],
+        ff_sums,
+        cross_sums,
+        self_sums,
+        [d_contract_b, gain3, shift3],
         d_expand_b,
         rows,
         wide,
     )
     small_blocks = small_blocks.reshape(place.dp_count, place.chips, 2, 8, D)
+    (own_contract,) = r_contract.result([((4 * rows, D), 0, 0)], self_sums, sent2)
     r_self = reduce(
-        place, [owner_blocks(place, d) for d in d_self + [d_so]] + [small_blocks]
-    )
-    (own_expand,) = r_expand.result([((rows, FF), 0, 0)], d_self, small_blocks)
-    dk2, dv2 = after((dk2, dv2), own_expand)
-    encoder_grad = dot_nt(dk2, ck) + dot_nt(dv2, cv)
-    sent = r_cross.last(encoder_grad)
-    hop = r_self.leave(0, sent)
-    dq, dk, dv = after((dq, dk, dv), hop)
-    input_grad = dr1 + dot_nt(dq, wq) + dot_nt(dk, wk) + dot_nt(dv, wv)
-    projects = [((3, rows, D), 0, 0), ((rows, D), 3 * rows, 0)]
-    own_cross = r_cross.result(projects, input_grad)
-    r_self.leave(1, own_cross)
-    r_self.last()
-    at = 4 * rows
+        place,
+        [owner_blocks(place, d) for d in after(d_self, sent2)] + [small_blocks],
+    )
+    dq, dk, dv, dk2, dv2 = after((dq, dk, dv, dk2, dv2), sent2, own_contract)
+    input_grad, encoder_grad = inputs_back(
+        dq, dk, dv, wq, wk, wv, dr1, dk2, dv2, ck, cv
+    )
+    sent = r_expand.last(input_grad)
+    sent2 = r_cross.leave(1, sent)
+    sent3 = r_self.leave(0, sent2)
+    (own_expand,) = r_expand.result([((rows, FF), 0, 0)], sent3)
+    sent = r_cross.last(own_expand)
+    sent = r_self.leave(1, sent)
+    sent = r_self.last(sent)
+    projects = ((3, rows, D), 0, 0)
+    square = (rows, D)
+    own_cross = r_cross.result(
+        [projects, (square, 3 * rows, 0), (square, 4 * rows, 0)], sent
+    )
+    at = 3 * rows
     own_self = r_self.result(
-        projects
-        + [
+        [
+            projects,
             ((6, rows), at, 0),
             ((1, wide), at, 256),
             ((1, rows), at + 6, 0),
@@ -810,6 +1095,7 @@
             ((3, rows), at + 3, 128),
         ]
     )
+    own_self = [own_self[0], own_cross[2], *own_self[1:]]
     return (
         output.reshape(shape),
         input_grad.reshape(shape),

time: 305 us -> 292 us (0.957)
  the two profiles are of different devices: /device:TPU:9 before, /device:TPU:0 now
where the time goes in v1:
time: 292 us; the launch traced here: 286 us
  waiting for transfers between devices  126 us (43%)
  Pallas kernels  74.9 us (26%)
  starting transfers between devices  53.2 us (18%)
  matrix products  17.6 us (6%)
  local copies, waits for them, and re-layouts  7.93 us (3%)
  other arithmetic  4.25 us (1%)
    ppermute x55, waiting for transfers between devices, permute(): return lax.ppermute(value, AXES, pairs)  126 us
    ppermute x55, starting transfers between devices, permute(): return lax.ppermute(value, AXES, pairs)  53.2 us
    dot_general x10, matrix products, dot_nn(): return jnp.dot(a, b, preferred_element_type=F32)  14.5 us
    pallas_call x11, Pallas kernels, copy_call(): pl.pallas_call(functools.partial(copy_kernel, plan, len(ins)), grid_spec=...  12.9 us
    pallas_call x8, Pallas kernels, leave(): self.call(functools.partial(leave_kernel, len(self.blocks)), (count,), sp...  9.65 us
    pallas_call x1, Pallas kernels, cross_back(): pl.pallas_call(functools.partial(cross_back_kernel, count), out_shape=[sq...  8.55 us
    pallas_call x1, Pallas kernels, expand_back(): pl.pallas_call(expand_back_kernel, grid=(FF // D,), in_specs=[still, movi...  7.95 us
    pallas_call x2, Pallas kernels, attend(): pl.pallas_call(functools.partial(attend_kernel, masked), grid_spec=pltpu....  7.66 us
  transfers between devices with their start and end apart: 55, of which 30 were waited for; matrix products, arithmetic and copies ran while one was open for 5% of the time, Pallas kernels for 22%

profile of v1, /device:TPU:0, one launch (start us, length us, event | category | flops | bytes accessed | tf_op | source)
XLA Modules:
  0.0 286.2 jit_solution(6022805773184079243)
XLA Ops:
  1.7 5.1 %collective-permute-start.2 = (bf16[104,768]{1,0:T(8,128)(2,1)S(1)}, bf16[104,768]{1,0:T(8,128)(2,1)S(1)}, u32[]{:S(2)}, u32[]{:S(2)}) collective-permute-start(bf16[104,768]{1,0:T(8,128)(2,1)S(1)} %pack_self.1.refs_0_), channel_id=1, source_target_pairs={{0,6},{1,7},{2,0},{3,1},{4,2},{5,3},{6,4},{7,5},{8,14},{9,15},{10,... | collective-permute-start | bytes 479240 | tf_op jit(solution)/shard_map/ppermute | solution.py:73
  11.3 9.0 %collective-permute-done.1.refs_2_ = bf16[104,768]{1,0:T(8,128)(2,1)S(1)} collective-permute-done((bf16[104,768]{1,0:T(8,128)(2,1)S(1)}, bf16[104,768]{1,0:T(8,128)(2,1)S(1)}, u32[]{:S(2)}, u32[]{:S(2)}) %collective-permute-start.1) | collective-permute-done | bytes 159776 | tf_op jit(solution)/shard_map/ppermute | solution.py:73
  30.9 8.9 %collective-permute-done.6.refs_2_ = bf16[96,768]{1,0:T(8,128)(2,1)S(1)} collective-permute-done((bf16[96,768]{1,0:T(8,128)(2,1)S(1)}, bf16[96,768]{1,0:T(8,128)(2,1)S(1)}, u32[]{:S(2)}, u32[]{:S(2)}) %collective-permute-start.6) | collective-permute-done | bytes 147488 | tf_op jit(solution)/shard_map/ppermute | solution.py:73
  41.8 8.5 %collective-permute-done.8.refs_3_ = bf16[4,104,768]{2,1,0:T(8,128)(2,1)S(1)} collective-permute-done((bf16[4,104,768]{2,1,0:T(8,128)(2,1)S(1)}, bf16[4,104,768]{2,1,0:T(8,128)(2,1)S(1)}, u32[]{:S(2)}, u32[]{:S(2)}) %collective-permute-start.8) | collective-permute-done | bytes 639008 | tf_op jit(solution)/shard_map/ppermute | solution.py:73
  61.6 3.9 %attend.2 = (bf16[512,768]{1,0:T(8,128)(2,1)S(1)}, bf16[2,12,256,256]{3,2,1,0:T(8,128)(2,1)S(1)}) custom-call(s32[2]{0:T(128)S(1)} %copy-done.21, s32[2]{0:T(128)S(1)} %copy-done.22, bf16[512,768]{1,0:T(8,128)(2,1)S(1)} %fusion.12.q_ref, bf16[512,768]{1,0:T(8,128)(2,1)S(1)} %fusion.15.k_ref, bf16[512,768]{1,0:T(8,128)(2,1)S(1)} %fusion.13.v_ref), custom_call_target="tpu_custom_call" | custom-call | flops 1000 | bytes 1000 | tf_op jit(solution)/shard_map/attend/pallas_call | solution.py:444
  72.2 7.8 %collective-permute-done.15.refs_3_ = bf16[4,96,768]{2,1,0:T(8,128)(2,1)S(1)} collective-permute-done((bf16[4,96,768]{2,1,0:T(8,128)(2,1)S(1)}, bf16[4,96,768]{2,1,0:T(8,128)(2,1)S(1)}, u32[]{:S(2)}, u32[]{:S(2)}) %collective-permute-start.15) | collective-permute-done | bytes 589856 | tf_op jit(solution)/shard_map/ppermute | solution.py:73
  91.3 3.8 %attend.3 = (bf16[512,768]{1,0:T(8,128)(2,1)S(1)}, bf16[2,12,256,256]{3,2,1,0:T(8,128)(2,1)S(1)}) custom-call(s32[2]{0:T(128)S(1)} %copy-done.21, s32[2]{0:T(128)S(1)} %copy-done.22, bf16[512,768]{1,0:T(8,128)(2,1)S(1)} %multiply_convert_fusion.1.q_ref, bf16[512,768]{1,0:T(8,128)(2,1)S(1)} %fusion.16.k_ref, bf16[512,768]{1,0:T(8,128)(2,1)S(1)} %fusion.14.v_ref), custom_call_target="tpu_custom_call" | custom-call | flops 1000 | bytes 1000 | tf_op jit(solution)/shard_map/attend/pallas_call | solution.py:444
  100.5 7.7 %collective-permute-done.22.refs_3_ = bf16[4,24,3072]{2,1,0:T(8,128)(2,1)S(1)} collective-permute-done((bf16[4,24,3072]{2,1,0:T(8,128)(2,1)S(1)}, bf16[4,24,3072]{2,1,0:T(8,128)(2,1)S(1)}, u32[]{:S(2)}, u32[]{:S(2)}) %collective-permute-start.22) | collective-permute-done | bytes 589856 | tf_op jit(solution)/shard_map/ppermute | solution.py:73
  114.8 5.1 %fusion.4 = (bf16[512,3072]{1,0:T(8,128)(2,1)S(1)}, bf16[512,3072]{1,0:T(8,128)(2,1)S(1)}) fusion(f32[3072]{0:T(1024)S(1)} %bitcast.194, bf16[512,768]{1,0:T(8,128)(2,1)S(1)} %fusion.18.x_ref, bf16[768,3072]{1,0:T(8,128)(2,1)S(1)} %bitcast.165), kind=kOutput, calls=%fused_computation.5 | convolution fusion | flops 2434793472 | bytes 11808768 | tf_op jit(solution)/shard_map/dot_general | solution.py:401
  119.9 5.4 %collective-permute-done.24.refs_1_ = bf16[4,96,768]{2,1,0:T(8,128)(2,1)S(1)} collective-permute-done((bf16[4,96,768]{2,1,0:T(8,128)(2,1)S(1)}, bf16[4,96,768]{2,1,0:T(8,128)(2,1)S(1)}, u32[]{:S(2)}, u32[]{:S(2)}) %collective-permute-start.24) | collective-permute-done | bytes 589856 | tf_op jit(solution)/shard_map/ppermute | solution.py:73
  126.0 9.2 %collective-permute-done.26.refs_3_ = bf16[4,96,768]{2,1,0:T(8,128)(2,1)S(1)} collective-permute-done((bf16[4,96,768]{2,1,0:T(8,128)(2,1)S(1)}, bf16[4,96,768]{2,1,0:T(8,128)(2,1)S(1)}, u32[]{:S(2)}, u32[]{:S(2)}) %collective-permute-start.26) | collective-permute-done | bytes 589856 | tf_op jit(solution)/shard_map/ppermute | solution.py:73
  148.0 3.9 %hidden_back.1 = (bf16[512,3072]{1,0:T(8,128)(2,1)S(1)}, f32[1,3072]{1,0:T(1,128)S(1)}) custom-call(bf16[512,768]{1,0:T(8,128)(2,1)S(1)} %get-tuple-element.249.df_ref, bf16[3072,768]{1,0:T(8,128)(2,1)S(1)} %bitcast.168, bf16[512,3072]{1,0:T(8,128)(2,1)S(1)} %get-tuple-element.358.slope_ref), custom_call_target="tpu_custom_call" | custom-call | flops 99999997952 | bytes 1000000 | tf_op jit(solution)/shard_map/hidden_back/pallas_call | solution.py:500
  154.3 8.0 %expand_back.1 = (bf16[768,3072]{1,0:T(8,128)(2,1)S(1)}, f32[512,768]{1,0:T(8,128)S(1)}, bf16[512,768]{1,0:T(8,128)(2,1)S(1)}, f32[8,768]{1,0:T(8,128)S(1)}) custom-call(bf16[512,768]{1,0:T(8,128)(2,1)S(1)} %fusion.18.x_ref, bf16[512,3072]{1,0:T(8,128)(2,1)S(1)} %get-tuple-element.252.du_ref, bf16[768,3072]{1,0:T(8,128)(2,1)S(1)} %bitcast.166, ...), custom_call_target="tpu_custom_call" | custom-call | flops 99999997952 | bytes 1000000 | tf_op jit(solution)/shard_map/expand_back/pallas_call | solution.py:549
  162.2 7.5 %collective-permute-done.32.refs_2_.refs_6_.refs_10_.refs_14_ = bf16[2,4,96,768]{3,2,1,0:T(8,128)(2,1)S(1)} collective-permute-done((bf16[2,4,96,768]{3,2,1,0:T(8,128)(2,1)S(1)}, bf16[2,4,96,768]{3,2,1,0:T(8,128)(2,1)S(1)}, u32[]{:S(2)}, u32[]{:S(2)}) %collective-permute-start.32) | collective-permute-done | bytes 1179680 | tf_op jit(solution)/shard_map/ppermute | solution.py:73
  171.9 4.2 %collective-permute-done.33.refs_1_.refs_5_.refs_9_.refs_13_ = bf16[4,4,24,3072]{3,2,1,0:T(8,128)(2,1)S(1)} collective-permute-done((bf16[4,4,24,3072]{3,2,1,0:T(8,128)(2,1)S(1)}, bf16[4,4,24,3072]{3,2,1,0:T(8,128)(2,1)S(1)}, u32[]{:S(2)}, u32[]{:S(2)}) %collective-permute-start.33) | collective-permute-done | bytes 2359328 | tf_op jit(solution)/shard_map/ppermute | solution.py:73
  180.4 8.6 %cross_back.1 = (bf16[768,768]{1,0:T(8,128)(2,1)S(1)}, bf16[768,768]{1,0:T(8,128)(2,1)S(1)}, bf16[768,768]{1,0:T(8,128)(2,1)S(1)}, bf16[768,768]{1,0:T(8,128)(2,...) custom-call(bf16[512,768]{1,0:T(8,128)(2,1)S(1)} %get-tuple-element., ...), custom_call_target="tpu_custom_call" | custom-call | flops 99999997952 | bytes 1000000 | tf_op jit(solution)/shard_map/cross_back/pallas_call | solution.py:654
  198.5 6.1 %self_back.1 = (bf16[768,768]{1,0:T(8,128)(2,1)S(1)}, bf16[768,768]{1,0:T(8,128)(2,1)S(1)}, bf16[768,768]{1,0:T(8,128)(2,1)S(1)}, bf16[512,768]{1,0:T(8,128)(2,1...) custom-call(bf16[512,768]{1,0:T(8,128)(2,1)S(1)} %copy-done.56, ...), custom_call_target="tpu_custom_call" | custom-call | flops 99999997952 | bytes 1000000 | tf_op jit(solution)/shard_map/self_back/pallas_call | solution.py:711
  214.4 4.8 %inputs_back.1 = (f32[512,768]{1,0:T(8,128)}, f32[512,768]{1,0:T(8,128)}) custom-call(bf16[512,768]{1,0:T(8,128)(2,1)S(1)} %get-tuple-element.285.dq_ref, bf16[512,768]{1,0:T(8,128)(2,1)S(1)} %copy-done.58, bf16[512,768]{1,0:T(8,128)(2,1)S(1)} %copy-done.60, bf16[768,768]{1,0:T(8,128)(2,1)S(1)} %bitcast.171, bf16[768,768]{1,0:T(8,128)(2,1)S(1)} %bitcast.173, ...), custom_call_target="tpu_custom_call" | custom-call | flops 99999997952 | bytes 1000000 | tf_op jit(solution)/shard_map/inputs_back/pallas_call | solution.py:738
  219.2 4.4 %collective-permute-done.42.refs_3_.refs_7_.refs_11_.refs_15_ = bf16[1,4,24,3072]{3,2,1,0:T(8,128)(2,1)S(1)} collective-permute-done((bf16[1,4,24,3072]{3,2,1,0:T(8,128)(2,1)S(1)}, bf16[1,4,24,3072]{3,2,1,0:T(8,128)(2,1)S(1)}, u32[]{:S(2)}, u32[]{:S(2)}) %collective-permute-start.42) | collective-permute-done | bytes 589856 | tf_op jit(solution)/shard_map/ppermute | solution.py:73
  225.6 6.4 %collective-permute-done.41.refs_6_.refs_14_.refs_22_.refs_30_ = bf16[2,4,120,768]{3,2,1,0:T(8,128)(2,1)S(1)} collective-permute-done((bf16[2,4,120,768]{3,2,1,0:T(8,128)(2,1)S(1)}, bf16[2,4,120,768]{3,2,1,0:T(8,128)(2,1)S(1)}, u32[]{:S(2)}, u32[]{:S(2)}) %collective-permute-start.41) | collective-permute-done | bytes 1474592 | tf_op jit(solution)/shard_map/ppermute | solution.py:73
  239.7 4.7 %collective-permute-done.45.refs_1_ = bf16[24,3072]{1,0:T(8,128)(2,1)S(1)} collective-permute-done((bf16[24,3072]{1,0:T(8,128)(2,1)S(1)}, bf16[24,3072]{1,0:T(8,128)(2,1)S(1)}, u32[]{:S(2)}, u32[]{:S(2)}) %collective-permute-start.45) | collective-permute-done | bytes 147488 | tf_op jit(solution)/shard_map/ppermute | solution.py:73
  244.4 5.3 %collective-permute-done.46.refs_2_ = bf16[24,3072]{1,0:T(8,128)(2,1)S(1)} collective-permute-done((bf16[24,3072]{1,0:T(8,128)(2,1)S(1)}, bf16[24,3072]{1,0:T(8,128)(2,1)S(1)}, u32[]{:S(2)}, u32[]{:S(2)}) %collective-permute-start.46) | collective-permute-done | bytes 147488 | tf_op jit(solution)/shard_map/ppermute | solution.py:73
  270.3 6.7 %collective-permute-done.53.refs_2_ = bf16[120,768]{1,0:T(8,128)(2,1)S(1)} collective-permute-done((bf16[120,768]{1,0:T(8,128)(2,1)S(1)}, bf16[120,768]{1,0:T(8,128)(2,1)S(1)}, u32[]{:S(2)}, u32[]{:S(2)}) %collective-permute-start.53) | collective-permute-done | bytes 184352 | tf_op jit(solution)/shard_map/ppermute | solution.py:73
  277.8 7.5 %collective-permute-done.50.refs_2_ = bf16[80,768]{1,0:T(8,128)(2,1)S(1)} collective-permute-done((bf16[80,768]{1,0:T(8,128)(2,1)S(1)}, bf16[80,768]{1,0:T(8,128)(2,1)S(1)}, u32[]{:S(2)}, u32[]{:S(2)}) %collective-permute-start.50) | collective-permute-done | bytes 122912 | tf_op jit(solution)/shard_map/ppermute | solution.py:73
  (291 shorter events, 131.8 us)
Async XLA Ops:
  21.7 18.1 %collective-permute-start.4 = (bf16[4,104,768]{2,1,0:T(8,128)(2,1)S(1)}, bf16[4,104,768]{2,1,0:T(8,128)(2,1)S(1)}, u32[]{:S(2)}, u32[]{:S(2)}) collective-permute-start(bf16[4,104,768]{2,1,0:T(8,128)(2,1)S(1)} %column.4.refs_0_), channel_id=1, source_target_pairs={{0,8},{1,17},{2,10},{3,19},{4,12},{5,21},{6,14},{7,23},{8,0},{9,25... | collective-permute-start | bytes 1916936 | tf_op jit(solution)/shard_map/ppermute | solution.py:73
  23.3 16.6 %collective-permute-start.3 = (bf16[4,104,768]{2,1,0:T(8,128)(2,1)S(1)}, bf16[4,104,768]{2,1,0:T(8,128)(2,1)S(1)}, u32[]{:S(2)}, u32[]{:S(2)}) collective-permute-start(bf16[4,104,768]{2,1,0:T(8,128)(2,1)S(1)} %column.4.refs_0_), channel_id=1, source_target_pairs={{0,16},{1,9},{2,18},{3,11},{4,20},{5,13},{6,22},{7,15},{8,24},{9,1... | collective-permute-start | bytes 1916936 | tf_op jit(solution)/shard_map/ppermute | solution.py:73
  51.8 16.0 %collective-permute-start.13 = (bf16[4,96,768]{2,1,0:T(8,128)(2,1)S(1)}, bf16[4,96,768]{2,1,0:T(8,128)(2,1)S(1)}, u32[]{:S(2)}, u32[]{:S(2)}) collective-permute-start(bf16[4,96,768]{2,1,0:T(8,128)(2,1)S(1)} %column.5.refs_0_), channel_id=1, source_target_pairs={{0,16},{1,9},{2,18},{3,11},{4,20},{5,13},{6,22},{7,15},{8,24},{9,1... | collective-permute-start | bytes 1769480 | tf_op jit(solution)/shard_map/ppermute | solution.py:73
  52.3 27.6 %collective-permute-start.14 = (bf16[4,96,768]{2,1,0:T(8,128)(2,1)S(1)}, bf16[4,96,768]{2,1,0:T(8,128)(2,1)S(1)}, u32[]{:S(2)}, u32[]{:S(2)}) collective-permute-start(bf16[4,96,768]{2,1,0:T(8,128)(2,1)S(1)} %column.5.refs_0_), channel_id=1, source_target_pairs={{0,8},{1,17},{2,10},{3,19},{4,12},{5,21},{6,14},{7,23},{8,0},{9,25... | collective-permute-start | bytes 1769480 | tf_op jit(solution)/shard_map/ppermute | solution.py:73
  52.9 14.9 %collective-permute-start.12 = (bf16[24,3072]{1,0:T(8,128)(2,1)S(1)}, bf16[24,3072]{1,0:T(8,128)(2,1)S(1)}, u32[]{:S(2)}, u32[]{:S(2)}) collective-permute-start(bf16[24,3072]{1,0:T(8,128)(2,1)S(1)} %copy-done.19), channel_id=1, source_target_pairs={{0,6},{1,7},{2,0},{3,1},{4,2},{5,3},{6,4},{7,5},{8,14},{9,15},{10,... | collective-permute-start | bytes 442376 | tf_op jit(solution)/shard_map/ppermute | solution.py:73
  52.9 15.8 %collective-permute-start.11 = (bf16[24,3072]{1,0:T(8,128)(2,1)S(1)}, bf16[24,3072]{1,0:T(8,128)(2,1)S(1)}, u32[]{:S(2)}, u32[]{:S(2)}) collective-permute-start(bf16[24,3072]{1,0:T(8,128)(2,1)S(1)} %copy-done.19), channel_id=1, source_target_pairs={{0,4},{1,5},{2,6},{3,7},{4,0},{5,1},{6,2},{7,3},{8,12},{9,13},{10,... | collective-permute-start | bytes 442376 | tf_op jit(solution)/shard_map/ppermute | solution.py:73
  90.0 18.2 %collective-permute-start.21 = (bf16[4,24,3072]{2,1,0:T(8,128)(2,1)S(1)}, bf16[4,24,3072]{2,1,0:T(8,128)(2,1)S(1)}, u32[]{:S(2)}, u32[]{:S(2)}) collective-permute-start(bf16[4,24,3072]{2,1,0:T(8,128)(2,1)S(1)} %column.6.refs_0_), channel_id=1, source_target_pairs={{0,8},{1,17},{2,10},{3,19},{4,12},{5,21},{6,14},{7,23},{8,0},{9,25... | collective-permute-start | bytes 1769480 | tf_op jit(solution)/shard_map/ppermute | solution.py:73
  109.4 16.0 %collective-permute-start.24 = (bf16[4,96,768]{2,1,0:T(8,128)(2,1)S(1)}, bf16[4,96,768]{2,1,0:T(8,128)(2,1)S(1)}, u32[]{:S(2)}, u32[]{:S(2)}) collective-permute-start(bf16[4,96,768]{2,1,0:T(8,128)(2,1)S(1)} %column.7.refs_0_), channel_id=1, source_target_pairs={{0,16},{1,9},{2,18},{3,11},{4,20},{5,13},{6,22},{7,15},{8,24},{9,1... | collective-permute-start | bytes 1769480 | tf_op jit(solution)/shard_map/ppermute | solution.py:73
  110.2 15.3 %collective-permute-start.25 = (bf16[4,96,768]{2,1,0:T(8,128)(2,1)S(1)}, bf16[4,96,768]{2,1,0:T(8,128)(2,1)S(1)}, u32[]{:S(2)}, u32[]{:S(2)}) collective-permute-start(bf16[4,96,768]{2,1,0:T(8,128)(2,1)S(1)} %column.7.refs_0_), channel_id=1, source_target_pairs={{0,8},{1,17},{2,10},{3,19},{4,12},{5,21},{6,14},{7,23},{8,0},{9,25... | collective-permute-start | bytes 1769480 | tf_op jit(solution)/shard_map/ppermute | solution.py:73
  153.4 16.3 %collective-permute-start.32 = (bf16[2,4,96,768]{3,2,1,0:T(8,128)(2,1)S(1)}, bf16[2,4,96,768]{3,2,1,0:T(8,128)(2,1)S(1)}, u32[]{:S(2)}, u32[]{:S(2)}) collective-permute-start(bf16[2,4,96,768]{3,2,1,0:T(8,128)(2,1)S(1)} %leave.8), channel_id=1, source_target_pairs={{0,16},{1,9},{2,18},{3,11},{4,20},{5,13},{6,22},{7,15},{8,24},{9,1... | collective-permute-start | bytes 3538952 | tf_op jit(solution)/shard_map/ppermute | solution.py:73
  171.6 17.4 %collective-permute-start.34 = (bf16[1,4,96,768]{3,2,1,0:T(8,128)(2,1)S(1)}, bf16[1,4,96,768]{3,2,1,0:T(8,128)(2,1)S(1)}, u32[]{:S(2)}, u32[]{:S(2)}) collective-permute-start(bf16[1,4,96,768]{3,2,1,0:T(8,128)(2,1)S(1)} %leave.9), channel_id=1, source_target_pairs={{0,8},{1,17},{2,10},{3,19},{4,12},{5,21},{6,14},{7,23},{8,0},{9,25... | collective-permute-start | bytes 1769480 | tf_op jit(solution)/shard_map/ppermute | solution.py:73
  178.4 27.3 %collective-permute-start.36 = (bf16[2,4,24,3072]{3,2,1,0:T(8,128)(2,1)}, bf16[2,4,24,3072]{3,2,1,0:T(8,128)(2,1)}, u32[]{:S(2)}, u32[]{:S(2)}) collective-permute-start(bf16[2,4,24,3072]{3,2,1,0:T(8,128)(2,1)} %leave.10), channel_id=1, source_target_pairs={{0,16},{1,9},{2,18},{3,11},{4,20},{5,13},{6,22},{7,15},{8,24},{9,1... | collective-permute-start | bytes 3538952 | tf_op jit(solution)/shard_map/ppermute | solution.py:73
  190.9 20.0 %collective-permute-start.37 = (bf16[96,768]{1,0:T(8,128)(2,1)S(1)}, bf16[96,768]{1,0:T(8,128)(2,1)S(1)}, u32[]{:S(2)}, u32[]{:S(2)}) collective-permute-start(bf16[96,768]{1,0:T(8,128)(2,1)S(1)} %get-tuple-element.279), channel_id=1, source_target_pairs={{0,2},{1,3},{2,4},{3,5},{4,6},{5,7},{6,0},{7,1},{8,10},{9,11},{10,... | collective-permute-start | bytes 442376 | tf_op jit(solution)/shard_map/ppermute | solution.py:73
  191.2 19.7 %collective-permute-start.38 = (bf16[96,768]{1,0:T(8,128)(2,1)S(1)}, bf16[96,768]{1,0:T(8,128)(2,1)S(1)}, u32[]{:S(2)}, u32[]{:S(2)}) collective-permute-start(bf16[96,768]{1,0:T(8,128)(2,1)S(1)} %get-tuple-element.280), channel_id=1, source_target_pairs={{0,4},{1,5},{2,6},{3,7},{4,0},{5,1},{6,2},{7,3},{8,12},{9,13},{10,... | collective-permute-start | bytes 442376 | tf_op jit(solution)/shard_map/ppermute | solution.py:73
  193.1 17.8 %collective-permute-start.39 = (bf16[96,768]{1,0:T(8,128)(2,1)S(1)}, bf16[96,768]{1,0:T(8,128)(2,1)S(1)}, u32[]{:S(2)}, u32[]{:S(2)}) collective-permute-start(bf16[96,768]{1,0:T(8,128)(2,1)S(1)} %get-tuple-element.281), channel_id=1, source_target_pairs={{0,6},{1,7},{2,0},{3,1},{4,2},{5,3},{6,4},{7,5},{8,14},{9,15},{10,... | collective-permute-start | bytes 442376 | tf_op jit(solution)/shard_map/ppermute | solution.py:73
  207.5 16.1 %collective-permute-start.42 = (bf16[1,4,24,3072]{3,2,1,0:T(8,128)(2,1)S(1)}, bf16[1,4,24,3072]{3,2,1,0:T(8,128)(2,1)S(1)}, u32[]{:S(2)}, u32[]{:S(2)}) collective-permute-start(bf16[1,4,24,3072]{3,2,1,0:T(8,128)(2,1)S(1)} %leave.11), channel_id=1, source_target_pairs={{0,8},{1,17},{2,10},{3,19},{4,12},{5,21},{6,14},{7,23},{8,0},{9,25... | collective-permute-start | bytes 1769480 | tf_op jit(solution)/shard_map/ppermute | solution.py:73
  210.0 22.0 %collective-permute-start.41 = (bf16[2,4,120,768]{3,2,1,0:T(8,128)(2,1)S(1)}, bf16[2,4,120,768]{3,2,1,0:T(8,128)(2,1)S(1)}, u32[]{:S(2)}, u32[]{:S(2)}) collective-permute-start(bf16[2,4,120,768]{3,2,1,0:T(8,128)(2,1)S(1)} %leave.12), channel_id=1, source_target_pairs={{0,16},{1,9},{2,18},{3,11},{4,20},{5,13},{6,22},{7,15},{8,24},{9,1... | collective-permute-start | bytes 4423688 | tf_op jit(solution)/shard_map/ppermute | solution.py:73
  212.7 20.1 %collective-permute-start.40 = (bf16[4,4,80,768]{3,2,1,0:T(8,128)(2,1)S(1)}, bf16[4,4,80,768]{3,2,1,0:T(8,128)(2,1)S(1)}, u32[]{:S(2)}, u32[]{:S(2)}) collective-permute-start(bf16[4,4,80,768]{3,2,1,0:T(8,128)(2,1)S(1)} %exchange.7), channel_id=1, source_target_pairs={{0,1},{1,0},{2,3},{3,2},{4,5},{5,4},{6,7},{7,6},{8,9},{9,8},{10,11... | collective-permute-start | bytes 5898248 | tf_op jit(solution)/shard_map/ppermute | solution.py:73
  233.9 22.1 %collective-permute-start.43 = (bf16[2,4,80,768]{3,2,1,0:T(8,128)(2,1)S(1)}, bf16[2,4,80,768]{3,2,1,0:T(8,128)(2,1)S(1)}, u32[]{:S(2)}, u32[]{:S(2)}) collective-permute-start(bf16[2,4,80,768]{3,2,1,0:T(8,128)(2,1)S(1)} %leave.14), channel_id=1, source_target_pairs={{0,16},{1,9},{2,18},{3,11},{4,20},{5,13},{6,22},{7,15},{8,24},{9,1... | collective-permute-start | bytes 2949128 | tf_op jit(solution)/shard_map/ppermute | solution.py:73
  234.4 19.4 %collective-permute-start.44 = (bf16[1,4,120,768]{3,2,1,0:T(8,128)(2,1)S(1)}, bf16[1,4,120,768]{3,2,1,0:T(8,128)(2,1)S(1)}, u32[]{:S(2)}, u32[]{:S(2)}) collective-permute-start(bf16[1,4,120,768]{3,2,1,0:T(8,128)(2,1)S(1)} %leave.13), channel_id=1, source_target_pairs={{0,8},{1,17},{2,10},{3,19},{4,12},{5,21},{6,14},{7,23},{8,0},{9,25... | collective-permute-start | bytes 2211848 | tf_op jit(solution)/shard_map/ppermute | solution.py:73
  257.8 19.1 %collective-permute-start.53 = (bf16[120,768]{1,0:T(8,128)(2,1)S(1)}, bf16[120,768]{1,0:T(8,128)(2,1)S(1)}, u32[]{:S(2)}, u32[]{:S(2)}) collective-permute-start(bf16[120,768]{1,0:T(8,128)(2,1)S(1)} %get-tuple-element.325), channel_id=1, source_target_pairs={{0,4},{1,5},{2,6},{3,7},{4,0},{5,1},{6,2},{7,3},{8,12},{9,13},{10,... | collective-permute-start | bytes 552968 | tf_op jit(solution)/shard_map/ppermute | solution.py:73
  259.0 17.9 %collective-permute-start.54 = (bf16[120,768]{1,0:T(8,128)(2,1)S(1)}, bf16[120,768]{1,0:T(8,128)(2,1)S(1)}, u32[]{:S(2)}, u32[]{:S(2)}) collective-permute-start(bf16[120,768]{1,0:T(8,128)(2,1)S(1)} %get-tuple-element.326), channel_id=1, source_target_pairs={{0,6},{1,7},{2,0},{3,1},{4,2},{5,3},{6,4},{7,5},{8,14},{9,15},{10,... | collective-permute-start | bytes 552968 | tf_op jit(solution)/shard_map/ppermute | solution.py:73
  266.4 18.8 %collective-permute-start.50 = (bf16[80,768]{1,0:T(8,128)(2,1)S(1)}, bf16[80,768]{1,0:T(8,128)(2,1)S(1)}, u32[]{:S(2)}, u32[]{:S(2)}) collective-permute-start(bf16[80,768]{1,0:T(8,128)(2,1)S(1)} %get-tuple-element.318), channel_id=1, source_target_pairs={{0,4},{1,5},{2,6},{3,7},{4,0},{5,1},{6,2},{7,3},{8,12},{9,13},{10,... | collective-permute-start | bytes 368648 | tf_op jit(solution)/shard_map/ppermute | solution.py:73
  267.3 18.0 %collective-permute-start.51 = (bf16[80,768]{1,0:T(8,128)(2,1)S(1)}, bf16[80,768]{1,0:T(8,128)(2,1)S(1)}, u32[]{:S(2)}, u32[]{:S(2)}) collective-permute-start(bf16[80,768]{1,0:T(8,128)(2,1)S(1)} %get-tuple-element.319), channel_id=1, source_target_pairs={{0,6},{1,7},{2,0},{3,1},{4,2},{5,3},{6,4},{7,5},{8,14},{9,15},{10,... | collective-permute-start | bytes 368648 | tf_op jit(solution)/shard_map/ppermute | solution.py:73
  (97 other events, 695.9 us)

commit v2 on v1

--- a/solution.py
+++ b/solution.py
@@ -268,6 +268,7 @@
             jax.ShapeDtypeStruct(shape, BF),
             "exchange",
         )(place.spots, *blocks)
+        self.sent = sent
         self.other = place.across_cores(sent)
         self.got = []
 
@@ -320,6 +321,9 @@
         )(place.spots, *self.blocks, self.other, *self.got)
         self.got.append(place.across_step(sent, step))
         return sent
+
+    def latest(self):
+        return self.got[-1]
 
     def last(self, *earlier):
         place = self.place
@@ -364,6 +368,82 @@
         return cut_sum([self.own] + self.came, parts)
 
 
+def line_kernel(n, each, chips, spots_ref, *refs):
+    outs = refs[2 * chips * each :]
+    for k in range(chips):
+        for i in range(2):
+            at = (2 * k + i) * each
+            value = sum_refs(refs[at : at + each], n)
+            outs[k][i] = value.astype(outs[k].dtype).reshape(outs[k].shape[1:])
+
+
+def turn_kernel(own_ref, *refs):
+    *came, keep_ref, send_ref = refs
+    total = own_ref[...]
+    for c in came:
+        total = total + c[...].astype(F32)
+    keep_ref[...] = total[0]
+    send_ref[...] = total[1].astype(BF)
+
+
+class ReduceHopLast(Reduce):
+    def line(self, *earlier):
+        place = self.place
+        self.got[-1] = after(self.got[-1], *earlier)
+        chips, core = place.chips, place.core_at
+        specs, ins = [], []
+        for k in range(chips):
+            up = place.up_at + k
+            for i in range(2):
+                for b in self.blocks:
+                    ins.append(b)
+                    specs.append(
+                        pl.BlockSpec(
+                            (1, 1, 1) + b.shape[3:],
+                            lambda _, s, up=up, i=i: (s[2 * i], s[up], s[core], 0, 0),
+                        )
+                    )
+                ins.append(self.other)
+                specs.append(
+                    pl.BlockSpec(
+                        (1, 1, self.rows, self.cols),
+                        lambda _, s, up=up, i=i: (s[2 * i], s[up], 0, 0),
+                    )
+                )
+                ins.append(self.got[0])
+                specs.append(
+                    pl.BlockSpec(
+                        (1, 1, self.rows, self.cols),
+                        lambda _, s, up=up, i=i: (i, s[up], 0, 0),
+                    )
+                )
+        shape = (2, self.rows, self.cols)
+        own, *sent = self.call(
+            functools.partial(line_kernel, len(self.blocks), len(ins) // chips // 2, chips),
+            (1,),
+            specs,
+            [pl.BlockSpec(shape, lambda _, s: (0, 0, 0))] * chips,
+            [jax.ShapeDtypeStruct(shape, F32 if k == 0 else BF) for k in range(chips)],
+            "line",
+        )(place.spots, *ins)
+        self.own = own
+        self.came = [place.along_chips(v, k + 1) for k, v in enumerate(sent)]
+        return own
+
+    def turn(self, *earlier):
+        came = after(self.came, *earlier)
+        shape = (self.rows, self.cols)
+        self.own, sent = pl.pallas_call(
+            turn_kernel,
+            out_shape=[jax.ShapeDtypeStruct(shape, F32), jax.ShapeDtypeStruct(shape, BF)],
+            compiler_params=pltpu.CompilerParams(vmem_limit_bytes=8 << 20),
+            cost_estimate=QUICK,
+            name="turn",
+        )(self.own, *came)
+        self.came = [self.place.across_step(sent, 1)]
+        return sent
+
+
 def owner_blocks(place, gradient):
     rows = gradient.shape[0] // (place.dp_count * place.inner)
     return gradient.reshape(
@@ -378,11 +458,21 @@
         self.sum = lax.psum_scatter(
             jnp.concatenate(flat, axis=1), AXES, scatter_dimension=0, tiled=False
         )
+        self.sent = self.sum
 
     def leave(self, step, *earlier):
         return self.sum
 
     def last(self, *earlier):
+        return self.sum
+
+    def latest(self):
+        return self.sum
+
+    def line(self, *earlier):
+        return self.sum
+
+    def turn(self, *earlier):
         return self.sum
 
     def result(self, parts, *earlier):
@@ -918,8 +1008,9 @@
     shape = layer_input.shape
     rows = self_output.shape[0]
     wide = expand_bias.shape[0]
-    fits = rows % 8 == 0
+    fits = rows % 8 == 0 and place.bits == 2
     reduce = Reduce if fits else PlainReduce
+    reduce_hop_last = ReduceHopLast if fits else PlainReduce
     x = layer_input.reshape(-1, D)
     memory = encoder_states.reshape(-1, D)
     grad_out = output_grad.reshape(-1, D).astype(F32)
@@ -943,13 +1034,20 @@
         g_self.hop(0, 0)
         g_self.hop(1, 0)
         g_cross = Gather(place, after(local_cross, line))
-        g_self.meet(g_cross)
+        g_self.blocks, g_cross.got = lax.optimization_barrier((g_self.blocks, g_cross.got))
         g_self.hop(1, 1)
         line = g_cross.column()
         g_cross.hop(0, 0)
         g_cross.hop(1, 0)
-        g_self.blocks[3] = after(g_self.blocks[3], line)
-        g_expand = Gather(place, after(expand_weight, g_self.blocks[3]))
+        g_expand = Gather(place, after(expand_weight, line))
+        g_self.blocks, g_cross.blocks, g_expand.got = lax.optimization_barrier(
+            (g_self.blocks, g_cross.blocks, g_expand.got)
+        )
+        g_cross.hop(1, 1)
+        line = g_expand.column()
+        g_expand.hop(0, 0)
+        g_expand.hop(1, 0)
+        g_contract = Gather(place, after(contract_weight, line))
         g_self.half(line)
         *w_self, smalls = g_self.spread(four + [(4 * rows, 8)])
         smalls = smalls.reshape(-1, 8, D)
@@ -990,69 +1088,65 @@
     v = (dot_nn(x, wv) + biases[1]).astype(BF)
     o, p = attend(q, k, v, span_start, span_length, True, count)
     if fits:
-        g_cross.hop(1, 1, o)
-        line = g_expand.column(o)
-        g_expand.hop(0, 0)
-        g_expand.hop(1, 0)
-        g_cross.blocks[3] = after(g_cross.blocks[3], line)
-        g_contract = Gather(place, after(contract_weight, g_cross.blocks[3]))
-        o = after(o, line)
+        g_cross.blocks, g_expand.blocks, g_contract.got, o = lax.optimization_barrier(
+            (g_cross.blocks, g_expand.blocks, g_contract.got, o)
+        )
+        g_expand.hop(1, 1)
+        line = g_contract.column()
+        g_contract.hop(0, 0)
+        g_contract.hop(1, 0)
+        g_cross.half(line)
+        w_cross = g_cross.spread(four)
     r1 = x.astype(F32) + (dot_nn(o, wo) + biases[2])
     n1, s1 = norm(r1)
     x1 = n1 * gains[0] + shifts[0]
     x1b = x1.astype(BF)
-    if fits:
-        g_cross.half(x1b)
-        w_cross = g_cross.spread(four)
     cq, ck, cv, co = w_cross
     q2 = ((dot_nn(x1b, cq) + biases[3]) * 0.125).astype(BF)
     k2 = dot_nn(memory, ck).astype(BF)
     v2 = (dot_nn(memory, cv) + biases[4]).astype(BF)
     o2, p2 = attend(q2, k2, v2, span_start, span_length, False, count)
     if fits:
-        g_expand.hop(1, 1, o2)
-        line = g_contract.column(o2)
-        g_contract.hop(0, 0)
-        g_contract.hop(1, 0)
-        g_expand.blocks[3] = after(g_expand.blocks[3], line)
-        o2 = after(o2, line)
+        g_expand.blocks, g_contract.blocks, o2 = lax.optimization_barrier(
+            (g_expand.blocks, g_contract.blocks, o2)
+        )
+        g_contract.hop(1, 1)
+        g_expand.half()
+        (expand,) = g_expand.spread([(0, rows)])
     r2 = x1 + (dot_nn(o2, co) + biases[5])
     n2, s2 = norm(r2)
     x2 = n2 * gains[1] + shifts[1]
     x2b = x2.astype(BF)
-    if fits:
-        g_expand.half(x2b)
-        (expand,) = g_expand.spread([(0, rows)])
     act, slope = gelu_and_slope(dot_nn(x2b, expand) + expand_b)
     act = act.astype(BF)
     slope = slope.astype(BF)
     if fits:
-        g_contract.hop(1, 1, act)
-        (contract,) = g_contract.spread([(0, 4 * rows)], act)
+        g_contract.blocks[3] = after(g_contract.blocks[3], act)
+        (contract,) = g_contract.spread([(0, 4 * rows)])
     n3, s3 = norm(x2 + (dot_nn(act, contract) + contract_b))
     output = (n3 * gains[2] + shifts[2]).astype(BF)
 
     dr3, gain3, shift3 = norm_back(n3, s3, gains[2], grad_out)
     df = dr3.astype(BF)
     d_contract = dot_tn(act, df).astype(BF)
-    r_contract = reduce(place, [owner_blocks(place, d_contract)])
+    r_contract = reduce_hop_last(place, [owner_blocks(place, d_contract)])
     d_contract_b = column_sum(df)
     du, d_expand_b = hidden_back(after(df, d_contract), contract, slope)
     sent = r_contract.leave(0, du)
     d_expand, dr2, dc, ff_sums = expand_back(
         x2b, after(du, sent), expand, dr3, r2, gains[1]
     )
-    sent = r_contract.leave(1, dc)
-    r_expand = reduce(place, [owner_blocks(place, after(d_expand, sent))])
+    sent = r_contract.line(dc)
+    r_expand = reduce_hop_last(place, [owner_blocks(place, after(d_expand, sent))])
     sent = r_expand.leave(0, dc)
     *d_cross, dk2, dv2, dr1, da, cross_sums = cross_back(
         after(dc, sent), co, cq, q2, k2, v2, p2, o2, x1b, memory, dr2, r1, gains[0], o, count
     )
     r_cross = reduce(place, [owner_blocks(place, d) for d in d_cross])
-    sent = r_contract.last(da)
+    sent = r_expand.line(da)
+    sent = r_contract.turn(sent)
     *d_self, dq, dk, dv, self_sums = self_back(after(da, sent), wo, q, k, v, p, x, count)
-    sent = r_expand.leave(1, self_sums)
-    sent2 = r_cross.leave(0, sent)
+    sent = r_cross.leave(0, self_sums)
     small_blocks = split_small(
         ff_sums,
         cross_sums,
@@ -1063,22 +1157,22 @@
         wide,
     )
     small_blocks = small_blocks.reshape(place.dp_count, place.chips, 2, 8, D)
-    (own_contract,) = r_contract.result([((4 * rows, D), 0, 0)], self_sums, sent2)
     r_self = reduce(
         place,
-        [owner_blocks(place, d) for d in after(d_self, sent2)] + [small_blocks],
-    )
-    dq, dk, dv, dk2, dv2 = after((dq, dk, dv, dk2, dv2), sent2, own_contract)
+        [owner_blocks(place, d) for d in after(d_self, sent)] + [small_blocks],
+    )
+    sent = r_expand.turn(r_self.sent)
+    (own_contract,) = r_contract.result([((4 * rows, D), 0, 0)], sent)
+    dq, dk, dv, dk2, dv2 = after((dq, dk, dv, dk2, dv2), own_contract)
     input_grad, encoder_grad = inputs_back(
         dq, dk, dv, wq, wk, wv, dr1, dk2, dv2, ck, cv
     )
-    sent = r_expand.last(input_grad)
-    sent2 = r_cross.leave(1, sent)
-    sent3 = r_self.leave(0, sent2)
-    (own_expand,) = r_expand.result([((rows, FF), 0, 0)], sent3)
-    sent = r_cross.last(own_expand)
+    r_cross.leave(1, input_grad)
+    sent = r_self.leave(0, r_cross.latest())
+    sent = r_cross.last(sent)
     sent = r_self.leave(1, sent)
-    sent = r_self.last(sent)
+    (own_expand,) = r_expand.result([((rows, FF), 0, 0)], sent)
+    sent = r_self.last(own_expand)
     projects = ((3, rows, D), 0, 0)
     square = (rows, D)
     own_cross = r_cross.result(

time: 292 us -> 285 us (0.976)
  starting transfers between devices: 53.2 us -> 61 us
  waiting for transfers between devices: 126 us -> 119 us
  Pallas kernels: 74.9 us -> 71.1 us
    ppermute x55, starting transfers between devices: 53.2 us -> 61 us  [permute(): return lax.ppermute(value, AXES, pairs)]
    ppermute x55, waiting for transfers between devices: 126 us -> 119 us  [permute(): return lax.ppermute(value, AXES, pairs)]
    pallas_call x8 -> x6, Pallas kernels: 9.65 us -> 6.3 us  [leave(): self.call(functools.partial(leave_kernel, len(self.blocks)), (count,), sp...]
    unnamed x133 -> x111, local copies, waits for them, and re-layouts: 7.13 us -> 5.9 us
  transfers between devices with their start and end apart: 55 -> 55, of which waited for: 30 -> 31; matrix products, arithmetic and copies ran while one was open for 5% -> 5% of each run, Pallas kernels for 22% -> 19%
where the time goes in v2:
time: 285 us; the launch traced here: 281 us
  waiting for transfers between devices  119 us (42%)
  Pallas kernels  71.1 us (25%)
  starting transfers between devices  61 us (21%)
  matrix products  17.4 us (6%)
  local copies, waits for them, and re-layouts  6.71 us (2%)
  other arithmetic  4.31 us (2%)
    ppermute x55, waiting for transfers between devices, permute(): return lax.ppermute(value, AXES, pairs)  119 us
    ppermute x55, starting transfers between devices, permute(): return lax.ppermute(value, AXES, pairs)  61 us
    dot_general x10, matrix products, dot_nn(): return jnp.dot(a, b, preferred_element_type=F32)  14.5 us
    pallas_call x11, Pallas kernels, copy_call(): pl.pallas_call(functools.partial(copy_kernel, plan, len(ins)), grid_spec=...  13.1 us
    pallas_call x1, Pallas kernels, cross_back(): pl.pallas_call(functools.partial(cross_back_kernel, count), out_shape=[sq...  8.72 us
    pallas_call x1, Pallas kernels, expand_back(): pl.pallas_call(expand_back_kernel, grid=(FF // D,), in_specs=[still, movi...  8 us
    pallas_call x2, Pallas kernels, attend(): pl.pallas_call(functools.partial(attend_kernel, masked), grid_spec=pltpu....  7.59 us
    pallas_call x6, Pallas kernels, leave(): self.call(functools.partial(leave_kernel, len(self.blocks)), (count,), sp...  6.3 us
  transfers between devices with their start and end apart: 55, of which 31 were waited for; matrix products, arithmetic and copies ran while one was open for 5% of the time, Pallas kernels for 19%

profile of v2, /device:TPU:0, one launch (start us, length us, event | category | flops | bytes accessed | tf_op | source)
XLA Modules:
  0.0 281.4 jit_solution(16386140307836061351)
XLA Ops:
  1.7 5.1 %collective-permute-start.2 = (bf16[104,768]{1,0:T(8,128)(2,1)S(1)}, bf16[104,768]{1,0:T(8,128)(2,1)S(1)}, u32[]{:S(2)}, u32[]{:S(2)}) collective-permute-start(bf16[104,768]{1,0:T(8,128)(2,1)S(1)} %pack_self.1.refs_0_), channel_id=1, source_target_pairs={{0,6},{1,7},{2,0},{3,1},{4,2},{5,3},{6,4},{7,5},{8,14},{9,15},{10,... | collective-permute-start | bytes 479240 | tf_op jit(solution)/shard_map/ppermute | solution.py:73
  11.4 9.0 %collective-permute-done.1.refs_2_ = bf16[104,768]{1,0:T(8,128)(2,1)S(1)} collective-permute-done((bf16[104,768]{1,0:T(8,128)(2,1)S(1)}, bf16[104,768]{1,0:T(8,128)(2,1)S(1)}, u32[]{:S(2)}, u32[]{:S(2)}) %collective-permute-start.1) | collective-permute-done | bytes 159776 | tf_op jit(solution)/shard_map/ppermute | solution.py:73
  30.9 8.9 %collective-permute-done.6.refs_2_ = bf16[96,768]{1,0:T(8,128)(2,1)S(1)} collective-permute-done((bf16[96,768]{1,0:T(8,128)(2,1)S(1)}, bf16[96,768]{1,0:T(8,128)(2,1)S(1)}, u32[]{:S(2)}, u32[]{:S(2)}) %collective-permute-start.6) | collective-permute-done | bytes 147488 | tf_op jit(solution)/shard_map/ppermute | solution.py:73
  45.3 4.2 %collective-permute-done.13.refs_3_ = bf16[24,3072]{1,0:T(8,128)(2,1)S(1)} collective-permute-done((bf16[24,3072]{1,0:T(8,128)(2,1)S(1)}, bf16[24,3072]{1,0:T(8,128)(2,1)S(1)}, u32[]{:S(2)}, u32[]{:S(2)}) %collective-permute-start.13) | collective-permute-done | bytes 147488 | tf_op jit(solution)/shard_map/ppermute | solution.py:73
  51.4 7.3 %collective-permute-done.12.refs_2_ = bf16[24,3072]{1,0:T(8,128)(2,1)S(1)} collective-permute-done((bf16[24,3072]{1,0:T(8,128)(2,1)S(1)}, bf16[24,3072]{1,0:T(8,128)(2,1)S(1)}, u32[]{:S(2)}, u32[]{:S(2)}) %collective-permute-start.12) | collective-permute-done | bytes 147488 | tf_op jit(solution)/shard_map/ppermute | solution.py:73
  58.7 4.3 %collective-permute-done.10.refs_2_ = bf16[4,96,768]{2,1,0:T(8,128)(2,1)S(1)} collective-permute-done((bf16[4,96,768]{2,1,0:T(8,128)(2,1)S(1)}, bf16[4,96,768]{2,1,0:T(8,128)(2,1)S(1)}, u32[]{:S(2)}, u32[]{:S(2)}) %collective-permute-start.10) | collective-permute-done | bytes 589856 | tf_op jit(solution)/shard_map/ppermute | solution.py:73
  76.2 3.9 %attend.2 = (bf16[512,768]{1,0:T(8,128)(2,1)S(1)}, bf16[2,12,256,256]{3,2,1,0:T(8,128)(2,1)S(1)}) custom-call(s32[2]{0:T(128)S(1)} %copy-done.18, s32[2]{0:T(128)S(1)} %copy-done.19, bf16[512,768]{1,0:T(8,128)(2,1)S(1)} %fusion.12.q_ref, bf16[512,768]{1,0:T(8,128)(2,1)S(1)} %fusion.15.k_ref, bf16[512,768]{1,0:T(8,128)(2,1)S(1)} %fusion.13.v_ref), custom_call_target="tpu_custom_call" | custom-call | flops 1000 | bytes 1000 | tf_op jit(solution)/shard_map/attend/pallas_call | solution.py:534
  83.3 5.7 %collective-permute-done.14.refs_3_ = bf16[4,96,768]{2,1,0:T(8,128)(2,1)S(1)} collective-permute-done((bf16[4,96,768]{2,1,0:T(8,128)(2,1)S(1)}, bf16[4,96,768]{2,1,0:T(8,128)(2,1)S(1)}, u32[]{:S(2)}, u32[]{:S(2)}) %collective-permute-start.14) | collective-permute-done | bytes 589856 | tf_op jit(solution)/shard_map/ppermute | solution.py:73
  100.9 3.7 %attend.3 = (bf16[512,768]{1,0:T(8,128)(2,1)S(1)}, bf16[2,12,256,256]{3,2,1,0:T(8,128)(2,1)S(1)}) custom-call(s32[2]{0:T(128)S(1)} %copy-done.18, s32[2]{0:T(128)S(1)} %copy-done.19, bf16[512,768]{1,0:T(8,128)(2,1)S(1)} %multiply_convert_fusion.1.q_ref, bf16[512,768]{1,0:T(8,128)(2,1)S(1)} %fusion.16.k_ref, bf16[512,768]{1,0:T(8,128)(2,1)S(1)} %fusion.14.v_ref), custom_call_target="tpu_custom_call" | custom-call | flops 1000 | bytes 1000 | tf_op jit(solution)/shard_map/attend/pallas_call | solution.py:534
  108.4 5.5 %collective-permute-done.21.refs_3_ = bf16[4,24,3072]{2,1,0:T(8,128)(2,1)S(1)} collective-permute-done((bf16[4,24,3072]{2,1,0:T(8,128)(2,1)S(1)}, bf16[4,24,3072]{2,1,0:T(8,128)(2,1)S(1)}, u32[]{:S(2)}, u32[]{:S(2)}) %collective-permute-start.21) | collective-permute-done | bytes 589856 | tf_op jit(solution)/shard_map/ppermute | solution.py:73
  120.8 5.1 %fusion.4 = (bf16[512,3072]{1,0:T(8,128)(2,1)S(1)}, bf16[512,3072]{1,0:T(8,128)(2,1)S(1)}) fusion(f32[3072]{0:T(1024)S(1)} %bitcast.198, bf16[512,768]{1,0:T(8,128)(2,1)S(1)} %fusion.18.x_ref, bf16[768,3072]{1,0:T(8,128)(2,1)S(1)} %bitcast.169), kind=kOutput, calls=%fused_computation.5 | convolution fusion | flops 2434793472 | bytes 11808768 | tf_op jit(solution)/shard_map/dot_general | solution.py:491
  139.1 3.9 %hidden_back.1 = (bf16[512,3072]{1,0:T(8,128)(2,1)S(1)}, f32[1,3072]{1,0:T(1,128)S(1)}) custom-call(bf16[512,768]{1,0:T(8,128)(2,1)S(1)} %get-tuple-element.301.df_ref, bf16[3072,768]{1,0:T(8,128)(2,1)S(1)} %bitcast.172, bf16[512,3072]{1,0:T(8,128)(2,1)S(1)} %get-tuple-element.414.slope_ref), custom_call_target="tpu_custom_call" | custom-call | flops 99999997952 | bytes 1000000 | tf_op jit(solution)/shard_map/hidden_back/pallas_call | solution.py:590
  144.9 8.0 %expand_back.1 = (bf16[768,3072]{1,0:T(8,128)(2,1)S(1)}, f32[512,768]{1,0:T(8,128)S(1)}, bf16[512,768]{1,0:T(8,128)(2,1)S(1)}, f32[8,768]{1,0:T(8,128)S(1)}) custom-call(bf16[512,768]{1,0:T(8,128)(2,1)S(1)} %fusion.18.x_ref, bf16[512,3072]{1,0:T(8,128)(2,1)S(1)} %get-tuple-element.304.du_ref, bf16[768,3072]{1,0:T(8,128)(2,1)S(1)} %bitcast.170, ...), custom_call_target="tpu_custom_call" | custom-call | flops 99999997952 | bytes 1000000 | tf_op jit(solution)/shard_map/expand_back/pallas_call | solution.py:639
  152.9 7.7 %collective-permute-done.32.refs_2_.refs_5_.refs_8_.refs_11_.refs_14_.refs_17_.refs_20_.refs_23_ = bf16[2,4,96,768]{3,2,1,0:T(8,128)(2,1)S(1)} collective-permute-done((bf16[2,4,96,768]{3,2,1,0:T(8,128)(2,1)S(1)}, bf16[2,4,96,768]{3,2,1,0:T(8,128)(2,1)S(1)}, u32[]{:S(2)}, u32[]{:S(2)}) %collective-permute-start.32) | collective-permute-done | bytes 1179680 | tf_op jit(solution)/shard_map/ppermute | solution.py:73
  171.1 8.7 %cross_back.1 = (bf16[768,768]{1,0:T(8,128)(2,1)S(1)}, bf16[768,768]{1,0:T(8,128)(2,1)S(1)}, bf16[768,768]{1,0:T(8,128)(2,1)S(1)}, bf16[768,768]{1,0:T(8,128)(2,...) custom-call(bf16[512,768]{1,0:T(8,128)(2,1)S(1)} %get-tuple-element., ...), custom_call_target="tpu_custom_call" | custom-call | flops 99999997952 | bytes 1000000 | tf_op jit(solution)/shard_map/cross_back/pallas_call | solution.py:744
  187.6 6.8 %collective-permute-start.39 = (bf16[2,24,3072]{2,1,0:T(8,128)(2,1)S(1)}, bf16[2,24,3072]{2,1,0:T(8,128)(2,1)S(1)}, u32[]{:S(2)}, u32[]{:S(2)}) collective-permute-start(bf16[2,24,3072]{2,1,0:T(8,128)(2,1)S(1)} %get-tuple-element.332), channel_id=1, source_target_pairs={{0,2},{1,3},{2,4},{3,5},{4,6},{5,7},{6,0},{7,1},{8,10},{9,11},{10,... | collective-permute-start | bytes 884744 | tf_op jit(solution)/shard_map/ppermute | solution.py:73
  197.0 6.3 %self_back.1 = (bf16[768,768]{1,0:T(8,128)(2,1)S(1)}, bf16[768,768]{1,0:T(8,128)(2,1)S(1)}, bf16[768,768]{1,0:T(8,128)(2,1)S(1)}, bf16[512,768]{1,0:T(8,128)(2,1...) custom-call(bf16[512,768]{1,0:T(8,128)(2,1)S(1)} %copy-done.51, ...), custom_call_target="tpu_custom_call" | custom-call | flops 99999997952 | bytes 1000000 | tf_op jit(solution)/shard_map/self_back/pallas_call | solution.py:801
  206.4 7.2 %collective-permute-done.40.refs_1_ = bf16[2,24,3072]{2,1,0:T(8,128)(2,1)S(1)} collective-permute-done((bf16[2,24,3072]{2,1,0:T(8,128)(2,1)S(1)}, bf16[2,24,3072]{2,1,0:T(8,128)(2,1)S(1)}, u32[]{:S(2)}, u32[]{:S(2)}) %collective-permute-start.40) | collective-permute-done | bytes 294944 | tf_op jit(solution)/shard_map/ppermute | solution.py:73
  214.5 4.8 %inputs_back.1 = (f32[512,768]{1,0:T(8,128)}, f32[512,768]{1,0:T(8,128)}) custom-call(bf16[512,768]{1,0:T(8,128)(2,1)S(1)} %get-tuple-element.356.dq_ref, bf16[512,768]{1,0:T(8,128)(2,1)S(1)} %get-tuple-element.357.dk_ref, bf16[512,768]{1,0:T(8,128)(2,1)S(1)} %get-tuple-element.358.dv_ref, bf16[768,768]{1,0:T(8,128)(2,1)S(1)} %bitcast.175, ...), custom_call_target="tpu_custom_call" | custom-call | flops 99999997952 | bytes 1000000 | tf_op jit(solution)/shard_map/inputs_back/pallas_call | solution.py:828
  219.3 4.7 %collective-permute-done.44.refs_6_.refs_14_.refs_22_.refs_30_ = bf16[2,4,120,768]{3,2,1,0:T(8,128)(2,1)S(1)} collective-permute-done((bf16[2,4,120,768]{3,2,1,0:T(8,128)(2,1)S(1)}, bf16[2,4,120,768]{3,2,1,0:T(8,128)(2,1)S(1)}, u32[]{:S(2)}, u32[]{:S(2)}) %collective-permute-start.44) | collective-permute-done | bytes 1474592 | tf_op jit(solution)/shard_map/ppermute | solution.py:73
  226.2 10.3 %collective-permute-done.45.refs_7_.refs_15_.refs_23_.refs_31_ = bf16[1,4,120,768]{3,2,1,0:T(8,128)(2,1)S(1)} collective-permute-done((bf16[1,4,120,768]{3,2,1,0:T(8,128)(2,1)S(1)}, bf16[1,4,120,768]{3,2,1,0:T(8,128)(2,1)S(1)}, u32[]{:S(2)}, u32[]{:S(2)}) %collective-permute-start.45) | collective-permute-done | bytes 737312 | tf_op jit(solution)/shard_map/ppermute | solution.py:73
  239.0 12.9 %collective-permute-done.46.refs_5_.refs_12_.refs_19_.refs_26_ = bf16[2,4,80,768]{3,2,1,0:T(8,128)(2,1)S(1)} collective-permute-done((bf16[2,4,80,768]{3,2,1,0:T(8,128)(2,1)S(1)}, bf16[2,4,80,768]{3,2,1,0:T(8,128)(2,1)S(1)}, u32[]{:S(2)}, u32[]{:S(2)}) %collective-permute-start.46) | collective-permute-done | bytes 983072 | tf_op jit(solution)/shard_map/ppermute | solution.py:73
  259.1 4.1 %collective-permute-done.48.refs_1_ = bf16[24,3072]{1,0:T(8,128)(2,1)S(1)} collective-permute-done((bf16[24,3072]{1,0:T(8,128)(2,1)S(1)}, bf16[24,3072]{1,0:T(8,128)(2,1)S(1)}, u32[]{:S(2)}, u32[]{:S(2)}) %collective-permute-start.48) | collective-permute-done | bytes 147488 | tf_op jit(solution)/shard_map/ppermute | solution.py:73
  273.3 7.2 %collective-permute-done.50.refs_2_ = bf16[80,768]{1,0:T(8,128)(2,1)S(1)} collective-permute-done((bf16[80,768]{1,0:T(8,128)(2,1)S(1)}, bf16[80,768]{1,0:T(8,128)(2,1)S(1)}, u32[]{:S(2)}, u32[]{:S(2)}) %collective-permute-start.50) | collective-permute-done | bytes 122912 | tf_op jit(solution)/shard_map/ppermute | solution.py:73
  (268 shorter events, 124.3 us)
Async XLA Ops:
  21.8 18.1 %collective-permute-start.4 = (bf16[4,104,768]{2,1,0:T(8,128)(2,1)S(1)}, bf16[4,104,768]{2,1,0:T(8,128)(2,1)S(1)}, u32[]{:S(2)}, u32[]{:S(2)}) collective-permute-start(bf16[4,104,768]{2,1,0:T(8,128)(2,1)S(1)} %column.4.refs_0_), channel_id=1, source_target_pairs={{0,8},{1,17},{2,10},{3,19},{4,12},{5,21},{6,14},{7,23},{8,0},{9,25... | collective-permute-start | bytes 1916936 | tf_op jit(solution)/shard_map/ppermute | solution.py:73
  23.3 16.6 %collective-permute-start.3 = (bf16[4,104,768]{2,1,0:T(8,128)(2,1)S(1)}, bf16[4,104,768]{2,1,0:T(8,128)(2,1)S(1)}, u32[]{:S(2)}, u32[]{:S(2)}) collective-permute-start(bf16[4,104,768]{2,1,0:T(8,128)(2,1)S(1)} %column.4.refs_0_), channel_id=1, source_target_pairs={{0,16},{1,9},{2,18},{3,11},{4,20},{5,13},{6,22},{7,15},{8,24},{9,1... | collective-permute-start | bytes 1916936 | tf_op jit(solution)/shard_map/ppermute | solution.py:73
  39.9 23.1 %collective-permute-start.8 = (bf16[4,104,768]{2,1,0:T(8,128)(2,1)S(1)}, bf16[4,104,768]{2,1,0:T(8,128)(2,1)S(1)}, u32[]{:S(2)}, u32[]{:S(2)}) collective-permute-start(bf16[4,104,768]{2,1,0:T(8,128)(2,1)S(1)} %collective-permute-done.3.refs_1_), channel_id=1, source_target_pairs={{0,8},{1,17},{2,10},{3,19},{4,12},{5,21},{6,14},{7,23},{8,0},{9,25... | collective-permute-start | bytes 1916936 | tf_op jit(solution)/shard_map/ppermute | solution.py:73
  41.8 21.2 %collective-permute-start.10 = (bf16[4,96,768]{2,1,0:T(8,128)(2,1)S(1)}, bf16[4,96,768]{2,1,0:T(8,128)(2,1)S(1)}, u32[]{:S(2)}, u32[]{:S(2)}) collective-permute-start(bf16[4,96,768]{2,1,0:T(8,128)(2,1)S(1)} %column.5.refs_0_), channel_id=1, source_target_pairs={{0,8},{1,17},{2,10},{3,19},{4,12},{5,21},{6,14},{7,23},{8,0},{9,25... | collective-permute-start | bytes 1769480 | tf_op jit(solution)/shard_map/ppermute | solution.py:73
  43.4 19.6 %collective-permute-start.9 = (bf16[4,96,768]{2,1,0:T(8,128)(2,1)S(1)}, bf16[4,96,768]{2,1,0:T(8,128)(2,1)S(1)}, u32[]{:S(2)}, u32[]{:S(2)}) collective-permute-start(bf16[4,96,768]{2,1,0:T(8,128)(2,1)S(1)} %column.5.refs_0_), channel_id=1, source_target_pairs={{0,16},{1,9},{2,18},{3,11},{4,20},{5,13},{6,22},{7,15},{8,24},{9,1... | collective-permute-start | bytes 1769480 | tf_op jit(solution)/shard_map/ppermute | solution.py:73
  67.4 15.9 %collective-permute-start.15 = (bf16[4,24,3072]{2,1,0:T(8,128)(2,1)S(1)}, bf16[4,24,3072]{2,1,0:T(8,128)(2,1)S(1)}, u32[]{:S(2)}, u32[]{:S(2)}) collective-permute-start(bf16[4,24,3072]{2,1,0:T(8,128)(2,1)S(1)} %column.6.refs_0_), channel_id=1, source_target_pairs={{0,16},{1,9},{2,18},{3,11},{4,20},{5,13},{6,22},{7,15},{8,24},{9,1... | collective-permute-start | bytes 1769480 | tf_op jit(solution)/shard_map/ppermute | solution.py:73
  70.6 18.4 %collective-permute-start.14 = (bf16[4,96,768]{2,1,0:T(8,128)(2,1)S(1)}, bf16[4,96,768]{2,1,0:T(8,128)(2,1)S(1)}, u32[]{:S(2)}, u32[]{:S(2)}) collective-permute-start(bf16[4,96,768]{2,1,0:T(8,128)(2,1)S(1)} %collective-permute-done.9.refs_1_), channel_id=1, source_target_pairs={{0,8},{1,17},{2,10},{3,19},{4,12},{5,21},{6,14},{7,23},{8,0},{9,25... | collective-permute-start | bytes 1769480 | tf_op jit(solution)/shard_map/ppermute | solution.py:73
  92.2 16.2 %collective-permute-start.22 = (bf16[4,96,768]{2,1,0:T(8,128)(2,1)S(1)}, bf16[4,96,768]{2,1,0:T(8,128)(2,1)S(1)}, u32[]{:S(2)}, u32[]{:S(2)}) collective-permute-start(bf16[4,96,768]{2,1,0:T(8,128)(2,1)S(1)} %column.7.refs_0_), channel_id=1, source_target_pairs={{0,16},{1,9},{2,18},{3,11},{4,20},{5,13},{6,22},{7,15},{8,24},{9,1... | collective-permute-start | bytes 1769480 | tf_op jit(solution)/shard_map/ppermute | solution.py:73
  92.7 14.8 %collective-permute-start.23 = (bf16[4,96,768]{2,1,0:T(8,128)(2,1)S(1)}, bf16[4,96,768]{2,1,0:T(8,128)(2,1)S(1)}, u32[]{:S(2)}, u32[]{:S(2)}) collective-permute-start(bf16[4,96,768]{2,1,0:T(8,128)(2,1)S(1)} %column.7.refs_0_), channel_id=1, source_target_pairs={{0,8},{1,17},{2,10},{3,19},{4,12},{5,21},{6,14},{7,23},{8,0},{9,25... | collective-permute-start | bytes 1769480 | tf_op jit(solution)/shard_map/ppermute | solution.py:73
  93.6 20.2 %collective-permute-start.21 = (bf16[4,24,3072]{2,1,0:T(8,128)(2,1)S(1)}, bf16[4,24,3072]{2,1,0:T(8,128)(2,1)S(1)}, u32[]{:S(2)}, u32[]{:S(2)}) collective-permute-start(bf16[4,24,3072]{2,1,0:T(8,128)(2,1)S(1)} %collective-permute-done.15.refs_1_), channel_id=1, source_target_pairs={{0,8},{1,17},{2,10},{3,19},{4,12},{5,21},{6,14},{7,23},{8,0},{9,25... | collective-permute-start | bytes 1769480 | tf_op jit(solution)/shard_map/ppermute | solution.py:73
  144.3 16.3 %collective-permute-start.32 = (bf16[2,4,96,768]{3,2,1,0:T(8,128)(2,1)S(1)}, bf16[2,4,96,768]{3,2,1,0:T(8,128)(2,1)S(1)}, u32[]{:S(2)}, u32[]{:S(2)}) collective-permute-start(bf16[2,4,96,768]{3,2,1,0:T(8,128)(2,1)S(1)} %leave.6), channel_id=1, source_target_pairs={{0,16},{1,9},{2,18},{3,11},{4,20},{5,13},{6,22},{7,15},{8,24},{9,1... | collective-permute-start | bytes 3538952 | tf_op jit(solution)/shard_map/ppermute | solution.py:73
  162.6 23.3 %collective-permute-start.34 = (bf16[2,96,768]{2,1,0:T(8,128)(2,1)S(1)}, bf16[2,96,768]{2,1,0:T(8,128)(2,1)S(1)}, u32[]{:S(2)}, u32[]{:S(2)}) collective-permute-start(bf16[2,96,768]{2,1,0:T(8,128)(2,1)S(1)} %get-tuple-element.315), channel_id=1, source_target_pairs={{0,2},{1,3},{2,4},{3,5},{4,6},{5,7},{6,0},{7,1},{8,10},{9,11},{10,... | collective-permute-start | bytes 884744 | tf_op jit(solution)/shard_map/ppermute | solution.py:73
  164.5 22.1 %collective-permute-start.35 = (bf16[2,96,768]{2,1,0:T(8,128)(2,1)S(1)}, bf16[2,96,768]{2,1,0:T(8,128)(2,1)S(1)}, u32[]{:S(2)}, u32[]{:S(2)}) collective-permute-start(bf16[2,96,768]{2,1,0:T(8,128)(2,1)S(1)} %get-tuple-element.316), channel_id=1, source_target_pairs={{0,4},{1,5},{2,6},{3,7},{4,0},{5,1},{6,2},{7,3},{8,12},{9,13},{10,... | collective-permute-start | bytes 884744 | tf_op jit(solution)/shard_map/ppermute | solution.py:73
  165.4 21.2 %collective-permute-start.36 = (bf16[2,96,768]{2,1,0:T(8,128)(2,1)S(1)}, bf16[2,96,768]{2,1,0:T(8,128)(2,1)S(1)}, u32[]{:S(2)}, u32[]{:S(2)}) collective-permute-start(bf16[2,96,768]{2,1,0:T(8,128)(2,1)S(1)} %get-tuple-element.317), channel_id=1, source_target_pairs={{0,6},{1,7},{2,0},{3,1},{4,2},{5,3},{6,4},{7,5},{8,14},{9,15},{10,... | collective-permute-start | bytes 884744 | tf_op jit(solution)/shard_map/ppermute | solution.py:73
  168.6 16.3 %collective-permute-start.37 = (bf16[2,4,24,3072]{3,2,1,0:T(8,128)(2,1)S(1)}, bf16[2,4,24,3072]{3,2,1,0:T(8,128)(2,1)S(1)}, u32[]{:S(2)}, u32[]{:S(2)}) collective-permute-start(bf16[2,4,24,3072]{3,2,1,0:T(8,128)(2,1)S(1)} %leave.7), channel_id=1, source_target_pairs={{0,16},{1,9},{2,18},{3,11},{4,20},{5,13},{6,22},{7,15},{8,24},{9,1... | collective-permute-start | bytes 3538952 | tf_op jit(solution)/shard_map/ppermute | solution.py:73
  182.0 21.4 %collective-permute-start.42 = (bf16[4,4,120,768]{3,2,1,0:T(8,128)(2,1)S(1)}, bf16[4,4,120,768]{3,2,1,0:T(8,128)(2,1)S(1)}, u32[]{:S(2)}, u32[]{:S(2)}) collective-permute-start(bf16[4,4,120,768]{3,2,1,0:T(8,128)(2,1)S(1)} %exchange.6), channel_id=1, source_target_pairs={{0,1},{1,0},{2,3},{3,2},{4,5},{5,4},{6,7},{7,6},{8,9},{9,8},{10,11... | collective-permute-start | bytes 8847368 | tf_op jit(solution)/shard_map/ppermute | solution.py:73
  186.7 27.0 %collective-permute-start.38 = (bf16[96,768]{1,0:T(8,128)(2,1)S(1)}, bf16[96,768]{1,0:T(8,128)(2,1)S(1)}, u32[]{:S(2)}, u32[]{:S(2)}) collective-permute-start(bf16[96,768]{1,0:T(8,128)(2,1)S(1)} %get-tuple-element.323), channel_id=1, source_target_pairs={{0,8},{1,17},{2,10},{3,19},{4,12},{5,21},{6,14},{7,23},{8,0},{9,25... | collective-permute-start | bytes 442376 | tf_op jit(solution)/shard_map/ppermute | solution.py:73
  187.6 18.7 %collective-permute-start.39 = (bf16[2,24,3072]{2,1,0:T(8,128)(2,1)S(1)}, bf16[2,24,3072]{2,1,0:T(8,128)(2,1)S(1)}, u32[]{:S(2)}, u32[]{:S(2)}) collective-permute-start(bf16[2,24,3072]{2,1,0:T(8,128)(2,1)S(1)} %get-tuple-element.332), channel_id=1, source_target_pairs={{0,2},{1,3},{2,4},{3,5},{4,6},{5,7},{6,0},{7,1},{8,10},{9,11},{10,... | collective-permute-start | bytes 884744 | tf_op jit(solution)/shard_map/ppermute | solution.py:73
  194.4 19.2 %collective-permute-start.40 = (bf16[2,24,3072]{2,1,0:T(8,128)(2,1)S(1)}, bf16[2,24,3072]{2,1,0:T(8,128)(2,1)S(1)}, u32[]{:S(2)}, u32[]{:S(2)}) collective-permute-start(bf16[2,24,3072]{2,1,0:T(8,128)(2,1)S(1)} %get-tuple-element.333), channel_id=1, source_target_pairs={{0,4},{1,5},{2,6},{3,7},{4,0},{5,1},{6,2},{7,3},{8,12},{9,13},{10,... | collective-permute-start | bytes 884744 | tf_op jit(solution)/shard_map/ppermute | solution.py:73
  195.0 18.6 %collective-permute-start.41 = (bf16[2,24,3072]{2,1,0:T(8,128)(2,1)S(1)}, bf16[2,24,3072]{2,1,0:T(8,128)(2,1)S(1)}, u32[]{:S(2)}, u32[]{:S(2)}) collective-permute-start(bf16[2,24,3072]{2,1,0:T(8,128)(2,1)S(1)} %get-tuple-element.334), channel_id=1, source_target_pairs={{0,6},{1,7},{2,0},{3,1},{4,2},{5,3},{6,4},{7,5},{8,14},{9,15},{10,... | collective-permute-start | bytes 884744 | tf_op jit(solution)/shard_map/ppermute | solution.py:73
  204.7 19.4 %collective-permute-start.44 = (bf16[2,4,120,768]{3,2,1,0:T(8,128)(2,1)S(1)}, bf16[2,4,120,768]{3,2,1,0:T(8,128)(2,1)S(1)}, u32[]{:S(2)}, u32[]{:S(2)}) collective-permute-start(bf16[2,4,120,768]{3,2,1,0:T(8,128)(2,1)S(1)} %leave.8), channel_id=1, source_target_pairs={{0,16},{1,9},{2,18},{3,11},{4,20},{5,13},{6,22},{7,15},{8,24},{9,1... | collective-permute-start | bytes 4423688 | tf_op jit(solution)/shard_map/ppermute | solution.py:73
  206.3 19.8 %collective-permute-start.43 = (bf16[4,4,80,768]{3,2,1,0:T(8,128)(2,1)S(1)}, bf16[4,4,80,768]{3,2,1,0:T(8,128)(2,1)S(1)}, u32[]{:S(2)}, u32[]{:S(2)}) collective-permute-start(bf16[4,4,80,768]{3,2,1,0:T(8,128)(2,1)S(1)} %exchange.7), channel_id=1, source_target_pairs={{0,1},{1,0},{2,3},{3,2},{4,5},{5,4},{6,7},{7,6},{8,9},{9,8},{10,11... | collective-permute-start | bytes 5898248 | tf_op jit(solution)/shard_map/ppermute | solution.py:73
  254.2 14.9 %collective-permute-start.52 = (bf16[120,768]{1,0:T(8,128)(2,1)S(1)}, bf16[120,768]{1,0:T(8,128)(2,1)S(1)}, u32[]{:S(2)}, u32[]{:S(2)}) collective-permute-start(bf16[120,768]{1,0:T(8,128)(2,1)S(1)} %get-tuple-element.380), channel_id=1, source_target_pairs={{0,2},{1,3},{2,4},{3,5},{4,6},{5,7},{6,0},{7,1},{8,10},{9,11},{10,... | collective-permute-start | bytes 552968 | tf_op jit(solution)/shard_map/ppermute | solution.py:73
  256.5 15.3 %collective-permute-start.53 = (bf16[120,768]{1,0:T(8,128)(2,1)S(1)}, bf16[120,768]{1,0:T(8,128)(2,1)S(1)}, u32[]{:S(2)}, u32[]{:S(2)}) collective-permute-start(bf16[120,768]{1,0:T(8,128)(2,1)S(1)} %get-tuple-element.381), channel_id=1, source_target_pairs={{0,4},{1,5},{2,6},{3,7},{4,0},{5,1},{6,2},{7,3},{8,12},{9,13},{10,... | collective-permute-start | bytes 552968 | tf_op jit(solution)/shard_map/ppermute | solution.py:73
  (86 other events, 736.2 us)

commit v3 on v2

--- a/solution.py
+++ b/solution.py
@@ -19,7 +19,7 @@
 BF = jnp.bfloat16
 F32 = jnp.float32
 QUICK = pl.CostEstimate(flops=1000, bytes_accessed=1000, transcendentals=0)
-LONG = pl.CostEstimate(flops=10**11, bytes_accessed=10**6, transcendentals=0)
+LONG = pl.CostEstimate(flops=4 * 10**10, bytes_accessed=10**6, transcendentals=0)
 
 
 class Place:
@@ -119,6 +119,26 @@
         cost_estimate=QUICK,
         name=name,
     )(place.spots, *ins)
+
+
+def fence_kernel(in_ref, out_ref):
+    for i in range(in_ref.shape[0]):
+        out_ref[i] = in_ref[i]
+
+
+def fence(place, *values):
+    spots = place.spots
+    scalars = pl.BlockSpec(memory_space=pltpu.SMEM)
+    place.spots = pl.pallas_call(
+        fence_kernel,
+        in_specs=[scalars],
+        out_specs=scalars,
+        out_shape=jax.ShapeDtypeStruct(spots.shape, spots.dtype),
+        compiler_params=pltpu.CompilerParams(vmem_limit_bytes=1 << 20),
+        cost_estimate=LONG,
+        name="fence",
+    )(after(spots, *values))
+    return place.spots
 
 
 class Gather:
@@ -1137,16 +1157,17 @@
         x2b, after(du, sent), expand, dr3, r2, gains[1]
     )
     sent = r_contract.line(dc)
-    r_expand = reduce_hop_last(place, [owner_blocks(place, after(d_expand, sent))])
+    r_expand = reduce(place, [owner_blocks(place, after(d_expand, sent))])
     sent = r_expand.leave(0, dc)
     *d_cross, dk2, dv2, dr1, da, cross_sums = cross_back(
         after(dc, sent), co, cq, q2, k2, v2, p2, o2, x1b, memory, dr2, r1, gains[0], o, count
     )
     r_cross = reduce(place, [owner_blocks(place, d) for d in d_cross])
-    sent = r_expand.line(da)
-    sent = r_contract.turn(sent)
-    *d_self, dq, dk, dv, self_sums = self_back(after(da, sent), wo, q, k, v, p, x, count)
-    sent = r_cross.leave(0, self_sums)
+    *d_self, dq, dk, dv, self_sums = self_back(
+        after(da, r_cross.sent), wo, q, k, v, p, x, count
+    )
+    sent = r_expand.leave(1, self_sums)
+    sent = r_cross.leave(0, sent)
     small_blocks = split_small(
         ff_sums,
         cross_sums,
@@ -1161,23 +1182,25 @@
         place,
         [owner_blocks(place, d) for d in after(d_self, sent)] + [small_blocks],
     )
-    sent = r_expand.turn(r_self.sent)
-    (own_contract,) = r_contract.result([((4 * rows, D), 0, 0)], sent)
-    dq, dk, dv, dk2, dv2 = after((dq, dk, dv, dk2, dv2), own_contract)
+    sent = r_contract.turn(r_self.sent)
+    dq, dk, dv, dk2, dv2 = after((dq, dk, dv, dk2, dv2), sent)
     input_grad, encoder_grad = inputs_back(
         dq, dk, dv, wq, wk, wv, dr1, dk2, dv2, ck, cv
     )
-    r_cross.leave(1, input_grad)
+    (own_contract,) = r_contract.result([((4 * rows, D), 0, 0)], input_grad)
+    sent = r_expand.last(own_contract)
+    sent = r_cross.leave(1, fence(place, sent))
+    (own_expand,) = r_expand.result([((rows, FF), 0, 0)], sent)
+    fence(place, own_expand)
     sent = r_self.leave(0, r_cross.latest())
     sent = r_cross.last(sent)
-    sent = r_self.leave(1, sent)
-    (own_expand,) = r_expand.result([((rows, FF), 0, 0)], sent)
-    sent = r_self.last(own_expand)
+    sent = r_self.leave(1, fence(place, sent))
     projects = ((3, rows, D), 0, 0)
     square = (rows, D)
     own_cross = r_cross.result(
         [projects, (square, 3 * rows, 0), (square, 4 * rows, 0)], sent
     )
+    r_self.last(fence(place, own_cross[0]))
     at = 3 * rows
     own_self = r_self.result(
         [

time: 285 us -> 273 us (0.958)
  waiting for transfers between devices: 119 us -> 94.9 us
  local copies, waits for them, and re-layouts: 6.71 us -> 16.1 us
  Pallas kernels: 71.1 us -> 77 us
  starting transfers between devices: 61 us -> 58 us
    ppermute x55, waiting for transfers between devices: 119 us -> 94.9 us  [permute(): return lax.ppermute(value, AXES, pairs)]
    unnamed x111 -> x123, local copies, waits for them, and re-layouts: 5.9 us -> 15.2 us
    pallas_call x0 -> x4, Pallas kernels: none -> 4.58 us  [fence(): pl.pallas_call(fence_kernel, in_specs=[scalars], out_specs=scalars, out_s...]
    ppermute x55, starting transfers between devices: 61 us -> 58 us  [permute(): return lax.ppermute(value, AXES, pairs)]
    pallas_call x6 -> x7, Pallas kernels: 6.3 us -> 7.02 us  [leave(): self.call(functools.partial(leave_kernel, len(self.blocks)), (count,), sp...]
  transfers between devices with their start and end apart: 55 -> 55, of which waited for: 31 -> 30; matrix products, arithmetic and copies ran while one was open for 5% -> 5% of each run, Pallas kernels for 19% -> 22%
where the time goes in v3:
time: 273 us; the launch traced here: 270 us
  waiting for transfers between devices  94.9 us (35%)
  Pallas kernels  77 us (28%)
  starting transfers between devices  58 us (21%)
  matrix products  17.5 us (6%)
  local copies, waits for them, and re-layouts  16.1 us (6%)
  other arithmetic  4.32 us (2%)
    ppermute x55, waiting for transfers between devices, permute(): return lax.ppermute(value, AXES, pairs)  94.9 us
    ppermute x55, starting transfers between devices, permute(): return lax.ppermute(value, AXES, pairs)  58 us
    unnamed x123, local copies, waits for them, and re-layouts  15.2 us
    dot_general x10, matrix products, dot_nn(): return jnp.dot(a, b, preferred_element_type=F32)  14.6 us
    pallas_call x11, Pallas kernels, copy_call(): pl.pallas_call(functools.partial(copy_kernel, plan, len(ins)), grid_spec=...  13.1 us
    pallas_call x1, Pallas kernels, cross_back(): pl.pallas_call(functools.partial(cross_back_kernel, count), out_shape=[sq...  8.52 us
    pallas_call x1, Pallas kernels, expand_back(): pl.pallas_call(expand_back_kernel, grid=(FF // D,), in_specs=[still, movi...  7.94 us
    pallas_call x2, Pallas kernels, attend(): pl.pallas_call(functools.partial(attend_kernel, masked), grid_spec=pltpu....  7.79 us
  transfers between devices with their start and end apart: 55, of which 30 were waited for; matrix products, arithmetic and copies ran while one was open for 5% of the time, Pallas kernels for 22%

profile of v3, /device:TPU:0, one launch (start us, length us, event | category | flops | bytes accessed | tf_op | source)
XLA Modules:
  0.0 269.7 jit_solution(10725746848028715452)
XLA Ops:
  1.7 5.1 %collective-permute-start.2 = (bf16[104,768]{1,0:T(8,128)(2,1)S(1)}, bf16[104,768]{1,0:T(8,128)(2,1)S(1)}, u32[]{:S(2)}, u32[]{:S(2)}) collective-permute-start(bf16[104,768]{1,0:T(8,128)(2,1)S(1)} %pack_self.1.refs_0_), channel_id=1, source_target_pairs={{0,6},{1,7},{2,0},{3,1},{4,2},{5,3},{6,4},{7,5},{8,14},{9,15},{10,... | collective-permute-start | bytes 479240 | tf_op jit(solution)/shard_map/ppermute | solution.py:73
  11.4 9.0 %collective-permute-done.1.refs_2_ = bf16[104,768]{1,0:T(8,128)(2,1)S(1)} collective-permute-done((bf16[104,768]{1,0:T(8,128)(2,1)S(1)}, bf16[104,768]{1,0:T(8,128)(2,1)S(1)}, u32[]{:S(2)}, u32[]{:S(2)}) %collective-permute-start.1) | collective-permute-done | bytes 159776 | tf_op jit(solution)/shard_map/ppermute | solution.py:73
  30.9 8.9 %collective-permute-done.6.refs_2_ = bf16[96,768]{1,0:T(8,128)(2,1)S(1)} collective-permute-done((bf16[96,768]{1,0:T(8,128)(2,1)S(1)}, bf16[96,768]{1,0:T(8,128)(2,1)S(1)}, u32[]{:S(2)}, u32[]{:S(2)}) %collective-permute-start.6) | collective-permute-done | bytes 147488 | tf_op jit(solution)/shard_map/ppermute | solution.py:73
  45.3 4.2 %collective-permute-done.13.refs_3_ = bf16[24,3072]{1,0:T(8,128)(2,1)S(1)} collective-permute-done((bf16[24,3072]{1,0:T(8,128)(2,1)S(1)}, bf16[24,3072]{1,0:T(8,128)(2,1)S(1)}, u32[]{:S(2)}, u32[]{:S(2)}) %collective-permute-start.13) | collective-permute-done | bytes 147488 | tf_op jit(solution)/shard_map/ppermute | solution.py:73
  51.4 7.3 %collective-permute-done.12.refs_2_ = bf16[24,3072]{1,0:T(8,128)(2,1)S(1)} collective-permute-done((bf16[24,3072]{1,0:T(8,128)(2,1)S(1)}, bf16[24,3072]{1,0:T(8,128)(2,1)S(1)}, u32[]{:S(2)}, u32[]{:S(2)}) %collective-permute-start.12) | collective-permute-done | bytes 147488 | tf_op jit(solution)/shard_map/ppermute | solution.py:73
  58.7 4.3 %collective-permute-done.10.refs_2_ = bf16[4,96,768]{2,1,0:T(8,128)(2,1)S(1)} collective-permute-done((bf16[4,96,768]{2,1,0:T(8,128)(2,1)S(1)}, bf16[4,96,768]{2,1,0:T(8,128)(2,1)S(1)}, u32[]{:S(2)}, u32[]{:S(2)}) %collective-permute-start.10) | collective-permute-done | bytes 589856 | tf_op jit(solution)/shard_map/ppermute | solution.py:73
  76.3 4.0 %attend.2 = (bf16[512,768]{1,0:T(8,128)(2,1)S(1)}, bf16[2,12,256,256]{3,2,1,0:T(8,128)(2,1)S(1)}) custom-call(s32[2]{0:T(128)S(1)} %copy-done.14, s32[2]{0:T(128)S(1)} %copy-done.15, bf16[512,768]{1,0:T(8,128)(2,1)S(1)} %fusion.12.q_ref, bf16[512,768]{1,0:T(8,128)(2,1)S(1)} %fusion.15.k_ref, bf16[512,768]{1,0:T(8,128)(2,1)S(1)} %fusion.13.v_ref), custom_call_target="tpu_custom_call" | custom-call | flops 1000 | bytes 1000 | tf_op jit(solution)/shard_map/attend/pallas_call | solution.py:554
  83.3 5.7 %collective-permute-done.14.refs_3_ = bf16[4,96,768]{2,1,0:T(8,128)(2,1)S(1)} collective-permute-done((bf16[4,96,768]{2,1,0:T(8,128)(2,1)S(1)}, bf16[4,96,768]{2,1,0:T(8,128)(2,1)S(1)}, u32[]{:S(2)}, u32[]{:S(2)}) %collective-permute-start.14) | collective-permute-done | bytes 589856 | tf_op jit(solution)/shard_map/ppermute | solution.py:73
  100.9 3.8 %attend.3 = (bf16[512,768]{1,0:T(8,128)(2,1)S(1)}, bf16[2,12,256,256]{3,2,1,0:T(8,128)(2,1)S(1)}) custom-call(s32[2]{0:T(128)S(1)} %copy-done.14, s32[2]{0:T(128)S(1)} %copy-done.15, bf16[512,768]{1,0:T(8,128)(2,1)S(1)} %multiply_convert_fusion.1.q_ref, bf16[512,768]{1,0:T(8,128)(2,1)S(1)} %fusion.16.k_ref, bf16[512,768]{1,0:T(8,128)(2,1)S(1)} %fusion.14.v_ref), custom_call_target="tpu_custom_call" | custom-call | flops 1000 | bytes 1000 | tf_op jit(solution)/shard_map/attend/pallas_call | solution.py:554
  108.4 5.5 %collective-permute-done.21.refs_3_ = bf16[4,24,3072]{2,1,0:T(8,128)(2,1)S(1)} collective-permute-done((bf16[4,24,3072]{2,1,0:T(8,128)(2,1)S(1)}, bf16[4,24,3072]{2,1,0:T(8,128)(2,1)S(1)}, u32[]{:S(2)}, u32[]{:S(2)}) %collective-permute-start.21) | collective-permute-done | bytes 589856 | tf_op jit(solution)/shard_map/ppermute | solution.py:73
  120.8 5.1 %fusion.4 = (bf16[512,3072]{1,0:T(8,128)(2,1)S(1)}, bf16[512,3072]{1,0:T(8,128)(2,1)S(1)}) fusion(f32[3072]{0:T(1024)S(1)} %bitcast.195, bf16[512,768]{1,0:T(8,128)(2,1)S(1)} %fusion.18.x_ref, bf16[768,3072]{1,0:T(8,128)(2,1)S(1)} %bitcast.166), kind=kOutput, calls=%fused_computation.5 | convolution fusion | flops 2434793472 | bytes 11808768 | tf_op jit(solution)/shard_map/dot_general | solution.py:511
  134.8 2.9 %convolution_convert_fusion = bf16[3072,768]{1,0:T(8,128)(2,1)S(1)} fusion(bf16[512,3072]{1,0:T(8,128)(2,1)S(1)} %get-tuple-element.419, bf16[512,768]{1,0:T(8,128)(2,1)S(1)} %get-tuple-element.303.df_ref), kind=kOutput, calls=%fused_computation.8 | convolution fusion | flops 2418278400 | bytes 8650752 | tf_op jit(solution)/shard_map/dot_general | solution.py:515
  139.1 3.9 %hidden_back.1 = (bf16[512,3072]{1,0:T(8,128)(2,1)S(1)}, f32[1,3072]{1,0:T(1,128)S(1)}) custom-call(bf16[512,768]{1,0:T(8,128)(2,1)S(1)} %get-tuple-element.303.df_ref, bf16[3072,768]{1,0:T(8,128)(2,1)S(1)} %bitcast.169, bf16[512,3072]{1,0:T(8,128)(2,1)S(1)} %get-tuple-element.418.slope_ref), custom_call_target="tpu_custom_call" | custom-call | flops 40000000000 | bytes 1000000 | tf_op jit(solution)/shard_map/hidden_back/pallas_call | solution.py:610
  144.9 7.9 %expand_back.1 = (bf16[768,3072]{1,0:T(8,128)(2,1)S(1)}, f32[512,768]{1,0:T(8,128)S(1)}, bf16[512,768]{1,0:T(8,128)(2,1)S(1)}, f32[8,768]{1,0:T(8,128)S(1)}) custom-call(bf16[512,768]{1,0:T(8,128)(2,1)S(1)} %fusion.18.x_ref, bf16[512,3072]{1,0:T(8,128)(2,1)S(1)} %get-tuple-element.306.du_ref, bf16[768,3072]{1,0:T(8,128)(2,1)S(1)} %bitcast.167, ...), custom_call_target="tpu_custom_call" | custom-call | flops 40000000000 | bytes 1000000 | tf_op jit(solution)/shard_map/expand_back/pallas_call | solution.py:659
  152.9 7.7 %collective-permute-done.32.refs_2_.refs_5_.refs_8_.refs_11_.refs_14_.refs_17_.refs_20_.refs_23_ = bf16[2,4,96,768]{3,2,1,0:T(8,128)(2,1)S(1)} collective-permute-done((bf16[2,4,96,768]{3,2,1,0:T(8,128)(2,1)S(1)}, bf16[2,4,96,768]{3,2,1,0:T(8,128)(2,1)S(1)}, u32[]{:S(2)}, u32[]{:S(2)}) %collective-permute-start.32) | collective-permute-done | bytes 1179680 | tf_op jit(solution)/shard_map/ppermute | solution.py:73
  169.9 8.5 %cross_back.1 = (bf16[768,768]{1,0:T(8,128)(2,1)S(1)}, bf16[768,768]{1,0:T(8,128)(2,1)S(1)}, bf16[768,768]{1,0:T(8,128)(2,1)S(1)}, bf16[768,768]{1,0:T(8,128)(2,...) custom-call(bf16[512,768]{1,0:T(8,128)(2,1)S(1)} %get-tuple-element., ...), custom_call_target="tpu_custom_call" | custom-call | flops 40000000000 | bytes 1000000 | tf_op jit(solution)/shard_map/cross_back/pallas_call | solution.py:764
  185.3 6.3 %self_back.1 = (bf16[768,768]{1,0:T(8,128)(2,1)S(1)}, bf16[768,768]{1,0:T(8,128)(2,1)S(1)}, bf16[768,768]{1,0:T(8,128)(2,1)S(1)}, bf16[512,768]{1,0:T(8,128)(2,1...) custom-call(bf16[512,768]{1,0:T(8,128)(2,1)S(1)} %copy-done.51, ...), custom_call_target="tpu_custom_call" | custom-call | flops 40000000000 | bytes 1000000 | tf_op jit(solution)/shard_map/self_back/pallas_call | solution.py:821
  204.1 4.8 %inputs_back.1 = (f32[512,768]{1,0:T(8,128)}, f32[512,768]{1,0:T(8,128)}) custom-call(bf16[512,768]{1,0:T(8,128)(2,1)S(1)} %copy-done.53, bf16[512,768]{1,0:T(8,128)(2,1)S(1)} %copy-done.55, bf16[512,768]{1,0:T(8,128)(2,1)S(1)} %copy-done.57, bf16[768,768]{1,0:T(8,128)(2,1)S(1)} %bitcast.172, bf16[768,768]{1,0:T(8,128)(2,1)S(1)} %bitcast.174, ...), custom_call_target="tpu_custom_call" | custom-call | flops 40000000000 | bytes 1000000 | tf_op jit(solution)/shard_map/inputs_back/pallas_call | solution.py:848
  221.6 3.9 %collective-permute-done.42.refs_2_ = bf16[24,3072]{1,0:T(8,128)(2,1)S(1)} collective-permute-done((bf16[24,3072]{1,0:T(8,128)(2,1)S(1)}, bf16[24,3072]{1,0:T(8,128)(2,1)S(1)}, u32[]{:S(2)}, u32[]{:S(2)}) %collective-permute-start.42) | collective-permute-done | bytes 147488 | tf_op jit(solution)/shard_map/ppermute | solution.py:73
  227.4 4.4 %collective-permute-done.45.refs_7_.refs_15_.refs_23_.refs_31_ = bf16[1,4,120,768]{3,2,1,0:T(8,128)(2,1)S(1)} collective-permute-done((bf16[1,4,120,768]{3,2,1,0:T(8,128)(2,1)S(1)}, bf16[1,4,120,768]{3,2,1,0:T(8,128)(2,1)S(1)}, u32[]{:S(2)}, u32[]{:S(2)}) %collective-permute-start.45) | collective-permute-done | bytes 737312 | tf_op jit(solution)/shard_map/ppermute | solution.py:73
  240.3 6.7 %collective-permute-done.50.refs_5_.refs_12_.refs_19_.refs_26_ = bf16[2,4,80,768]{3,2,1,0:T(8,128)(2,1)S(1)} collective-permute-done((bf16[2,4,80,768]{3,2,1,0:T(8,128)(2,1)S(1)}, bf16[2,4,80,768]{3,2,1,0:T(8,128)(2,1)S(1)}, u32[]{:S(2)}, u32[]{:S(2)}) %collective-permute-start.50) | collective-permute-done | bytes 983072 | tf_op jit(solution)/shard_map/ppermute | solution.py:73
  252.9 3.8 %collective-permute-done.51.refs_6_.refs_13_.refs_20_.refs_27_ = bf16[1,4,80,768]{3,2,1,0:T(8,128)(2,1)S(1)} collective-permute-done((bf16[1,4,80,768]{3,2,1,0:T(8,128)(2,1)S(1)}, bf16[1,4,80,768]{3,2,1,0:T(8,128)(2,1)S(1)}, u32[]{:S(2)}, u32[]{:S(2)}) %collective-permute-start.51) | collective-permute-done | bytes 491552 | tf_op jit(solution)/shard_map/ppermute | solution.py:73
  261.8 3.9 %collective-permute-done.52.refs_1_ = bf16[80,768]{1,0:T(8,128)(2,1)S(1)} collective-permute-done((bf16[80,768]{1,0:T(8,128)(2,1)S(1)}, bf16[80,768]{1,0:T(8,128)(2,1)S(1)}, u32[]{:S(2)}, u32[]{:S(2)}) %collective-permute-start.52) | collective-permute-done | bytes 122912 | tf_op jit(solution)/shard_map/ppermute | solution.py:73
  265.6 3.1 %collective-permute-done.53.refs_2_ = bf16[80,768]{1,0:T(8,128)(2,1)S(1)} collective-permute-done((bf16[80,768]{1,0:T(8,128)(2,1)S(1)}, bf16[80,768]{1,0:T(8,128)(2,1)S(1)}, u32[]{:S(2)}, u32[]{:S(2)}) %collective-permute-start.53) | collective-permute-done | bytes 122912 | tf_op jit(solution)/shard_map/ppermute | solution.py:73
  (284 shorter events, 136.9 us)
Async XLA Ops:
  21.8 18.1 %collective-permute-start.4 = (bf16[4,104,768]{2,1,0:T(8,128)(2,1)S(1)}, bf16[4,104,768]{2,1,0:T(8,128)(2,1)S(1)}, u32[]{:S(2)}, u32[]{:S(2)}) collective-permute-start(bf16[4,104,768]{2,1,0:T(8,128)(2,1)S(1)} %column.4.refs_0_), channel_id=1, source_target_pairs={{0,8},{1,17},{2,10},{3,19},{4,12},{5,21},{6,14},{7,23},{8,0},{9,25... | collective-permute-start | bytes 1916936 | tf_op jit(solution)/shard_map/ppermute | solution.py:73
  23.3 16.6 %collective-permute-start.3 = (bf16[4,104,768]{2,1,0:T(8,128)(2,1)S(1)}, bf16[4,104,768]{2,1,0:T(8,128)(2,1)S(1)}, u32[]{:S(2)}, u32[]{:S(2)}) collective-permute-start(bf16[4,104,768]{2,1,0:T(8,128)(2,1)S(1)} %column.4.refs_0_), channel_id=1, source_target_pairs={{0,16},{1,9},{2,18},{3,11},{4,20},{5,13},{6,22},{7,15},{8,24},{9,1... | collective-permute-start | bytes 1916936 | tf_op jit(solution)/shard_map/ppermute | solution.py:73
  39.9 23.1 %collective-permute-start.8 = (bf16[4,104,768]{2,1,0:T(8,128)(2,1)S(1)}, bf16[4,104,768]{2,1,0:T(8,128)(2,1)S(1)}, u32[]{:S(2)}, u32[]{:S(2)}) collective-permute-start(bf16[4,104,768]{2,1,0:T(8,128)(2,1)S(1)} %collective-permute-done.3.refs_1_), channel_id=1, source_target_pairs={{0,8},{1,17},{2,10},{3,19},{4,12},{5,21},{6,14},{7,23},{8,0},{9,25... | collective-permute-start | bytes 1916936 | tf_op jit(solution)/shard_map/ppermute | solution.py:73
  41.8 21.2 %collective-permute-start.10 = (bf16[4,96,768]{2,1,0:T(8,128)(2,1)S(1)}, bf16[4,96,768]{2,1,0:T(8,128)(2,1)S(1)}, u32[]{:S(2)}, u32[]{:S(2)}) collective-permute-start(bf16[4,96,768]{2,1,0:T(8,128)(2,1)S(1)} %column.5.refs_0_), channel_id=1, source_target_pairs={{0,8},{1,17},{2,10},{3,19},{4,12},{5,21},{6,14},{7,23},{8,0},{9,25... | collective-permute-start | bytes 1769480 | tf_op jit(solution)/shard_map/ppermute | solution.py:73
  43.4 19.6 %collective-permute-start.9 = (bf16[4,96,768]{2,1,0:T(8,128)(2,1)S(1)}, bf16[4,96,768]{2,1,0:T(8,128)(2,1)S(1)}, u32[]{:S(2)}, u32[]{:S(2)}) collective-permute-start(bf16[4,96,768]{2,1,0:T(8,128)(2,1)S(1)} %column.5.refs_0_), channel_id=1, source_target_pairs={{0,16},{1,9},{2,18},{3,11},{4,20},{5,13},{6,22},{7,15},{8,24},{9,1... | collective-permute-start | bytes 1769480 | tf_op jit(solution)/shard_map/ppermute | solution.py:73
  43.9 14.8 %collective-permute-start.12 = (bf16[24,3072]{1,0:T(8,128)(2,1)S(1)}, bf16[24,3072]{1,0:T(8,128)(2,1)S(1)}, u32[]{:S(2)}, u32[]{:S(2)}) collective-permute-start(bf16[24,3072]{1,0:T(8,128)(2,1)S(1)} %copy-done.12), channel_id=1, source_target_pairs={{0,4},{1,5},{2,6},{3,7},{4,0},{5,1},{6,2},{7,3},{8,12},{9,13},{10,... | collective-permute-start | bytes 442376 | tf_op jit(solution)/shard_map/ppermute | solution.py:73
  65.9 16.1 %collective-permute-start.18 = (bf16[96,768]{1,0:T(8,128)(2,1)S(1)}, bf16[96,768]{1,0:T(8,128)(2,1)S(1)}, u32[]{:S(2)}, u32[]{:S(2)}) collective-permute-start(bf16[96,768]{1,0:T(8,128)(2,1)S(1)} %copy-done.13), channel_id=1, source_target_pairs={{0,4},{1,5},{2,6},{3,7},{4,0},{5,1},{6,2},{7,3},{8,12},{9,13},{10,... | collective-permute-start | bytes 442376 | tf_op jit(solution)/shard_map/ppermute | solution.py:73
  67.4 15.9 %collective-permute-start.15 = (bf16[4,24,3072]{2,1,0:T(8,128)(2,1)S(1)}, bf16[4,24,3072]{2,1,0:T(8,128)(2,1)S(1)}, u32[]{:S(2)}, u32[]{:S(2)}) collective-permute-start(bf16[4,24,3072]{2,1,0:T(8,128)(2,1)S(1)} %column.6.refs_0_), channel_id=1, source_target_pairs={{0,16},{1,9},{2,18},{3,11},{4,20},{5,13},{6,22},{7,15},{8,24},{9,1... | collective-permute-start | bytes 1769480 | tf_op jit(solution)/shard_map/ppermute | solution.py:73
  67.9 14.8 %collective-permute-start.16 = (bf16[4,24,3072]{2,1,0:T(8,128)(2,1)S(1)}, bf16[4,24,3072]{2,1,0:T(8,128)(2,1)S(1)}, u32[]{:S(2)}, u32[]{:S(2)}) collective-permute-start(bf16[4,24,3072]{2,1,0:T(8,128)(2,1)S(1)} %column.6.refs_0_), channel_id=1, source_target_pairs={{0,8},{1,17},{2,10},{3,19},{4,12},{5,21},{6,14},{7,23},{8,0},{9,25... | collective-permute-start | bytes 1769480 | tf_op jit(solution)/shard_map/ppermute | solution.py:73
  70.6 18.4 %collective-permute-start.14 = (bf16[4,96,768]{2,1,0:T(8,128)(2,1)S(1)}, bf16[4,96,768]{2,1,0:T(8,128)(2,1)S(1)}, u32[]{:S(2)}, u32[]{:S(2)}) collective-permute-start(bf16[4,96,768]{2,1,0:T(8,128)(2,1)S(1)} %collective-permute-done.9.refs_1_), channel_id=1, source_target_pairs={{0,8},{1,17},{2,10},{3,19},{4,12},{5,21},{6,14},{7,23},{8,0},{9,25... | collective-permute-start | bytes 1769480 | tf_op jit(solution)/shard_map/ppermute | solution.py:73
  92.2 16.2 %collective-permute-start.22 = (bf16[4,96,768]{2,1,0:T(8,128)(2,1)S(1)}, bf16[4,96,768]{2,1,0:T(8,128)(2,1)S(1)}, u32[]{:S(2)}, u32[]{:S(2)}) collective-permute-start(bf16[4,96,768]{2,1,0:T(8,128)(2,1)S(1)} %column.7.refs_0_), channel_id=1, source_target_pairs={{0,16},{1,9},{2,18},{3,11},{4,20},{5,13},{6,22},{7,15},{8,24},{9,1... | collective-permute-start | bytes 1769480 | tf_op jit(solution)/shard_map/ppermute | solution.py:73
  92.7 14.8 %collective-permute-start.23 = (bf16[4,96,768]{2,1,0:T(8,128)(2,1)S(1)}, bf16[4,96,768]{2,1,0:T(8,128)(2,1)S(1)}, u32[]{:S(2)}, u32[]{:S(2)}) collective-permute-start(bf16[4,96,768]{2,1,0:T(8,128)(2,1)S(1)} %column.7.refs_0_), channel_id=1, source_target_pairs={{0,8},{1,17},{2,10},{3,19},{4,12},{5,21},{6,14},{7,23},{8,0},{9,25... | collective-permute-start | bytes 1769480 | tf_op jit(solution)/shard_map/ppermute | solution.py:73
  93.6 20.2 %collective-permute-start.21 = (bf16[4,24,3072]{2,1,0:T(8,128)(2,1)S(1)}, bf16[4,24,3072]{2,1,0:T(8,128)(2,1)S(1)}, u32[]{:S(2)}, u32[]{:S(2)}) collective-permute-start(bf16[4,24,3072]{2,1,0:T(8,128)(2,1)S(1)} %collective-permute-done.15.refs_1_), channel_id=1, source_target_pairs={{0,8},{1,17},{2,10},{3,19},{4,12},{5,21},{6,14},{7,23},{8,0},{9,25... | collective-permute-start | bytes 1769480 | tf_op jit(solution)/shard_map/ppermute | solution.py:73
  144.3 16.3 %collective-permute-start.32 = (bf16[2,4,96,768]{3,2,1,0:T(8,128)(2,1)S(1)}, bf16[2,4,96,768]{3,2,1,0:T(8,128)(2,1)S(1)}, u32[]{:S(2)}, u32[]{:S(2)}) collective-permute-start(bf16[2,4,96,768]{3,2,1,0:T(8,128)(2,1)S(1)} %leave.7), channel_id=1, source_target_pairs={{0,16},{1,9},{2,18},{3,11},{4,20},{5,13},{6,22},{7,15},{8,24},{9,1... | collective-permute-start | bytes 3538952 | tf_op jit(solution)/shard_map/ppermute | solution.py:73
  163.3 34.4 %collective-permute-start.34 = (bf16[2,96,768]{2,1,0:T(8,128)(2,1)}, bf16[2,96,768]{2,1,0:T(8,128)(2,1)S(1)}, u32[]{:S(2)}, u32[]{:S(2)}) collective-permute-start(bf16[2,96,768]{2,1,0:T(8,128)(2,1)} %get-tuple-element.329), channel_id=1, source_target_pairs={{0,2},{1,3},{2,4},{3,5},{4,6},{5,7},{6,0},{7,1},{8,10},{9,11},{10,... | collective-permute-start | bytes 884744 | tf_op jit(solution)/shard_map/ppermute | solution.py:73
  165.2 32.7 %collective-permute-start.35 = (bf16[2,96,768]{2,1,0:T(8,128)(2,1)}, bf16[2,96,768]{2,1,0:T(8,128)(2,1)S(1)}, u32[]{:S(2)}, u32[]{:S(2)}) collective-permute-start(bf16[2,96,768]{2,1,0:T(8,128)(2,1)} %get-tuple-element.330), channel_id=1, source_target_pairs={{0,4},{1,5},{2,6},{3,7},{4,0},{5,1},{6,2},{7,3},{8,12},{9,13},{10,... | collective-permute-start | bytes 884744 | tf_op jit(solution)/shard_map/ppermute | solution.py:73
  166.1 31.8 %collective-permute-start.36 = (bf16[2,96,768]{2,1,0:T(8,128)(2,1)S(1)}, bf16[2,96,768]{2,1,0:T(8,128)(2,1)S(1)}, u32[]{:S(2)}, u32[]{:S(2)}) collective-permute-start(bf16[2,96,768]{2,1,0:T(8,128)(2,1)S(1)} %get-tuple-element.331), channel_id=1, source_target_pairs={{0,6},{1,7},{2,0},{3,1},{4,2},{5,3},{6,4},{7,5},{8,14},{9,15},{10,... | collective-permute-start | bytes 884744 | tf_op jit(solution)/shard_map/ppermute | solution.py:73
  169.3 22.5 %collective-permute-start.38 = (bf16[2,4,24,3072]{3,2,1,0:T(8,128)(2,1)S(1)}, bf16[2,4,24,3072]{3,2,1,0:T(8,128)(2,1)S(1)}, u32[]{:S(2)}, u32[]{:S(2)}) collective-permute-start(bf16[2,4,24,3072]{3,2,1,0:T(8,128)(2,1)S(1)} %leave.8), channel_id=1, source_target_pairs={{0,16},{1,9},{2,18},{3,11},{4,20},{5,13},{6,22},{7,15},{8,24},{9,1... | collective-permute-start | bytes 3538952 | tf_op jit(solution)/shard_map/ppermute | solution.py:73
  193.0 19.4 %collective-permute-start.39 = (bf16[1,4,24,3072]{3,2,1,0:T(8,128)(2,1)S(1)}, bf16[1,4,24,3072]{3,2,1,0:T(8,128)(2,1)S(1)}, u32[]{:S(2)}, u32[]{:S(2)}) collective-permute-start(bf16[1,4,24,3072]{3,2,1,0:T(8,128)(2,1)S(1)} %leave.9), channel_id=1, source_target_pairs={{0,8},{1,17},{2,10},{3,19},{4,12},{5,21},{6,14},{7,23},{8,0},{9,25... | collective-permute-start | bytes 1769480 | tf_op jit(solution)/shard_map/ppermute | solution.py:73
  195.1 24.4 %collective-permute-start.44 = (bf16[2,4,120,768]{3,2,1,0:T(8,128)(2,1)S(1)}, bf16[2,4,120,768]{3,2,1,0:T(8,128)(2,1)S(1)}, u32[]{:S(2)}, u32[]{:S(2)}) collective-permute-start(bf16[2,4,120,768]{3,2,1,0:T(8,128)(2,1)S(1)} %leave.10), channel_id=1, source_target_pairs={{0,16},{1,9},{2,18},{3,11},{4,20},{5,13},{6,22},{7,15},{8,24},{9,1... | collective-permute-start | bytes 4423688 | tf_op jit(solution)/shard_map/ppermute | solution.py:73
  197.7 29.7 %collective-permute-start.46 = (bf16[4,4,80,768]{3,2,1,0:T(8,128)(2,1)S(1)}, bf16[4,4,80,768]{3,2,1,0:T(8,128)(2,1)S(1)}, u32[]{:S(2)}, u32[]{:S(2)}) collective-permute-start(bf16[4,4,80,768]{3,2,1,0:T(8,128)(2,1)S(1)} %exchange.7), channel_id=1, source_target_pairs={{0,1},{1,0},{2,3},{3,2},{4,5},{5,4},{6,7},{7,6},{8,9},{9,8},{10,11... | collective-permute-start | bytes 5898248 | tf_op jit(solution)/shard_map/ppermute | solution.py:73
  232.9 14.2 %collective-permute-start.50 = (bf16[2,4,80,768]{3,2,1,0:T(8,128)(2,1)S(1)}, bf16[2,4,80,768]{3,2,1,0:T(8,128)(2,1)S(1)}, u32[]{:S(2)}, u32[]{:S(2)}) collective-permute-start(bf16[2,4,80,768]{3,2,1,0:T(8,128)(2,1)S(1)} %leave.12), channel_id=1, source_target_pairs={{0,16},{1,9},{2,18},{3,11},{4,20},{5,13},{6,22},{7,15},{8,24},{9,1... | collective-permute-start | bytes 2949128 | tf_op jit(solution)/shard_map/ppermute | solution.py:73
  235.1 13.9 %collective-permute-start.47 = (bf16[120,768]{1,0:T(8,128)(2,1)S(1)}, bf16[120,768]{1,0:T(8,128)(2,1)S(1)}, u32[]{:S(2)}, u32[]{:S(2)}) collective-permute-start(bf16[120,768]{1,0:T(8,128)(2,1)S(1)} %get-tuple-element.373), channel_id=1, source_target_pairs={{0,2},{1,3},{2,4},{3,5},{4,6},{5,7},{6,0},{7,1},{8,10},{9,11},{10,... | collective-permute-start | bytes 552968 | tf_op jit(solution)/shard_map/ppermute | solution.py:73
  236.2 14.7 %collective-permute-start.48 = (bf16[120,768]{1,0:T(8,128)(2,1)S(1)}, bf16[120,768]{1,0:T(8,128)(2,1)S(1)}, u32[]{:S(2)}, u32[]{:S(2)}) collective-permute-start(bf16[120,768]{1,0:T(8,128)(2,1)S(1)} %get-tuple-element.374), channel_id=1, source_target_pairs={{0,4},{1,5},{2,6},{3,7},{4,0},{5,1},{6,2},{7,3},{8,12},{9,13},{10,... | collective-permute-start | bytes 552968 | tf_op jit(solution)/shard_map/ppermute | solution.py:73
  (92 other events, 603.7 us)

commit v4 on v3

--- a/solution.py
+++ b/solution.py
@@ -489,6 +489,8 @@
     def latest(self):
         return self.sum
 
+    got = [None]
+
     def line(self, *earlier):
         return self.sum
 
@@ -630,18 +632,15 @@
 
 
 def expand_back_kernel(
-    x_ref, du_ref, e_ref, dr3_ref, r2_ref, gain_ref, de_ref, dr2_ref, dc_ref, sum_ref, xt_ref
+    du_ref, e_ref, dr3_ref, r2_ref, gain_ref, dr2_ref, dc_ref, sum_ref
 ):
     j = pl.program_id(0)
 
     @pl.when(j == 0)
     def _():
-        xt_ref[...] = x_ref[...].T
         dr2_ref[...] = dr3_ref[...]
 
-    du = du_ref[...]
-    de_ref[...] = dot_nn(xt_ref[...], du).astype(BF)
-    dr2_ref[...] += dot_nt(du, e_ref[...])
+    dr2_ref[...] += dot_nt(du_ref[...], e_ref[...])
 
     @pl.when(j == pl.num_programs(0) - 1)
     def _():
@@ -652,33 +651,30 @@
         put_rows(sum_ref, sums + [row_sum(dc)])
 
 
-def expand_back(x2b, du, expand, dr3, r2, gain):
-    tokens = x2b.shape[0]
+def expand_back(du, expand, dr3, r2, gain):
+    tokens = du.shape[0]
     still = pl.BlockSpec((tokens, D), lambda j: (0, 0))
     moving = lambda n: pl.BlockSpec((n, D), lambda j: (0, j))
     return pl.pallas_call(
         expand_back_kernel,
         grid=(FF // D,),
         in_specs=[
-            still,
             moving(tokens),
             moving(D),
             still,
             still,
             pl.BlockSpec((1, D), lambda j: (0, 0)),
         ],
-        out_specs=[moving(D), still, still, pl.BlockSpec((8, D), lambda j: (0, 0))],
+        out_specs=[still, still, pl.BlockSpec((8, D), lambda j: (0, 0))],
         out_shape=[
-            jax.ShapeDtypeStruct((D, FF), BF),
             jax.ShapeDtypeStruct((tokens, D), F32),
             jax.ShapeDtypeStruct((tokens, D), BF),
             jax.ShapeDtypeStruct((8, D), F32),
         ],
-        scratch_shapes=[pltpu.VMEM((D, tokens), BF)],
-        compiler_params=pltpu.CompilerParams(vmem_limit_bytes=24 << 20),
+        compiler_params=pltpu.CompilerParams(vmem_limit_bytes=20 << 20),
         cost_estimate=LONG,
         name="expand_back",
-    )(x2b, du, expand, dr3, r2, gain)
+    )(du, expand, dr3, r2, gain)
 
 
 def heads_back(count, q_ref, k_ref, v_ref, p_ref, g_ref, outs, moved_ref, ds_ref):
@@ -832,29 +828,22 @@
     )(da, wo, q, k, v, p, x)
 
 
-def inputs_back_kernel(
-    dq_ref, dk_ref, dv_ref, wq_ref, wk_ref, wv_ref, dr1_ref, dk2_ref, dv2_ref, ck_ref, cv_ref, dx_ref, de_ref
-):
-    de_ref[...] = dot_nt(dk2_ref[...], ck_ref[...]) + dot_nt(dv2_ref[...], cv_ref[...])
-    dx_ref[...] = (
-        dr1_ref[...]
-        + dot_nt(dq_ref[...], wq_ref[...])
-        + dot_nt(dk_ref[...], wk_ref[...])
-        + dot_nt(dv_ref[...], wv_ref[...])
-    )
-
-
-def inputs_back(dq, dk, dv, wq, wk, wv, dr1, dk2, dv2, ck, cv):
+def rows_back_kernel(n, *refs):
+    total = None if len(refs) == 2 * n + 1 else refs[2 * n][...]
+    for g, w in zip(refs[:n], refs[n : 2 * n]):
+        part = dot_nt(g[...], w[...])
+        total = part if total is None else total + part
+    refs[-1][...] = total
+
+
+def rows_back(grads, weights, start=()):
     return pl.pallas_call(
-        inputs_back_kernel,
-        out_shape=[
-            jax.ShapeDtypeStruct(dr1.shape, F32),
-            jax.ShapeDtypeStruct(dk2.shape, F32),
-        ],
+        functools.partial(rows_back_kernel, len(grads)),
+        out_shape=jax.ShapeDtypeStruct(grads[0].shape, F32),
         compiler_params=pltpu.CompilerParams(vmem_limit_bytes=10 << 20),
         cost_estimate=LONG,
-        name="inputs_back",
-    )(dq, dk, dv, wq, wk, wv, dr1, dk2, dv2, ck, cv)
+        name="rows_back",
+    )(*grads, *weights, *start)
 
 
 def norm(summed):
@@ -1153,21 +1142,22 @@
     d_contract_b = column_sum(df)
     du, d_expand_b = hidden_back(after(df, d_contract), contract, slope)
     sent = r_contract.leave(0, du)
-    d_expand, dr2, dc, ff_sums = expand_back(
-        x2b, after(du, sent), expand, dr3, r2, gains[1]
-    )
-    sent = r_contract.line(dc)
-    r_expand = reduce(place, [owner_blocks(place, after(d_expand, sent))])
+    d_expand = dot_tn(x2b, after(du, sent)).astype(BF)
+    r_expand = reduce(place, [owner_blocks(place, d_expand)])
+    dr2, dc, ff_sums = expand_back(
+        after(du, r_expand.sent), expand, dr3, r2, gains[1]
+    )
     sent = r_expand.leave(0, dc)
+    sent = r_contract.line(sent)
     *d_cross, dk2, dv2, dr1, da, cross_sums = cross_back(
         after(dc, sent), co, cq, q2, k2, v2, p2, o2, x1b, memory, dr2, r1, gains[0], o, count
     )
     r_cross = reduce(place, [owner_blocks(place, d) for d in d_cross])
-    *d_self, dq, dk, dv, self_sums = self_back(
-        after(da, r_cross.sent), wo, q, k, v, p, x, count
-    )
-    sent = r_expand.leave(1, self_sums)
-    sent = r_cross.leave(0, sent)
+    sent = r_expand.leave(1, r_cross.sent)
+    fence(place, sent)
+    sent = r_cross.leave(0, place.spots)
+    *d_self, dq, dk, dv, self_sums = self_back(after(da, sent), wo, q, k, v, p, x, count)
+    sent = r_expand.last(self_sums)
     small_blocks = split_small(
         ff_sums,
         cross_sums,
@@ -1183,15 +1173,12 @@
         [owner_blocks(place, d) for d in after(d_self, sent)] + [small_blocks],
     )
     sent = r_contract.turn(r_self.sent)
-    dq, dk, dv, dk2, dv2 = after((dq, dk, dv, dk2, dv2), sent)
-    input_grad, encoder_grad = inputs_back(
-        dq, dk, dv, wq, wk, wv, dr1, dk2, dv2, ck, cv
-    )
-    (own_contract,) = r_contract.result([((4 * rows, D), 0, 0)], input_grad)
-    sent = r_expand.last(own_contract)
-    sent = r_cross.leave(1, fence(place, sent))
+    encoder_grad = rows_back(after([dk2, dv2], sent), [ck, cv])
+    sent = r_cross.leave(1, encoder_grad)
     (own_expand,) = r_expand.result([((rows, FF), 0, 0)], sent)
-    fence(place, own_expand)
+    (own_contract,) = r_contract.result([((4 * rows, D), 0, 0)], own_expand)
+    input_grad = rows_back(after([dq, dk, dv], own_contract), [wq, wk, wv], [dr1])
+    r_cross.got[-1] = after(r_cross.latest(), input_grad)
     sent = r_self.leave(0, r_cross.latest())
     sent = r_cross.last(sent)
     sent = r_self.leave(1, fence(place, sent))

time: 273 us -> 262 us (0.960)
  local copies, waits for them, and re-layouts: 16.1 us -> 8.49 us
  matrix products: 17.5 us -> 22.9 us
  waiting for transfers between devices: 94.9 us -> 89.6 us
  Pallas kernels: 77 us -> 73.9 us
    unnamed x123 -> x107, local copies, waits for them, and re-layouts: 15.2 us -> 7.69 us
    ppermute x55, waiting for transfers between devices: 94.9 us -> 89.6 us  [permute(): return lax.ppermute(value, AXES, pairs)]
    dot_general x1 -> x2, matrix products: 2.92 us -> 6.27 us  [dot_tn(): lax.dot_general(a, b, (((0,), (0,)), ((), ())), preferred_element_type=F32)]
    pallas_call x2 -> x3, Pallas kernels: 12.7 us -> 10.9 us  [the longest x2 5.78 us: rows_back(): pl.pallas_call(functools.partial(rows_back_kernel, len(grads)), out_shape...]
  transfers between devices with their start and end apart: 55 -> 55, of which waited for: 30 -> 27; matrix products, arithmetic and copies ran while one was open for 5% -> 7% of each run, Pallas kernels for 22% -> 23%
where the time goes in v4:
time: 262 us; the launch traced here: 259 us
  waiting for transfers between devices  89.6 us (34%)
  Pallas kernels  73.9 us (28%)
  starting transfers between devices  57.9 us (22%)
  matrix products  22.9 us (9%)
  local copies, waits for them, and re-layouts  8.49 us (3%)
  other arithmetic  3.99 us (2%)
    ppermute x55, waiting for transfers between devices, permute(): return lax.ppermute(value, AXES, pairs)  89.6 us
    ppermute x55, starting transfers between devices, permute(): return lax.ppermute(value, AXES, pairs)  57.9 us
    dot_general x10, matrix products, dot_nn(): return jnp.dot(a, b, preferred_element_type=F32)  16.6 us
    pallas_call x11, Pallas kernels, copy_call(): pl.pallas_call(functools.partial(copy_kernel, plan, len(ins)), grid_spec=...  13.2 us
    pallas_call x1, Pallas kernels, cross_back(): pl.pallas_call(functools.partial(cross_back_kernel, count), out_shape=[sq...  8.57 us
    pallas_call x2, Pallas kernels, attend(): pl.pallas_call(functools.partial(attend_kernel, masked), grid_spec=pltpu....  7.77 us
    unnamed x107, local copies, waits for them, and re-layouts  7.69 us
    pallas_call x7, Pallas kernels, leave(): self.call(functools.partial(leave_kernel, len(self.blocks)), (count,), sp...  6.63 us
  transfers between devices with their start and end apart: 55, of which 27 were waited for; matrix products, arithmetic and copies ran while one was open for 7% of the time, Pallas kernels for 23%

profile of v4, /device:TPU:0, one launch (start us, length us, event | category | flops | bytes accessed | tf_op | source)
XLA Modules:
  0.0 258.6 jit_solution(4883544506667517582)
XLA Ops:
  1.7 5.1 %collective-permute-start.2 = (bf16[104,768]{1,0:T(8,128)(2,1)S(1)}, bf16[104,768]{1,0:T(8,128)(2,1)S(1)}, u32[]{:S(2)}, u32[]{:S(2)}) collective-permute-start(bf16[104,768]{1,0:T(8,128)(2,1)S(1)} %pack_self.1.refs_0_), channel_id=1, source_target_pairs={{0,6},{1,7},{2,0},{3,1},{4,2},{5,3},{6,4},{7,5},{8,14},{9,15},{10,... | collective-permute-start | bytes 479240 | tf_op jit(solution)/shard_map/ppermute | solution.py:73
  8.5 2.9 %collective-permute-done.2.refs_3_ = bf16[104,768]{1,0:T(8,128)(2,1)S(1)} collective-permute-done((bf16[104,768]{1,0:T(8,128)(2,1)S(1)}, bf16[104,768]{1,0:T(8,128)(2,1)S(1)}, u32[]{:S(2)}, u32[]{:S(2)}) %collective-permute-start.2) | collective-permute-done | bytes 159776 | tf_op jit(solution)/shard_map/ppermute | solution.py:73
  11.4 9.0 %collective-permute-done.1.refs_2_ = bf16[104,768]{1,0:T(8,128)(2,1)S(1)} collective-permute-done((bf16[104,768]{1,0:T(8,128)(2,1)S(1)}, bf16[104,768]{1,0:T(8,128)(2,1)S(1)}, u32[]{:S(2)}, u32[]{:S(2)}) %collective-permute-start.1) | collective-permute-done | bytes 159776 | tf_op jit(solution)/shard_map/ppermute | solution.py:73
  30.9 8.9 %collective-permute-done.6.refs_2_ = bf16[96,768]{1,0:T(8,128)(2,1)S(1)} collective-permute-done((bf16[96,768]{1,0:T(8,128)(2,1)S(1)}, bf16[96,768]{1,0:T(8,128)(2,1)S(1)}, u32[]{:S(2)}, u32[]{:S(2)}) %collective-permute-start.6) | collective-permute-done | bytes 147488 | tf_op jit(solution)/shard_map/ppermute | solution.py:73
  45.3 4.2 %collective-permute-done.13.refs_3_ = bf16[24,3072]{1,0:T(8,128)(2,1)S(1)} collective-permute-done((bf16[24,3072]{1,0:T(8,128)(2,1)S(1)}, bf16[24,3072]{1,0:T(8,128)(2,1)S(1)}, u32[]{:S(2)}, u32[]{:S(2)}) %collective-permute-start.13) | collective-permute-done | bytes 147488 | tf_op jit(solution)/shard_map/ppermute | solution.py:73
  51.4 7.3 %collective-permute-done.12.refs_2_ = bf16[24,3072]{1,0:T(8,128)(2,1)S(1)} collective-permute-done((bf16[24,3072]{1,0:T(8,128)(2,1)S(1)}, bf16[24,3072]{1,0:T(8,128)(2,1)S(1)}, u32[]{:S(2)}, u32[]{:S(2)}) %collective-permute-start.12) | collective-permute-done | bytes 147488 | tf_op jit(solution)/shard_map/ppermute | solution.py:73
  58.7 4.3 %collective-permute-done.10.refs_2_ = bf16[4,96,768]{2,1,0:T(8,128)(2,1)S(1)} collective-permute-done((bf16[4,96,768]{2,1,0:T(8,128)(2,1)S(1)}, bf16[4,96,768]{2,1,0:T(8,128)(2,1)S(1)}, u32[]{:S(2)}, u32[]{:S(2)}) %collective-permute-start.10) | collective-permute-done | bytes 589856 | tf_op jit(solution)/shard_map/ppermute | solution.py:73
  76.2 4.0 %attend.2 = (bf16[512,768]{1,0:T(8,128)(2,1)S(1)}, bf16[2,12,256,256]{3,2,1,0:T(8,128)(2,1)S(1)}) custom-call(s32[2]{0:T(128)S(1)} %copy-done.10, s32[2]{0:T(128)S(1)} %copy-done.11, bf16[512,768]{1,0:T(8,128)(2,1)S(1)} %fusion.12.q_ref, bf16[512,768]{1,0:T(8,128)(2,1)S(1)} %fusion.15.k_ref, bf16[512,768]{1,0:T(8,128)(2,1)S(1)} %fusion.13.v_ref), custom_call_target="tpu_custom_call" | custom-call | flops 1000 | bytes 1000 | tf_op jit(solution)/shard_map/attend/pallas_call | solution.py:556
  83.3 5.7 %collective-permute-done.14.refs_3_ = bf16[4,96,768]{2,1,0:T(8,128)(2,1)S(1)} collective-permute-done((bf16[4,96,768]{2,1,0:T(8,128)(2,1)S(1)}, bf16[4,96,768]{2,1,0:T(8,128)(2,1)S(1)}, u32[]{:S(2)}, u32[]{:S(2)}) %collective-permute-start.14) | collective-permute-done | bytes 589856 | tf_op jit(solution)/shard_map/ppermute | solution.py:73
  100.8 3.7 %attend.3 = (bf16[512,768]{1,0:T(8,128)(2,1)S(1)}, bf16[2,12,256,256]{3,2,1,0:T(8,128)(2,1)S(1)}) custom-call(s32[2]{0:T(128)S(1)} %copy-done.10, s32[2]{0:T(128)S(1)} %copy-done.11, bf16[512,768]{1,0:T(8,128)(2,1)S(1)} %multiply_convert_fusion.1.q_ref, bf16[512,768]{1,0:T(8,128)(2,1)S(1)} %fusion.16.k_ref, bf16[512,768]{1,0:T(8,128)(2,1)S(1)} %fusion.14.v_ref), custom_call_target="tpu_custom_call" | custom-call | flops 1000 | bytes 1000 | tf_op jit(solution)/shard_map/attend/pallas_call | solution.py:556
  108.4 5.5 %collective-permute-done.21.refs_3_ = bf16[4,24,3072]{2,1,0:T(8,128)(2,1)S(1)} collective-permute-done((bf16[4,24,3072]{2,1,0:T(8,128)(2,1)S(1)}, bf16[4,24,3072]{2,1,0:T(8,128)(2,1)S(1)}, u32[]{:S(2)}, u32[]{:S(2)}) %collective-permute-start.21) | collective-permute-done | bytes 589856 | tf_op jit(solution)/shard_map/ppermute | solution.py:73
  120.8 7.2 %fusion.4 = (bf16[512,3072]{1,0:T(8,128)(2,1)}, bf16[512,3072]{1,0:T(8,128)(2,1)S(1)}) fusion(f32[3072]{0:T(1024)S(1)} %bitcast.195, bf16[768,3072]{1,0:T(8,128)(2,1)S(1)} %bitcast.166, f32[512,768]{1,0:T(8,128)S(1)} %get-tuple-element.420.r2_ref, f32[768]{0:T(1024)S(1)} %get-tuple-element.401, f32[768]{0:T(1024)S(1)} %get-tuple-element.398, ...), kind=kOutput, calls=%fused_computation.5 | convolution fusion | flops 2436759552 | bytes 12605440 | tf_op jit(solution)/shard_map/dot_general | solution.py:513
  136.8 2.9 %convolution_convert_fusion.1 = bf16[3072,768]{1,0:T(8,128)(2,1)S(1)} fusion(bf16[512,3072]{1,0:T(8,128)(2,1)S(1)} %get-tuple-element.413, bf16[512,768]{1,0:T(8,128)(2,1)S(1)} %get-tuple-element.300.df_ref), kind=kOutput, calls=%fused_computation.9 | convolution fusion | flops 2418278400 | bytes 8650752 | tf_op jit(solution)/shard_map/dot_general | solution.py:517
  141.6 3.9 %hidden_back.1 = (bf16[512,3072]{1,0:T(8,128)(2,1)S(1)}, f32[1,3072]{1,0:T(1,128)S(1)}) custom-call(bf16[512,768]{1,0:T(8,128)(2,1)S(1)} %get-tuple-element.300.df_ref, bf16[3072,768]{1,0:T(8,128)(2,1)S(1)} %bitcast.169, bf16[512,3072]{1,0:T(8,128)(2,1)S(1)} %copy-done.41), custom_call_target="tpu_custom_call" | custom-call | flops 40000000000 | bytes 1000000 | tf_op jit(solution)/shard_map/hidden_back/pallas_call | solution.py:612
  147.3 3.4 %convolution_convert_fusion = bf16[768,3072]{1,0:T(8,128)(2,1)S(1)} fusion(bf16[512,3072]{1,0:T(8,128)(2,1)S(1)} %get-tuple-element.304.du_ref, f32[512,768]{1,0:T(8,128)S(1)} %get-tuple-element.420.r2_ref, f32[768]{0:T(1024)S(1)} %get-tuple-element.401, f32[768]{0:T(1024)S(1)} %get-tuple-element.398, f32[512]{0:T(512)S(1)} %add_rsqrt_fusion.1, ...), kind=kOutput, calls=%fused_computation.8 | convolution fusion | flops 2420244480 | bytes 9447424 | tf_op jit(solution)/shard_map/dot_general | solution.py:517
  152.5 5.1 %expand_back.1 = (f32[512,768]{1,0:T(8,128)S(1)}, bf16[512,768]{1,0:T(8,128)(2,1)S(1)}, f32[8,768]{1,0:T(8,128)S(1)}) custom-call(bf16[512,3072]{1,0:T(8,128)(2,1)S(1)} %copy-done.40, bf16[768,3072]{1,0:T(8,128)(2,1)S(1)} %bitcast.167, f32[512,768]{1,0:T(8,128)S(1)} %get-tuple-element.411.dr3_ref, f32[512,768]{1,0:T(8,128)S(1)} %get-tuple-element.420.r2_ref, ...), custom_call_target="tpu_custom_call" | custom-call | flops 40000000000 | bytes 1000000 | tf_op jit(solution)/shard_map/expand_back/pallas_call | solution.py:658
  169.2 8.6 %cross_back.1 = (bf16[768,768]{1,0:T(8,128)(2,1)S(1)}, bf16[768,768]{1,0:T(8,128)(2,1)S(1)}, bf16[768,768]{1,0:T(8,128)(2,1)S(1)}, bf16[768,768]{1,0:T(8,128)(2,...) custom-call(bf16[512,768]{1,0:T(8,128)(2,1)S(1)} %get-tuple-element., ...), custom_call_target="tpu_custom_call" | custom-call | flops 40000000000 | bytes 1000000 | tf_op jit(solution)/shard_map/cross_back/pallas_call | solution.py:760
  188.5 6.3 %self_back.1 = (bf16[768,768]{1,0:T(8,128)(2,1)S(1)}, bf16[768,768]{1,0:T(8,128)(2,1)S(1)}, bf16[768,768]{1,0:T(8,128)(2,1)S(1)}, bf16[512,768]{1,0:T(8,128)(2,1...) custom-call(bf16[512,768]{1,0:T(8,128)(2,1)S(1)} %copy-done.49, ...), custom_call_target="tpu_custom_call" | custom-call | flops 40000000000 | bytes 1000000 | tf_op jit(solution)/shard_map/self_back/pallas_call | solution.py:817
  205.4 3.5 %collective-permute-done.44.refs_6_.refs_14_.refs_22_.refs_30_ = bf16[2,4,120,768]{3,2,1,0:T(8,128)(2,1)S(1)} collective-permute-done((bf16[2,4,120,768]{3,2,1,0:T(8,128)(2,1)S(1)}, bf16[2,4,120,768]{3,2,1,0:T(8,128)(2,1)S(1)}, u32[]{:S(2)}, u32[]{:S(2)}) %collective-permute-start.44) | collective-permute-done | bytes 1474592 | tf_op jit(solution)/shard_map/ppermute | solution.py:73
  212.9 3.2 %rows_back.3 = f32[512,768]{1,0:T(8,128)} custom-call(bf16[512,768]{1,0:T(8,128)(2,1)S(1)} %get-tuple-element.358.refs_0_, bf16[512,768]{1,0:T(8,128)(2,1)S(1)} %get-tuple-element.359.refs_1_, bf16[512,768]{1,0:T(8,128)(2,1)S(1)} %get-tuple-element.360.refs_2_, bf16[768,768]{1,0:T(8,128)(2,1)S(1)} %bitcast.172, bf16[768,768]{1,0:T(8,128)(2,1)S(1)} %bitcast.174, ...), custom_call_target="tpu_custom_call" | custom-call | flops 40000000000 | bytes 1000000 | tf_op jit(solution)/shard_map/rows_back/pallas_call | solution.py:840
  216.1 5.8 %collective-permute-done.45.refs_7_.refs_15_.refs_23_.refs_31_ = bf16[1,4,120,768]{3,2,1,0:T(8,128)(2,1)S(1)} collective-permute-done((bf16[1,4,120,768]{3,2,1,0:T(8,128)(2,1)S(1)}, bf16[1,4,120,768]{3,2,1,0:T(8,128)(2,1)S(1)}, u32[]{:S(2)}, u32[]{:S(2)}) %collective-permute-start.45) | collective-permute-done | bytes 737312 | tf_op jit(solution)/shard_map/ppermute | solution.py:73
  230.2 7.0 %collective-permute-done.50.refs_5_.refs_12_.refs_19_.refs_26_ = bf16[2,4,80,768]{3,2,1,0:T(8,128)(2,1)S(1)} collective-permute-done((bf16[2,4,80,768]{3,2,1,0:T(8,128)(2,1)S(1)}, bf16[2,4,80,768]{3,2,1,0:T(8,128)(2,1)S(1)}, u32[]{:S(2)}, u32[]{:S(2)}) %collective-permute-start.50) | collective-permute-done | bytes 983072 | tf_op jit(solution)/shard_map/ppermute | solution.py:73
  242.2 4.6 %collective-permute-done.51.refs_6_.refs_13_.refs_20_.refs_27_ = bf16[1,4,80,768]{3,2,1,0:T(8,128)(2,1)S(1)} collective-permute-done((bf16[1,4,80,768]{3,2,1,0:T(8,128)(2,1)S(1)}, bf16[1,4,80,768]{3,2,1,0:T(8,128)(2,1)S(1)}, u32[]{:S(2)}, u32[]{:S(2)}) %collective-permute-start.51) | collective-permute-done | bytes 491552 | tf_op jit(solution)/shard_map/ppermute | solution.py:73
  252.0 3.0 %collective-permute-done.52.refs_1_ = bf16[80,768]{1,0:T(8,128)(2,1)S(1)} collective-permute-done((bf16[80,768]{1,0:T(8,128)(2,1)S(1)}, bf16[80,768]{1,0:T(8,128)(2,1)S(1)}, u32[]{:S(2)}, u32[]{:S(2)}) %collective-permute-start.52) | collective-permute-done | bytes 122912 | tf_op jit(solution)/shard_map/ppermute | solution.py:73
  (268 shorter events, 131.4 us)
Async XLA Ops:
  21.8 18.1 %collective-permute-start.4 = (bf16[4,104,768]{2,1,0:T(8,128)(2,1)S(1)}, bf16[4,104,768]{2,1,0:T(8,128)(2,1)S(1)}, u32[]{:S(2)}, u32[]{:S(2)}) collective-permute-start(bf16[4,104,768]{2,1,0:T(8,128)(2,1)S(1)} %column.4.refs_0_), channel_id=1, source_target_pairs={{0,8},{1,17},{2,10},{3,19},{4,12},{5,21},{6,14},{7,23},{8,0},{9,25... | collective-permute-start | bytes 1916936 | tf_op jit(solution)/shard_map/ppermute | solution.py:73
  23.3 16.6 %collective-permute-start.3 = (bf16[4,104,768]{2,1,0:T(8,128)(2,1)S(1)}, bf16[4,104,768]{2,1,0:T(8,128)(2,1)S(1)}, u32[]{:S(2)}, u32[]{:S(2)}) collective-permute-start(bf16[4,104,768]{2,1,0:T(8,128)(2,1)S(1)} %column.4.refs_0_), channel_id=1, source_target_pairs={{0,16},{1,9},{2,18},{3,11},{4,20},{5,13},{6,22},{7,15},{8,24},{9,1... | collective-permute-start | bytes 1916936 | tf_op jit(solution)/shard_map/ppermute | solution.py:73
  26.1 13.8 %collective-permute-start.6 = (bf16[96,768]{1,0:T(8,128)(2,1)S(1)}, bf16[96,768]{1,0:T(8,128)(2,1)S(1)}, u32[]{:S(2)}, u32[]{:S(2)}) collective-permute-start(bf16[96,768]{1,0:T(8,128)(2,1)S(1)} %pad_maximum_fusion.refs_0_), channel_id=1, source_target_pairs={{0,4},{1,5},{2,6},{3,7},{4,0},{5,1},{6,2},{7,3},{8,12},{9,13},{10,... | collective-permute-start | bytes 442376 | tf_op jit(solution)/shard_map/ppermute | solution.py:73
  39.9 23.1 %collective-permute-start.8 = (bf16[4,104,768]{2,1,0:T(8,128)(2,1)S(1)}, bf16[4,104,768]{2,1,0:T(8,128)(2,1)S(1)}, u32[]{:S(2)}, u32[]{:S(2)}) collective-permute-start(bf16[4,104,768]{2,1,0:T(8,128)(2,1)S(1)} %collective-permute-done.3.refs_1_), channel_id=1, source_target_pairs={{0,8},{1,17},{2,10},{3,19},{4,12},{5,21},{6,14},{7,23},{8,0},{9,25... | collective-permute-start | bytes 1916936 | tf_op jit(solution)/shard_map/ppermute | solution.py:73
  41.8 21.2 %collective-permute-start.10 = (bf16[4,96,768]{2,1,0:T(8,128)(2,1)S(1)}, bf16[4,96,768]{2,1,0:T(8,128)(2,1)S(1)}, u32[]{:S(2)}, u32[]{:S(2)}) collective-permute-start(bf16[4,96,768]{2,1,0:T(8,128)(2,1)S(1)} %column.5.refs_0_), channel_id=1, source_target_pairs={{0,8},{1,17},{2,10},{3,19},{4,12},{5,21},{6,14},{7,23},{8,0},{9,25... | collective-permute-start | bytes 1769480 | tf_op jit(solution)/shard_map/ppermute | solution.py:73
  43.4 19.6 %collective-permute-start.9 = (bf16[4,96,768]{2,1,0:T(8,128)(2,1)S(1)}, bf16[4,96,768]{2,1,0:T(8,128)(2,1)S(1)}, u32[]{:S(2)}, u32[]{:S(2)}) collective-permute-start(bf16[4,96,768]{2,1,0:T(8,128)(2,1)S(1)} %column.5.refs_0_), channel_id=1, source_target_pairs={{0,16},{1,9},{2,18},{3,11},{4,20},{5,13},{6,22},{7,15},{8,24},{9,1... | collective-permute-start | bytes 1769480 | tf_op jit(solution)/shard_map/ppermute | solution.py:73
  43.9 14.8 %collective-permute-start.12 = (bf16[24,3072]{1,0:T(8,128)(2,1)S(1)}, bf16[24,3072]{1,0:T(8,128)(2,1)S(1)}, u32[]{:S(2)}, u32[]{:S(2)}) collective-permute-start(bf16[24,3072]{1,0:T(8,128)(2,1)S(1)} %copy-done.8), channel_id=1, source_target_pairs={{0,4},{1,5},{2,6},{3,7},{4,0},{5,1},{6,2},{7,3},{8,12},{9,13},{10,... | collective-permute-start | bytes 442376 | tf_op jit(solution)/shard_map/ppermute | solution.py:73
  65.9 16.0 %collective-permute-start.18 = (bf16[96,768]{1,0:T(8,128)(2,1)S(1)}, bf16[96,768]{1,0:T(8,128)(2,1)S(1)}, u32[]{:S(2)}, u32[]{:S(2)}) collective-permute-start(bf16[96,768]{1,0:T(8,128)(2,1)S(1)} %copy-done.9), channel_id=1, source_target_pairs={{0,4},{1,5},{2,6},{3,7},{4,0},{5,1},{6,2},{7,3},{8,12},{9,13},{10,... | collective-permute-start | bytes 442376 | tf_op jit(solution)/shard_map/ppermute | solution.py:73
  67.4 15.9 %collective-permute-start.15 = (bf16[4,24,3072]{2,1,0:T(8,128)(2,1)S(1)}, bf16[4,24,3072]{2,1,0:T(8,128)(2,1)S(1)}, u32[]{:S(2)}, u32[]{:S(2)}) collective-permute-start(bf16[4,24,3072]{2,1,0:T(8,128)(2,1)S(1)} %column.6.refs_0_), channel_id=1, source_target_pairs={{0,16},{1,9},{2,18},{3,11},{4,20},{5,13},{6,22},{7,15},{8,24},{9,1... | collective-permute-start | bytes 1769480 | tf_op jit(solution)/shard_map/ppermute | solution.py:73
  67.9 14.8 %collective-permute-start.16 = (bf16[4,24,3072]{2,1,0:T(8,128)(2,1)S(1)}, bf16[4,24,3072]{2,1,0:T(8,128)(2,1)S(1)}, u32[]{:S(2)}, u32[]{:S(2)}) collective-permute-start(bf16[4,24,3072]{2,1,0:T(8,128)(2,1)S(1)} %column.6.refs_0_), channel_id=1, source_target_pairs={{0,8},{1,17},{2,10},{3,19},{4,12},{5,21},{6,14},{7,23},{8,0},{9,25... | collective-permute-start | bytes 1769480 | tf_op jit(solution)/shard_map/ppermute | solution.py:73
  70.6 18.4 %collective-permute-start.14 = (bf16[4,96,768]{2,1,0:T(8,128)(2,1)S(1)}, bf16[4,96,768]{2,1,0:T(8,128)(2,1)S(1)}, u32[]{:S(2)}, u32[]{:S(2)}) collective-permute-start(bf16[4,96,768]{2,1,0:T(8,128)(2,1)S(1)} %collective-permute-done.9.refs_1_), channel_id=1, source_target_pairs={{0,8},{1,17},{2,10},{3,19},{4,12},{5,21},{6,14},{7,23},{8,0},{9,25... | collective-permute-start | bytes 1769480 | tf_op jit(solution)/shard_map/ppermute | solution.py:73
  92.2 16.2 %collective-permute-start.22 = (bf16[4,96,768]{2,1,0:T(8,128)(2,1)S(1)}, bf16[4,96,768]{2,1,0:T(8,128)(2,1)S(1)}, u32[]{:S(2)}, u32[]{:S(2)}) collective-permute-start(bf16[4,96,768]{2,1,0:T(8,128)(2,1)S(1)} %column.7.refs_0_), channel_id=1, source_target_pairs={{0,16},{1,9},{2,18},{3,11},{4,20},{5,13},{6,22},{7,15},{8,24},{9,1... | collective-permute-start | bytes 1769480 | tf_op jit(solution)/shard_map/ppermute | solution.py:73
  92.7 14.8 %collective-permute-start.23 = (bf16[4,96,768]{2,1,0:T(8,128)(2,1)S(1)}, bf16[4,96,768]{2,1,0:T(8,128)(2,1)S(1)}, u32[]{:S(2)}, u32[]{:S(2)}) collective-permute-start(bf16[4,96,768]{2,1,0:T(8,128)(2,1)S(1)} %column.7.refs_0_), channel_id=1, source_target_pairs={{0,8},{1,17},{2,10},{3,19},{4,12},{5,21},{6,14},{7,23},{8,0},{9,25... | collective-permute-start | bytes 1769480 | tf_op jit(solution)/shard_map/ppermute | solution.py:73
  93.6 20.2 %collective-permute-start.21 = (bf16[4,24,3072]{2,1,0:T(8,128)(2,1)S(1)}, bf16[4,24,3072]{2,1,0:T(8,128)(2,1)S(1)}, u32[]{:S(2)}, u32[]{:S(2)}) collective-permute-start(bf16[4,24,3072]{2,1,0:T(8,128)(2,1)S(1)} %collective-permute-done.15.refs_1_), channel_id=1, source_target_pairs={{0,8},{1,17},{2,10},{3,19},{4,12},{5,21},{6,14},{7,23},{8,0},{9,25... | collective-permute-start | bytes 1769480 | tf_op jit(solution)/shard_map/ppermute | solution.py:73
  146.6 16.3 %collective-permute-start.32 = (bf16[2,4,96,768]{3,2,1,0:T(8,128)(2,1)S(1)}, bf16[2,4,96,768]{3,2,1,0:T(8,128)(2,1)S(1)}, u32[]{:S(2)}, u32[]{:S(2)}) collective-permute-start(bf16[2,4,96,768]{3,2,1,0:T(8,128)(2,1)S(1)} %leave.7), channel_id=1, source_target_pairs={{0,16},{1,9},{2,18},{3,11},{4,20},{5,13},{6,22},{7,15},{8,24},{9,1... | collective-permute-start | bytes 3538952 | tf_op jit(solution)/shard_map/ppermute | solution.py:73
  158.7 22.6 %collective-permute-start.34 = (bf16[2,4,24,3072]{3,2,1,0:T(8,128)(2,1)S(1)}, bf16[2,4,24,3072]{3,2,1,0:T(8,128)(2,1)S(1)}, u32[]{:S(2)}, u32[]{:S(2)}) collective-permute-start(bf16[2,4,24,3072]{3,2,1,0:T(8,128)(2,1)S(1)} %leave.8), channel_id=1, source_target_pairs={{0,16},{1,9},{2,18},{3,11},{4,20},{5,13},{6,22},{7,15},{8,24},{9,1... | collective-permute-start | bytes 3538952 | tf_op jit(solution)/shard_map/ppermute | solution.py:73
  164.6 32.9 %collective-permute-start.36 = (bf16[2,96,768]{2,1,0:T(8,128)(2,1)}, bf16[2,96,768]{2,1,0:T(8,128)(2,1)S(1)}, u32[]{:S(2)}, u32[]{:S(2)}) collective-permute-start(bf16[2,96,768]{2,1,0:T(8,128)(2,1)} %get-tuple-element.326), channel_id=1, source_target_pairs={{0,2},{1,3},{2,4},{3,5},{4,6},{5,7},{6,0},{7,1},{8,10},{9,11},{10,... | collective-permute-start | bytes 884744 | tf_op jit(solution)/shard_map/ppermute | solution.py:73
  166.4 33.3 %collective-permute-start.37 = (bf16[2,96,768]{2,1,0:T(8,128)(2,1)}, bf16[2,96,768]{2,1,0:T(8,128)(2,1)S(1)}, u32[]{:S(2)}, u32[]{:S(2)}) collective-permute-start(bf16[2,96,768]{2,1,0:T(8,128)(2,1)} %get-tuple-element.327), channel_id=1, source_target_pairs={{0,4},{1,5},{2,6},{3,7},{4,0},{5,1},{6,2},{7,3},{8,12},{9,13},{10,... | collective-permute-start | bytes 884744 | tf_op jit(solution)/shard_map/ppermute | solution.py:73
  167.2 34.5 %collective-permute-start.38 = (bf16[2,96,768]{2,1,0:T(8,128)(2,1)}, bf16[2,96,768]{2,1,0:T(8,128)(2,1)S(1)}, u32[]{:S(2)}, u32[]{:S(2)}) collective-permute-start(bf16[2,96,768]{2,1,0:T(8,128)(2,1)} %get-tuple-element.328), channel_id=1, source_target_pairs={{0,6},{1,7},{2,0},{3,1},{4,2},{5,3},{6,4},{7,5},{8,14},{9,15},{10,... | collective-permute-start | bytes 884744 | tf_op jit(solution)/shard_map/ppermute | solution.py:73
  187.9 21.0 %collective-permute-start.44 = (bf16[2,4,120,768]{3,2,1,0:T(8,128)(2,1)S(1)}, bf16[2,4,120,768]{3,2,1,0:T(8,128)(2,1)S(1)}, u32[]{:S(2)}, u32[]{:S(2)}) collective-permute-start(bf16[2,4,120,768]{3,2,1,0:T(8,128)(2,1)S(1)} %leave.10), channel_id=1, source_target_pairs={{0,16},{1,9},{2,18},{3,11},{4,20},{5,13},{6,22},{7,15},{8,24},{9,1... | collective-permute-start | bytes 4423688 | tf_op jit(solution)/shard_map/ppermute | solution.py:73
  195.7 14.7 %collective-permute-start.41 = (bf16[24,3072]{1,0:T(8,128)(2,1)S(1)}, bf16[24,3072]{1,0:T(8,128)(2,1)S(1)}, u32[]{:S(2)}, u32[]{:S(2)}) collective-permute-start(bf16[24,3072]{1,0:T(8,128)(2,1)S(1)} %get-tuple-element.346), channel_id=1, source_target_pairs={{0,2},{1,3},{2,4},{3,5},{4,6},{5,7},{6,0},{7,1},{8,10},{9,11},{10,... | collective-permute-start | bytes 442376 | tf_op jit(solution)/shard_map/ppermute | solution.py:73
  223.0 14.2 %collective-permute-start.50 = (bf16[2,4,80,768]{3,2,1,0:T(8,128)(2,1)S(1)}, bf16[2,4,80,768]{3,2,1,0:T(8,128)(2,1)S(1)}, u32[]{:S(2)}, u32[]{:S(2)}) collective-permute-start(bf16[2,4,80,768]{3,2,1,0:T(8,128)(2,1)S(1)} %leave.12), channel_id=1, source_target_pairs={{0,16},{1,9},{2,18},{3,11},{4,20},{5,13},{6,22},{7,15},{8,24},{9,1... | collective-permute-start | bytes 2949128 | tf_op jit(solution)/shard_map/ppermute | solution.py:73
  224.2 14.6 %collective-permute-start.47 = (bf16[120,768]{1,0:T(8,128)(2,1)S(1)}, bf16[120,768]{1,0:T(8,128)(2,1)S(1)}, u32[]{:S(2)}, u32[]{:S(2)}) collective-permute-start(bf16[120,768]{1,0:T(8,128)(2,1)S(1)} %get-tuple-element.367), channel_id=1, source_target_pairs={{0,2},{1,3},{2,4},{3,5},{4,6},{5,7},{6,0},{7,1},{8,10},{9,11},{10,... | collective-permute-start | bytes 552968 | tf_op jit(solution)/shard_map/ppermute | solution.py:73
  224.9 15.4 %collective-permute-start.48 = (bf16[120,768]{1,0:T(8,128)(2,1)S(1)}, bf16[120,768]{1,0:T(8,128)(2,1)S(1)}, u32[]{:S(2)}, u32[]{:S(2)}) collective-permute-start(bf16[120,768]{1,0:T(8,128)(2,1)S(1)} %get-tuple-element.368), channel_id=1, source_target_pairs={{0,4},{1,5},{2,6},{3,7},{4,0},{5,1},{6,2},{7,3},{8,12},{9,13},{10,... | collective-permute-start | bytes 552968 | tf_op jit(solution)/shard_map/ppermute | solution.py:73
  (84 other events, 640.5 us)

commit v5 on v4

--- a/solution.py
+++ b/solution.py
@@ -299,7 +299,9 @@
                 num_scalar_prefetch=1, grid=grid, in_specs=in_specs, out_specs=out_specs
             ),
             out_shape=out_shape,
-            compiler_params=pltpu.CompilerParams(vmem_limit_bytes=24 << 20),
+            compiler_params=pltpu.CompilerParams(
+                vmem_limit_bytes=(14 if name == "line" else 8) << 20
+            ),
             cost_estimate=QUICK,
             name=name,
         )
@@ -773,7 +775,7 @@
             pltpu.VMEM((H, keys, rows), F32),
             pltpu.VMEM((H, keys, rows), BF),
         ],
-        compiler_params=pltpu.CompilerParams(vmem_limit_bytes=18 << 20),
+        compiler_params=pltpu.CompilerParams(vmem_limit_bytes=14 << 20),
         cost_estimate=LONG,
         name="cross_back",
     )(dc, co, cq, q2, k2, v2, p2, o2, x1b, memory, dr2, r1, gain, o)
@@ -822,7 +824,7 @@
             pltpu.VMEM((H, rows, rows), F32),
             pltpu.VMEM((H, rows, rows), BF),
         ],
-        compiler_params=pltpu.CompilerParams(vmem_limit_bytes=14 << 20),
+        compiler_params=pltpu.CompilerParams(vmem_limit_bytes=10 << 20),
         cost_estimate=LONG,
         name="self_back",
     )(da, wo, q, k, v, p, x)

time: 262 us -> 259 us (0.989)
    unnamed x107 -> x85, local copies, waits for them, and re-layouts: 7.69 us -> 6.29 us
  transfers between devices with their start and end apart: 55 -> 55, of which waited for: 27 -> 28; matrix products, arithmetic and copies ran while one was open for 7% -> 8% of each run, Pallas kernels for 23% -> 23%
where the time goes in v5:
time: 259 us; the launch traced here: 256 us
  waiting for transfers between devices  89 us (34%)
  Pallas kernels  72.6 us (28%)
  starting transfers between devices  57.6 us (22%)
  matrix products  23.6 us (9%)
  local copies, waits for them, and re-layouts  7.09 us (3%)
  other arithmetic  3.95 us (2%)
    ppermute x55, waiting for transfers between devices, permute(): return lax.ppermute(value, AXES, pairs)  89 us
    ppermute x55, starting transfers between devices, permute(): return lax.ppermute(value, AXES, pairs)  57.6 us
    dot_general x10, matrix products, dot_nn(): return jnp.dot(a, b, preferred_element_type=F32)  15.6 us
    pallas_call x11, Pallas kernels, copy_call(): pl.pallas_call(functools.partial(copy_kernel, plan, len(ins)), grid_spec=...  13.2 us
    pallas_call x1, Pallas kernels, cross_back(): pl.pallas_call(functools.partial(cross_back_kernel, count), out_shape=[sq...  8.64 us
    dot_general x2, matrix products, dot_tn(): lax.dot_general(a, b, (((0,), (0,)), ((), ())), preferred_element_type=F32)  7.93 us
    pallas_call x2, Pallas kernels, attend(): pl.pallas_call(functools.partial(attend_kernel, masked), grid_spec=pltpu....  7.46 us
    pallas_call x7, Pallas kernels, leave(): self.call(functools.partial(leave_kernel, len(self.blocks)), (count,), sp...  6.55 us
  transfers between devices with their start and end apart: 55, of which 28 were waited for; matrix products, arithmetic and copies ran while one was open for 8% of the time, Pallas kernels for 23%

profile of v5, /device:TPU:0, one launch (start us, length us, event | category | flops | bytes accessed | tf_op | source)
XLA Modules:
  0.0 255.6 jit_solution(12828470384731427216)
XLA Ops:
  1.7 5.1 %collective-permute-start.2 = (bf16[104,768]{1,0:T(8,128)(2,1)S(1)}, bf16[104,768]{1,0:T(8,128)(2,1)S(1)}, u32[]{:S(2)}, u32[]{:S(2)}) collective-permute-start(bf16[104,768]{1,0:T(8,128)(2,1)S(1)} %pack_self.1.refs_0_), channel_id=1, source_target_pairs={{0,6},{1,7},{2,0},{3,1},{4,2},{5,3},{6,4},{7,5},{8,14},{9,15},{10,... | collective-permute-start | bytes 479240 | tf_op jit(solution)/shard_map/ppermute | solution.py:73
  8.5 2.9 %collective-permute-done.2.refs_3_ = bf16[104,768]{1,0:T(8,128)(2,1)S(1)} collective-permute-done((bf16[104,768]{1,0:T(8,128)(2,1)S(1)}, bf16[104,768]{1,0:T(8,128)(2,1)S(1)}, u32[]{:S(2)}, u32[]{:S(2)}) %collective-permute-start.2) | collective-permute-done | bytes 159776 | tf_op jit(solution)/shard_map/ppermute | solution.py:73
  11.4 9.0 %collective-permute-done.1.refs_2_ = bf16[104,768]{1,0:T(8,128)(2,1)S(1)} collective-permute-done((bf16[104,768]{1,0:T(8,128)(2,1)S(1)}, bf16[104,768]{1,0:T(8,128)(2,1)S(1)}, u32[]{:S(2)}, u32[]{:S(2)}) %collective-permute-start.1) | collective-permute-done | bytes 159776 | tf_op jit(solution)/shard_map/ppermute | solution.py:73
  30.9 8.9 %collective-permute-done.6.refs_2_ = bf16[96,768]{1,0:T(8,128)(2,1)S(1)} collective-permute-done((bf16[96,768]{1,0:T(8,128)(2,1)S(1)}, bf16[96,768]{1,0:T(8,128)(2,1)S(1)}, u32[]{:S(2)}, u32[]{:S(2)}) %collective-permute-start.6) | collective-permute-done | bytes 147488 | tf_op jit(solution)/shard_map/ppermute | solution.py:73
  45.3 4.2 %collective-permute-done.13.refs_3_ = bf16[24,3072]{1,0:T(8,128)(2,1)S(1)} collective-permute-done((bf16[24,3072]{1,0:T(8,128)(2,1)S(1)}, bf16[24,3072]{1,0:T(8,128)(2,1)S(1)}, u32[]{:S(2)}, u32[]{:S(2)}) %collective-permute-start.13) | collective-permute-done | bytes 147488 | tf_op jit(solution)/shard_map/ppermute | solution.py:73
  51.4 7.3 %collective-permute-done.12.refs_2_ = bf16[24,3072]{1,0:T(8,128)(2,1)S(1)} collective-permute-done((bf16[24,3072]{1,0:T(8,128)(2,1)S(1)}, bf16[24,3072]{1,0:T(8,128)(2,1)S(1)}, u32[]{:S(2)}, u32[]{:S(2)}) %collective-permute-start.12) | collective-permute-done | bytes 147488 | tf_op jit(solution)/shard_map/ppermute | solution.py:73
  58.7 4.3 %collective-permute-done.10.refs_2_ = bf16[4,96,768]{2,1,0:T(8,128)(2,1)S(1)} collective-permute-done((bf16[4,96,768]{2,1,0:T(8,128)(2,1)S(1)}, bf16[4,96,768]{2,1,0:T(8,128)(2,1)S(1)}, u32[]{:S(2)}, u32[]{:S(2)}) %collective-permute-start.10) | collective-permute-done | bytes 589856 | tf_op jit(solution)/shard_map/ppermute | solution.py:73
  76.2 3.8 %attend.2 = (bf16[512,768]{1,0:T(8,128)(2,1)S(1)}, bf16[2,12,256,256]{3,2,1,0:T(8,128)(2,1)S(1)}) custom-call(s32[2]{0:T(128)S(1)} %copy-done.10, s32[2]{0:T(128)S(1)} %copy-done.11, bf16[512,768]{1,0:T(8,128)(2,1)S(1)} %fusion.12.q_ref, bf16[512,768]{1,0:T(8,128)(2,1)S(1)} %fusion.15.k_ref, bf16[512,768]{1,0:T(8,128)(2,1)S(1)} %fusion.13.v_ref), custom_call_target="tpu_custom_call" | custom-call | flops 1000 | bytes 1000 | tf_op jit(solution)/shard_map/attend/pallas_call | solution.py:558
  83.3 5.7 %collective-permute-done.14.refs_3_ = bf16[4,96,768]{2,1,0:T(8,128)(2,1)S(1)} collective-permute-done((bf16[4,96,768]{2,1,0:T(8,128)(2,1)S(1)}, bf16[4,96,768]{2,1,0:T(8,128)(2,1)S(1)}, u32[]{:S(2)}, u32[]{:S(2)}) %collective-permute-start.14) | collective-permute-done | bytes 589856 | tf_op jit(solution)/shard_map/ppermute | solution.py:73
  100.8 3.6 %attend.3 = (bf16[512,768]{1,0:T(8,128)(2,1)S(1)}, bf16[2,12,256,256]{3,2,1,0:T(8,128)(2,1)S(1)}) custom-call(s32[2]{0:T(128)S(1)} %copy-done.10, s32[2]{0:T(128)S(1)} %copy-done.11, bf16[512,768]{1,0:T(8,128)(2,1)S(1)} %multiply_convert_fusion.1.q_ref, bf16[512,768]{1,0:T(8,128)(2,1)S(1)} %fusion.16.k_ref, bf16[512,768]{1,0:T(8,128)(2,1)S(1)} %fusion.14.v_ref), custom_call_target="tpu_custom_call" | custom-call | flops 1000 | bytes 1000 | tf_op jit(solution)/shard_map/attend/pallas_call | solution.py:558
  108.4 5.5 %collective-permute-done.21.refs_3_ = bf16[4,24,3072]{2,1,0:T(8,128)(2,1)S(1)} collective-permute-done((bf16[4,24,3072]{2,1,0:T(8,128)(2,1)S(1)}, bf16[4,24,3072]{2,1,0:T(8,128)(2,1)S(1)}, u32[]{:S(2)}, u32[]{:S(2)}) %collective-permute-start.21) | collective-permute-done | bytes 589856 | tf_op jit(solution)/shard_map/ppermute | solution.py:73
  120.8 6.3 %fusion.4 = (bf16[512,3072]{1,0:T(8,128)(2,1)S(1)}, bf16[512,3072]{1,0:T(8,128)(2,1)S(1)}) fusion(f32[3072]{0:T(1024)S(1)} %bitcast.195, bf16[768,3072]{1,0:T(8,128)(2,1)S(1)} %bitcast.166, f32[512,768]{1,0:T(8,128)S(1)} %get-tuple-element.420.r2_ref, f32[768]{0:T(1024)S(1)} %get-tuple-element.401, f32[768]{0:T(1024)S(1)} %get-tuple-element.398, ...), kind=kOutput, calls=%fused_computation.5 | convolution fusion | flops 2436759552 | bytes 12605440 | tf_op jit(solution)/shard_map/dot_general | solution.py:515
  136.5 2.9 %convolution_convert_fusion.1 = bf16[3072,768]{1,0:T(8,128)(2,1)S(1)} fusion(bf16[512,3072]{1,0:T(8,128)(2,1)S(1)} %copy-done.41, bf16[512,768]{1,0:T(8,128)(2,1)S(1)} %get-tuple-element.300.df_ref), kind=kOutput, calls=%fused_computation.9 | convolution fusion | flops 2418278400 | bytes 8650752 | tf_op jit(solution)/shard_map/dot_general | solution.py:519
  140.8 3.9 %hidden_back.1 = (bf16[512,3072]{1,0:T(8,128)(2,1)S(1)}, f32[1,3072]{1,0:T(1,128)S(1)}) custom-call(bf16[512,768]{1,0:T(8,128)(2,1)S(1)} %get-tuple-element.300.df_ref, bf16[3072,768]{1,0:T(8,128)(2,1)S(1)} %bitcast.169, bf16[512,3072]{1,0:T(8,128)(2,1)S(1)} %get-tuple-element.412.slope_ref), custom_call_target="tpu_custom_call" | custom-call | flops 40000000000 | bytes 1000000 | tf_op jit(solution)/shard_map/hidden_back/pallas_call | solution.py:614
  146.9 5.0 %convolution_convert_fusion = bf16[768,3072]{1,0:T(8,128)(2,1)S(1)} fusion(bf16[512,3072]{1,0:T(8,128)(2,1)} %copy-done.35, f32[512,768]{1,0:T(8,128)S(1)} %get-tuple-element.420.r2_ref, f32[768]{0:T(1024)S(1)} %get-tuple-element.401, f32[768]{0:T(1024)S(1)} %get-tuple-element.398, f32[512]{0:T(512)S(1)} %add_rsqrt_fusion.1, f32[512]{0:T(512)S(1)} %broadcast_multiply_fusion.2), kind=kOutput, calls=%fused_computation.8 | convolution fusion | flops 2420244480 | bytes 9447424 | tf_op jit(solution)/shard_map/dot_general | solution.py:519
  153.8 5.1 %expand_back.1 = (f32[512,768]{1,0:T(8,128)S(1)}, bf16[512,768]{1,0:T(8,128)(2,1)S(1)}, f32[8,768]{1,0:T(8,128)S(1)}) custom-call(bf16[512,3072]{1,0:T(8,128)(2,1)S(1)} %copy-done.36, bf16[768,3072]{1,0:T(8,128)(2,1)S(1)} %bitcast.167, f32[512,768]{1,0:T(8,128)S(1)} %get-tuple-element.411.dr3_ref, f32[512,768]{1,0:T(8,128)S(1)} %get-tuple-element.420.r2_ref, ...), custom_call_target="tpu_custom_call" | custom-call | flops 40000000000 | bytes 1000000 | tf_op jit(solution)/shard_map/expand_back/pallas_call | solution.py:660
  168.3 8.6 %cross_back.1 = (bf16[768,768]{1,0:T(8,128)(2,1)S(1)}, bf16[768,768]{1,0:T(8,128)(2,1)S(1)}, bf16[768,768]{1,0:T(8,128)(2,1)S(1)}, bf16[768,768]{1,0:T(8,128)(2,...) custom-call(bf16[512,768]{1,0:T(8,128)(2,1)S(1)} %get-tuple-element., ...), custom_call_target="tpu_custom_call" | custom-call | flops 40000000000 | bytes 1000000 | tf_op jit(solution)/shard_map/cross_back/pallas_call | solution.py:762
  185.6 6.2 %self_back.1 = (bf16[768,768]{1,0:T(8,128)(2,1)S(1)}, bf16[768,768]{1,0:T(8,128)(2,1)S(1)}, bf16[768,768]{1,0:T(8,128)(2,1)S(1)}, bf16[512,768]{1,0:T(8,128)(2,1...) custom-call(bf16[512,768]{1,0:T(8,128)(2,1)S(1)} %get-tuple-element.321.da_ref, ...), custom_call_target="tpu_custom_call" | custom-call | flops 40000000000 | bytes 1000000 | tf_op jit(solution)/shard_map/self_back/pallas_call | solution.py:819
  202.2 3.8 %collective-permute-done.44.refs_6_.refs_14_.refs_22_.refs_30_ = bf16[2,4,120,768]{3,2,1,0:T(8,128)(2,1)S(1)} collective-permute-done((bf16[2,4,120,768]{3,2,1,0:T(8,128)(2,1)S(1)}, bf16[2,4,120,768]{3,2,1,0:T(8,128)(2,1)S(1)}, u32[]{:S(2)}, u32[]{:S(2)}) %collective-permute-start.44) | collective-permute-done | bytes 1474592 | tf_op jit(solution)/shard_map/ppermute | solution.py:73
  210.0 3.2 %rows_back.3 = f32[512,768]{1,0:T(8,128)} custom-call(bf16[512,768]{1,0:T(8,128)(2,1)S(1)} %get-tuple-element.358.refs_0_, bf16[512,768]{1,0:T(8,128)(2,1)S(1)} %get-tuple-element.359.refs_1_, bf16[512,768]{1,0:T(8,128)(2,1)S(1)} %get-tuple-element.360.refs_2_, bf16[768,768]{1,0:T(8,128)(2,1)S(1)} %bitcast.172, bf16[768,768]{1,0:T(8,128)(2,1)S(1)} %bitcast.174, ...), custom_call_target="tpu_custom_call" | custom-call | flops 40000000000 | bytes 1000000 | tf_op jit(solution)/shard_map/rows_back/pallas_call | solution.py:842
  213.2 5.9 %collective-permute-done.45.refs_7_.refs_15_.refs_23_.refs_31_ = bf16[1,4,120,768]{3,2,1,0:T(8,128)(2,1)S(1)} collective-permute-done((bf16[1,4,120,768]{3,2,1,0:T(8,128)(2,1)S(1)}, bf16[1,4,120,768]{3,2,1,0:T(8,128)(2,1)S(1)}, u32[]{:S(2)}, u32[]{:S(2)}) %collective-permute-start.45) | collective-permute-done | bytes 737312 | tf_op jit(solution)/shard_map/ppermute | solution.py:73
  227.1 7.1 %collective-permute-done.50.refs_5_.refs_12_.refs_19_.refs_26_ = bf16[2,4,80,768]{3,2,1,0:T(8,128)(2,1)S(1)} collective-permute-done((bf16[2,4,80,768]{3,2,1,0:T(8,128)(2,1)S(1)}, bf16[2,4,80,768]{3,2,1,0:T(8,128)(2,1)S(1)}, u32[]{:S(2)}, u32[]{:S(2)}) %collective-permute-start.50) | collective-permute-done | bytes 983072 | tf_op jit(solution)/shard_map/ppermute | solution.py:73
  239.3 4.6 %collective-permute-done.51.refs_6_.refs_13_.refs_20_.refs_27_ = bf16[1,4,80,768]{3,2,1,0:T(8,128)(2,1)S(1)} collective-permute-done((bf16[1,4,80,768]{3,2,1,0:T(8,128)(2,1)S(1)}, bf16[1,4,80,768]{3,2,1,0:T(8,128)(2,1)S(1)}, u32[]{:S(2)}, u32[]{:S(2)}) %collective-permute-start.51) | collective-permute-done | bytes 491552 | tf_op jit(solution)/shard_map/ppermute | solution.py:73
  249.0 3.1 %collective-permute-done.52.refs_1_ = bf16[80,768]{1,0:T(8,128)(2,1)S(1)} collective-permute-done((bf16[80,768]{1,0:T(8,128)(2,1)S(1)}, bf16[80,768]{1,0:T(8,128)(2,1)S(1)}, u32[]{:S(2)}, u32[]{:S(2)}) %collective-permute-start.52) | collective-permute-done | bytes 122912 | tf_op jit(solution)/shard_map/ppermute | solution.py:73
  (246 shorter events, 127.7 us)
Async XLA Ops:
  21.8 18.1 %collective-permute-start.4 = (bf16[4,104,768]{2,1,0:T(8,128)(2,1)S(1)}, bf16[4,104,768]{2,1,0:T(8,128)(2,1)S(1)}, u32[]{:S(2)}, u32[]{:S(2)}) collective-permute-start(bf16[4,104,768]{2,1,0:T(8,128)(2,1)S(1)} %column.4.refs_0_), channel_id=1, source_target_pairs={{0,8},{1,17},{2,10},{3,19},{4,12},{5,21},{6,14},{7,23},{8,0},{9,25... | collective-permute-start | bytes 1916936 | tf_op jit(solution)/shard_map/ppermute | solution.py:73
  23.3 16.6 %collective-permute-start.3 = (bf16[4,104,768]{2,1,0:T(8,128)(2,1)S(1)}, bf16[4,104,768]{2,1,0:T(8,128)(2,1)S(1)}, u32[]{:S(2)}, u32[]{:S(2)}) collective-permute-start(bf16[4,104,768]{2,1,0:T(8,128)(2,1)S(1)} %column.4.refs_0_), channel_id=1, source_target_pairs={{0,16},{1,9},{2,18},{3,11},{4,20},{5,13},{6,22},{7,15},{8,24},{9,1... | collective-permute-start | bytes 1916936 | tf_op jit(solution)/shard_map/ppermute | solution.py:73
  39.9 23.1 %collective-permute-start.8 = (bf16[4,104,768]{2,1,0:T(8,128)(2,1)S(1)}, bf16[4,104,768]{2,1,0:T(8,128)(2,1)S(1)}, u32[]{:S(2)}, u32[]{:S(2)}) collective-permute-start(bf16[4,104,768]{2,1,0:T(8,128)(2,1)S(1)} %collective-permute-done.3.refs_1_), channel_id=1, source_target_pairs={{0,8},{1,17},{2,10},{3,19},{4,12},{5,21},{6,14},{7,23},{8,0},{9,25... | collective-permute-start | bytes 1916936 | tf_op jit(solution)/shard_map/ppermute | solution.py:73
  41.8 21.2 %collective-permute-start.10 = (bf16[4,96,768]{2,1,0:T(8,128)(2,1)S(1)}, bf16[4,96,768]{2,1,0:T(8,128)(2,1)S(1)}, u32[]{:S(2)}, u32[]{:S(2)}) collective-permute-start(bf16[4,96,768]{2,1,0:T(8,128)(2,1)S(1)} %column.5.refs_0_), channel_id=1, source_target_pairs={{0,8},{1,17},{2,10},{3,19},{4,12},{5,21},{6,14},{7,23},{8,0},{9,25... | collective-permute-start | bytes 1769480 | tf_op jit(solution)/shard_map/ppermute | solution.py:73
  43.4 19.6 %collective-permute-start.9 = (bf16[4,96,768]{2,1,0:T(8,128)(2,1)S(1)}, bf16[4,96,768]{2,1,0:T(8,128)(2,1)S(1)}, u32[]{:S(2)}, u32[]{:S(2)}) collective-permute-start(bf16[4,96,768]{2,1,0:T(8,128)(2,1)S(1)} %column.5.refs_0_), channel_id=1, source_target_pairs={{0,16},{1,9},{2,18},{3,11},{4,20},{5,13},{6,22},{7,15},{8,24},{9,1... | collective-permute-start | bytes 1769480 | tf_op jit(solution)/shard_map/ppermute | solution.py:73
  43.9 14.8 %collective-permute-start.12 = (bf16[24,3072]{1,0:T(8,128)(2,1)S(1)}, bf16[24,3072]{1,0:T(8,128)(2,1)S(1)}, u32[]{:S(2)}, u32[]{:S(2)}) collective-permute-start(bf16[24,3072]{1,0:T(8,128)(2,1)S(1)} %copy-done.8), channel_id=1, source_target_pairs={{0,4},{1,5},{2,6},{3,7},{4,0},{5,1},{6,2},{7,3},{8,12},{9,13},{10,... | collective-permute-start | bytes 442376 | tf_op jit(solution)/shard_map/ppermute | solution.py:73
  65.9 15.8 %collective-permute-start.18 = (bf16[96,768]{1,0:T(8,128)(2,1)S(1)}, bf16[96,768]{1,0:T(8,128)(2,1)S(1)}, u32[]{:S(2)}, u32[]{:S(2)}) collective-permute-start(bf16[96,768]{1,0:T(8,128)(2,1)S(1)} %copy-done.9), channel_id=1, source_target_pairs={{0,4},{1,5},{2,6},{3,7},{4,0},{5,1},{6,2},{7,3},{8,12},{9,13},{10,... | collective-permute-start | bytes 442376 | tf_op jit(solution)/shard_map/ppermute | solution.py:73
  67.4 15.9 %collective-permute-start.15 = (bf16[4,24,3072]{2,1,0:T(8,128)(2,1)S(1)}, bf16[4,24,3072]{2,1,0:T(8,128)(2,1)S(1)}, u32[]{:S(2)}, u32[]{:S(2)}) collective-permute-start(bf16[4,24,3072]{2,1,0:T(8,128)(2,1)S(1)} %column.6.refs_0_), channel_id=1, source_target_pairs={{0,16},{1,9},{2,18},{3,11},{4,20},{5,13},{6,22},{7,15},{8,24},{9,1... | collective-permute-start | bytes 1769480 | tf_op jit(solution)/shard_map/ppermute | solution.py:73
  67.9 14.8 %collective-permute-start.16 = (bf16[4,24,3072]{2,1,0:T(8,128)(2,1)S(1)}, bf16[4,24,3072]{2,1,0:T(8,128)(2,1)S(1)}, u32[]{:S(2)}, u32[]{:S(2)}) collective-permute-start(bf16[4,24,3072]{2,1,0:T(8,128)(2,1)S(1)} %column.6.refs_0_), channel_id=1, source_target_pairs={{0,8},{1,17},{2,10},{3,19},{4,12},{5,21},{6,14},{7,23},{8,0},{9,25... | collective-permute-start | bytes 1769480 | tf_op jit(solution)/shard_map/ppermute | solution.py:73
  70.6 18.4 %collective-permute-start.14 = (bf16[4,96,768]{2,1,0:T(8,128)(2,1)S(1)}, bf16[4,96,768]{2,1,0:T(8,128)(2,1)S(1)}, u32[]{:S(2)}, u32[]{:S(2)}) collective-permute-start(bf16[4,96,768]{2,1,0:T(8,128)(2,1)S(1)} %collective-permute-done.9.refs_1_), channel_id=1, source_target_pairs={{0,8},{1,17},{2,10},{3,19},{4,12},{5,21},{6,14},{7,23},{8,0},{9,25... | collective-permute-start | bytes 1769480 | tf_op jit(solution)/shard_map/ppermute | solution.py:73
  92.2 16.2 %collective-permute-start.22 = (bf16[4,96,768]{2,1,0:T(8,128)(2,1)S(1)}, bf16[4,96,768]{2,1,0:T(8,128)(2,1)S(1)}, u32[]{:S(2)}, u32[]{:S(2)}) collective-permute-start(bf16[4,96,768]{2,1,0:T(8,128)(2,1)S(1)} %column.7.refs_0_), channel_id=1, source_target_pairs={{0,16},{1,9},{2,18},{3,11},{4,20},{5,13},{6,22},{7,15},{8,24},{9,1... | collective-permute-start | bytes 1769480 | tf_op jit(solution)/shard_map/ppermute | solution.py:73
  92.7 14.8 %collective-permute-start.23 = (bf16[4,96,768]{2,1,0:T(8,128)(2,1)S(1)}, bf16[4,96,768]{2,1,0:T(8,128)(2,1)S(1)}, u32[]{:S(2)}, u32[]{:S(2)}) collective-permute-start(bf16[4,96,768]{2,1,0:T(8,128)(2,1)S(1)} %column.7.refs_0_), channel_id=1, source_target_pairs={{0,8},{1,17},{2,10},{3,19},{4,12},{5,21},{6,14},{7,23},{8,0},{9,25... | collective-permute-start | bytes 1769480 | tf_op jit(solution)/shard_map/ppermute | solution.py:73
  93.6 20.2 %collective-permute-start.21 = (bf16[4,24,3072]{2,1,0:T(8,128)(2,1)S(1)}, bf16[4,24,3072]{2,1,0:T(8,128)(2,1)S(1)}, u32[]{:S(2)}, u32[]{:S(2)}) collective-permute-start(bf16[4,24,3072]{2,1,0:T(8,128)(2,1)S(1)} %collective-permute-done.15.refs_1_), channel_id=1, source_target_pairs={{0,8},{1,17},{2,10},{3,19},{4,12},{5,21},{6,14},{7,23},{8,0},{9,25... | collective-permute-start | bytes 1769480 | tf_op jit(solution)/shard_map/ppermute | solution.py:73
  146.4 16.2 %collective-permute-start.32 = (bf16[2,4,96,768]{3,2,1,0:T(8,128)(2,1)S(1)}, bf16[2,4,96,768]{3,2,1,0:T(8,128)(2,1)S(1)}, u32[]{:S(2)}, u32[]{:S(2)}) collective-permute-start(bf16[2,4,96,768]{3,2,1,0:T(8,128)(2,1)S(1)} %leave.7), channel_id=1, source_target_pairs={{0,16},{1,9},{2,18},{3,11},{4,20},{5,13},{6,22},{7,15},{8,24},{9,1... | collective-permute-start | bytes 3538952 | tf_op jit(solution)/shard_map/ppermute | solution.py:73
  160.0 18.4 %collective-permute-start.34 = (bf16[2,4,24,3072]{3,2,1,0:T(8,128)(2,1)S(1)}, bf16[2,4,24,3072]{3,2,1,0:T(8,128)(2,1)S(1)}, u32[]{:S(2)}, u32[]{:S(2)}) collective-permute-start(bf16[2,4,24,3072]{3,2,1,0:T(8,128)(2,1)S(1)} %leave.8), channel_id=1, source_target_pairs={{0,16},{1,9},{2,18},{3,11},{4,20},{5,13},{6,22},{7,15},{8,24},{9,1... | collective-permute-start | bytes 3538952 | tf_op jit(solution)/shard_map/ppermute | solution.py:73
  163.6 30.8 %collective-permute-start.36 = (bf16[2,96,768]{2,1,0:T(8,128)(2,1)S(1)}, bf16[2,96,768]{2,1,0:T(8,128)(2,1)S(1)}, u32[]{:S(2)}, u32[]{:S(2)}) collective-permute-start(bf16[2,96,768]{2,1,0:T(8,128)(2,1)S(1)} %get-tuple-element.326), channel_id=1, source_target_pairs={{0,2},{1,3},{2,4},{3,5},{4,6},{5,7},{6,0},{7,1},{8,10},{9,11},{10,... | collective-permute-start | bytes 884744 | tf_op jit(solution)/shard_map/ppermute | solution.py:73
  165.4 31.2 %collective-permute-start.37 = (bf16[2,96,768]{2,1,0:T(8,128)(2,1)S(1)}, bf16[2,96,768]{2,1,0:T(8,128)(2,1)S(1)}, u32[]{:S(2)}, u32[]{:S(2)}) collective-permute-start(bf16[2,96,768]{2,1,0:T(8,128)(2,1)S(1)} %get-tuple-element.327), channel_id=1, source_target_pairs={{0,4},{1,5},{2,6},{3,7},{4,0},{5,1},{6,2},{7,3},{8,12},{9,13},{10,... | collective-permute-start | bytes 884744 | tf_op jit(solution)/shard_map/ppermute | solution.py:73
  166.3 32.3 %collective-permute-start.38 = (bf16[2,96,768]{2,1,0:T(8,128)(2,1)S(1)}, bf16[2,96,768]{2,1,0:T(8,128)(2,1)S(1)}, u32[]{:S(2)}, u32[]{:S(2)}) collective-permute-start(bf16[2,96,768]{2,1,0:T(8,128)(2,1)S(1)} %get-tuple-element.328), channel_id=1, source_target_pairs={{0,6},{1,7},{2,0},{3,1},{4,2},{5,3},{6,4},{7,5},{8,14},{9,15},{10,... | collective-permute-start | bytes 884744 | tf_op jit(solution)/shard_map/ppermute | solution.py:73
  185.0 21.0 %collective-permute-start.44 = (bf16[2,4,120,768]{3,2,1,0:T(8,128)(2,1)S(1)}, bf16[2,4,120,768]{3,2,1,0:T(8,128)(2,1)S(1)}, u32[]{:S(2)}, u32[]{:S(2)}) collective-permute-start(bf16[2,4,120,768]{3,2,1,0:T(8,128)(2,1)S(1)} %leave.10), channel_id=1, source_target_pairs={{0,16},{1,9},{2,18},{3,11},{4,20},{5,13},{6,22},{7,15},{8,24},{9,1... | collective-permute-start | bytes 4423688 | tf_op jit(solution)/shard_map/ppermute | solution.py:73
  192.7 14.8 %collective-permute-start.41 = (bf16[24,3072]{1,0:T(8,128)(2,1)S(1)}, bf16[24,3072]{1,0:T(8,128)(2,1)S(1)}, u32[]{:S(2)}, u32[]{:S(2)}) collective-permute-start(bf16[24,3072]{1,0:T(8,128)(2,1)S(1)} %get-tuple-element.346), channel_id=1, source_target_pairs={{0,2},{1,3},{2,4},{3,5},{4,6},{5,7},{6,0},{7,1},{8,10},{9,11},{10,... | collective-permute-start | bytes 442376 | tf_op jit(solution)/shard_map/ppermute | solution.py:73
  194.4 14.0 %collective-permute-start.42 = (bf16[24,3072]{1,0:T(8,128)(2,1)S(1)}, bf16[24,3072]{1,0:T(8,128)(2,1)S(1)}, u32[]{:S(2)}, u32[]{:S(2)}) collective-permute-start(bf16[24,3072]{1,0:T(8,128)(2,1)S(1)} %get-tuple-element.347), channel_id=1, source_target_pairs={{0,4},{1,5},{2,6},{3,7},{4,0},{5,1},{6,2},{7,3},{8,12},{9,13},{10,... | collective-permute-start | bytes 442376 | tf_op jit(solution)/shard_map/ppermute | solution.py:73
  220.1 14.2 %collective-permute-start.50 = (bf16[2,4,80,768]{3,2,1,0:T(8,128)(2,1)S(1)}, bf16[2,4,80,768]{3,2,1,0:T(8,128)(2,1)S(1)}, u32[]{:S(2)}, u32[]{:S(2)}) collective-permute-start(bf16[2,4,80,768]{3,2,1,0:T(8,128)(2,1)S(1)} %leave.12), channel_id=1, source_target_pairs={{0,16},{1,9},{2,18},{3,11},{4,20},{5,13},{6,22},{7,15},{8,24},{9,1... | collective-permute-start | bytes 2949128 | tf_op jit(solution)/shard_map/ppermute | solution.py:73
  221.5 14.4 %collective-permute-start.47 = (bf16[120,768]{1,0:T(8,128)(2,1)S(1)}, bf16[120,768]{1,0:T(8,128)(2,1)S(1)}, u32[]{:S(2)}, u32[]{:S(2)}) collective-permute-start(bf16[120,768]{1,0:T(8,128)(2,1)S(1)} %get-tuple-element.367), channel_id=1, source_target_pairs={{0,2},{1,3},{2,4},{3,5},{4,6},{5,7},{6,0},{7,1},{8,10},{9,11},{10,... | collective-permute-start | bytes 552968 | tf_op jit(solution)/shard_map/ppermute | solution.py:73
  222.0 15.4 %collective-permute-start.48 = (bf16[120,768]{1,0:T(8,128)(2,1)S(1)}, bf16[120,768]{1,0:T(8,128)(2,1)S(1)}, u32[]{:S(2)}, u32[]{:S(2)}) collective-permute-start(bf16[120,768]{1,0:T(8,128)(2,1)S(1)} %get-tuple-element.368), channel_id=1, source_target_pairs={{0,4},{1,5},{2,6},{3,7},{4,0},{5,1},{6,2},{7,3},{8,12},{9,13},{10,... | collective-permute-start | bytes 552968 | tf_op jit(solution)/shard_map/ppermute | solution.py:73
  (73 other events, 554.4 us)

commit v6 on v5

--- a/solution.py
+++ b/solution.py
@@ -1058,9 +1058,9 @@
         line = g_expand.column()
         g_expand.hop(0, 0)
         g_expand.hop(1, 0)
-        g_contract = Gather(place, after(contract_weight, line))
         g_self.half(line)
         *w_self, smalls = g_self.spread(four + [(4 * rows, 8)])
+        g_contract = Gather(place, after(contract_weight, smalls))
         smalls = smalls.reshape(-1, 8, D)
     else:
         whole = lax.all_gather(

time: 259 us -> 259 us (level)
  no operation moved by 1% of the time
where the time goes in v6:
time: 259 us; the launch traced here: 256 us
  waiting for transfers between devices  89 us (34%)
  Pallas kernels  72.6 us (28%)
  starting transfers between devices  57.6 us (22%)
  matrix products  23.6 us (9%)
  local copies, waits for them, and re-layouts  7.09 us (3%)
  other arithmetic  3.95 us (2%)
    ppermute x55, waiting for transfers between devices, permute(): return lax.ppermute(value, AXES, pairs)  89 us
    ppermute x55, starting transfers between devices, permute(): return lax.ppermute(value, AXES, pairs)  57.6 us
    dot_general x10, matrix products, dot_nn(): return jnp.dot(a, b, preferred_element_type=F32)  15.6 us
    pallas_call x11, Pallas kernels, copy_call(): pl.pallas_call(functools.partial(copy_kernel, plan, len(ins)), grid_spec=...  13.2 us
    pallas_call x1, Pallas kernels, cross_back(): pl.pallas_call(functools.partial(cross_back_kernel, count), out_shape=[sq...  8.64 us
    dot_general x2, matrix products, dot_tn(): lax.dot_general(a, b, (((0,), (0,)), ((), ())), preferred_element_type=F32)  7.93 us
    pallas_call x2, Pallas kernels, attend(): pl.pallas_call(functools.partial(attend_kernel, masked), grid_spec=pltpu....  7.46 us
    pallas_call x7, Pallas kernels, leave(): self.call(functools.partial(leave_kernel, len(self.blocks)), (count,), sp...  6.55 us
  transfers between devices with their start and end apart: 55, of which 28 were waited for; matrix products, arithmetic and copies ran while one was open for 8% of the time, Pallas kernels for 23%

profile of v6, /device:TPU:0, one launch (start us, length us, event | category | flops | bytes accessed | tf_op | source)
XLA Modules:
  0.0 255.6 jit_solution(12828470384731427216)
XLA Ops:
  1.7 5.1 %collective-permute-start.2 = (bf16[104,768]{1,0:T(8,128)(2,1)S(1)}, bf16[104,768]{1,0:T(8,128)(2,1)S(1)}, u32[]{:S(2)}, u32[]{:S(2)}) collective-permute-start(bf16[104,768]{1,0:T(8,128)(2,1)S(1)} %pack_self.1.refs_0_), channel_id=1, source_target_pairs={{0,6},{1,7},{2,0},{3,1},{4,2},{5,3},{6,4},{7,5},{8,14},{9,15},{10,... | collective-permute-start | bytes 479240 | tf_op jit(solution)/shard_map/ppermute | solution.py:73
  8.5 2.9 %collective-permute-done.2.refs_3_ = bf16[104,768]{1,0:T(8,128)(2,1)S(1)} collective-permute-done((bf16[104,768]{1,0:T(8,128)(2,1)S(1)}, bf16[104,768]{1,0:T(8,128)(2,1)S(1)}, u32[]{:S(2)}, u32[]{:S(2)}) %collective-permute-start.2) | collective-permute-done | bytes 159776 | tf_op jit(solution)/shard_map/ppermute | solution.py:73
  11.4 9.0 %collective-permute-done.1.refs_2_ = bf16[104,768]{1,0:T(8,128)(2,1)S(1)} collective-permute-done((bf16[104,768]{1,0:T(8,128)(2,1)S(1)}, bf16[104,768]{1,0:T(8,128)(2,1)S(1)}, u32[]{:S(2)}, u32[]{:S(2)}) %collective-permute-start.1) | collective-permute-done | bytes 159776 | tf_op jit(solution)/shard_map/ppermute | solution.py:73
  30.9 8.9 %collective-permute-done.6.refs_2_ = bf16[96,768]{1,0:T(8,128)(2,1)S(1)} collective-permute-done((bf16[96,768]{1,0:T(8,128)(2,1)S(1)}, bf16[96,768]{1,0:T(8,128)(2,1)S(1)}, u32[]{:S(2)}, u32[]{:S(2)}) %collective-permute-start.6) | collective-permute-done | bytes 147488 | tf_op jit(solution)/shard_map/ppermute | solution.py:73
  45.3 4.2 %collective-permute-done.13.refs_3_ = bf16[24,3072]{1,0:T(8,128)(2,1)S(1)} collective-permute-done((bf16[24,3072]{1,0:T(8,128)(2,1)S(1)}, bf16[24,3072]{1,0:T(8,128)(2,1)S(1)}, u32[]{:S(2)}, u32[]{:S(2)}) %collective-permute-start.13) | collective-permute-done | bytes 147488 | tf_op jit(solution)/shard_map/ppermute | solution.py:73
  51.4 7.3 %collective-permute-done.12.refs_2_ = bf16[24,3072]{1,0:T(8,128)(2,1)S(1)} collective-permute-done((bf16[24,3072]{1,0:T(8,128)(2,1)S(1)}, bf16[24,3072]{1,0:T(8,128)(2,1)S(1)}, u32[]{:S(2)}, u32[]{:S(2)}) %collective-permute-start.12) | collective-permute-done | bytes 147488 | tf_op jit(solution)/shard_map/ppermute | solution.py:73
  58.7 4.3 %collective-permute-done.10.refs_2_ = bf16[4,96,768]{2,1,0:T(8,128)(2,1)S(1)} collective-permute-done((bf16[4,96,768]{2,1,0:T(8,128)(2,1)S(1)}, bf16[4,96,768]{2,1,0:T(8,128)(2,1)S(1)}, u32[]{:S(2)}, u32[]{:S(2)}) %collective-permute-start.10) | collective-permute-done | bytes 589856 | tf_op jit(solution)/shard_map/ppermute | solution.py:73
  76.2 3.8 %attend.2 = (bf16[512,768]{1,0:T(8,128)(2,1)S(1)}, bf16[2,12,256,256]{3,2,1,0:T(8,128)(2,1)S(1)}) custom-call(s32[2]{0:T(128)S(1)} %copy-done.10, s32[2]{0:T(128)S(1)} %copy-done.11, bf16[512,768]{1,0:T(8,128)(2,1)S(1)} %fusion.12.q_ref, bf16[512,768]{1,0:T(8,128)(2,1)S(1)} %fusion.15.k_ref, bf16[512,768]{1,0:T(8,128)(2,1)S(1)} %fusion.13.v_ref), custom_call_target="tpu_custom_call" | custom-call | flops 1000 | bytes 1000 | tf_op jit(solution)/shard_map/attend/pallas_call | solution.py:558
  83.3 5.7 %collective-permute-done.14.refs_3_ = bf16[4,96,768]{2,1,0:T(8,128)(2,1)S(1)} collective-permute-done((bf16[4,96,768]{2,1,0:T(8,128)(2,1)S(1)}, bf16[4,96,768]{2,1,0:T(8,128)(2,1)S(1)}, u32[]{:S(2)}, u32[]{:S(2)}) %collective-permute-start.14) | collective-permute-done | bytes 589856 | tf_op jit(solution)/shard_map/ppermute | solution.py:73
  100.8 3.6 %attend.3 = (bf16[512,768]{1,0:T(8,128)(2,1)S(1)}, bf16[2,12,256,256]{3,2,1,0:T(8,128)(2,1)S(1)}) custom-call(s32[2]{0:T(128)S(1)} %copy-done.10, s32[2]{0:T(128)S(1)} %copy-done.11, bf16[512,768]{1,0:T(8,128)(2,1)S(1)} %multiply_convert_fusion.1.q_ref, bf16[512,768]{1,0:T(8,128)(2,1)S(1)} %fusion.16.k_ref, bf16[512,768]{1,0:T(8,128)(2,1)S(1)} %fusion.14.v_ref), custom_call_target="tpu_custom_call" | custom-call | flops 1000 | bytes 1000 | tf_op jit(solution)/shard_map/attend/pallas_call | solution.py:558
  108.4 5.5 %collective-permute-done.21.refs_3_ = bf16[4,24,3072]{2,1,0:T(8,128)(2,1)S(1)} collective-permute-done((bf16[4,24,3072]{2,1,0:T(8,128)(2,1)S(1)}, bf16[4,24,3072]{2,1,0:T(8,128)(2,1)S(1)}, u32[]{:S(2)}, u32[]{:S(2)}) %collective-permute-start.21) | collective-permute-done | bytes 589856 | tf_op jit(solution)/shard_map/ppermute | solution.py:73
  120.8 6.3 %fusion.4 = (bf16[512,3072]{1,0:T(8,128)(2,1)S(1)}, bf16[512,3072]{1,0:T(8,128)(2,1)S(1)}) fusion(f32[3072]{0:T(1024)S(1)} %bitcast.195, bf16[768,3072]{1,0:T(8,128)(2,1)S(1)} %bitcast.166, f32[512,768]{1,0:T(8,128)S(1)} %get-tuple-element.418.r2_ref, f32[768]{0:T(1024)S(1)} %get-tuple-element.399, f32[768]{0:T(1024)S(1)} %get-tuple-element.396, ...), kind=kOutput, calls=%fused_computation.5 | convolution fusion | flops 2436759552 | bytes 12605440 | tf_op jit(solution)/shard_map/dot_general | solution.py:515
  136.5 2.9 %convolution_convert_fusion.1 = bf16[3072,768]{1,0:T(8,128)(2,1)S(1)} fusion(bf16[512,3072]{1,0:T(8,128)(2,1)S(1)} %copy-done.41, bf16[512,768]{1,0:T(8,128)(2,1)S(1)} %get-tuple-element.298.df_ref), kind=kOutput, calls=%fused_computation.9 | convolution fusion | flops 2418278400 | bytes 8650752 | tf_op jit(solution)/shard_map/dot_general | solution.py:519
  140.8 3.9 %hidden_back.1 = (bf16[512,3072]{1,0:T(8,128)(2,1)S(1)}, f32[1,3072]{1,0:T(1,128)S(1)}) custom-call(bf16[512,768]{1,0:T(8,128)(2,1)S(1)} %get-tuple-element.298.df_ref, bf16[3072,768]{1,0:T(8,128)(2,1)S(1)} %bitcast.169, bf16[512,3072]{1,0:T(8,128)(2,1)S(1)} %get-tuple-element.410.slope_ref), custom_call_target="tpu_custom_call" | custom-call | flops 40000000000 | bytes 1000000 | tf_op jit(solution)/shard_map/hidden_back/pallas_call | solution.py:614
  146.9 5.0 %convolution_convert_fusion = bf16[768,3072]{1,0:T(8,128)(2,1)S(1)} fusion(bf16[512,3072]{1,0:T(8,128)(2,1)} %copy-done.35, f32[512,768]{1,0:T(8,128)S(1)} %get-tuple-element.418.r2_ref, f32[768]{0:T(1024)S(1)} %get-tuple-element.399, f32[768]{0:T(1024)S(1)} %get-tuple-element.396, f32[512]{0:T(512)S(1)} %add_rsqrt_fusion.1, f32[512]{0:T(512)S(1)} %broadcast_multiply_fusion.2), kind=kOutput, calls=%fused_computation.8 | convolution fusion | flops 2420244480 | bytes 9447424 | tf_op jit(solution)/shard_map/dot_general | solution.py:519
  153.8 5.1 %expand_back.1 = (f32[512,768]{1,0:T(8,128)S(1)}, bf16[512,768]{1,0:T(8,128)(2,1)S(1)}, f32[8,768]{1,0:T(8,128)S(1)}) custom-call(bf16[512,3072]{1,0:T(8,128)(2,1)S(1)} %copy-done.36, bf16[768,3072]{1,0:T(8,128)(2,1)S(1)} %bitcast.167, f32[512,768]{1,0:T(8,128)S(1)} %get-tuple-element.409.dr3_ref, f32[512,768]{1,0:T(8,128)S(1)} %get-tuple-element.418.r2_ref, ...), custom_call_target="tpu_custom_call" | custom-call | flops 40000000000 | bytes 1000000 | tf_op jit(solution)/shard_map/expand_back/pallas_call | solution.py:660
  168.3 8.6 %cross_back.1 = (bf16[768,768]{1,0:T(8,128)(2,1)S(1)}, bf16[768,768]{1,0:T(8,128)(2,1)S(1)}, bf16[768,768]{1,0:T(8,128)(2,1)S(1)}, bf16[768,768]{1,0:T(8,128)(2,...) custom-call(bf16[512,768]{1,0:T(8,128)(2,1)S(1)} %get-tuple-element., ...), custom_call_target="tpu_custom_call" | custom-call | flops 40000000000 | bytes 1000000 | tf_op jit(solution)/shard_map/cross_back/pallas_call | solution.py:762
  185.6 6.2 %self_back.1 = (bf16[768,768]{1,0:T(8,128)(2,1)S(1)}, bf16[768,768]{1,0:T(8,128)(2,1)S(1)}, bf16[768,768]{1,0:T(8,128)(2,1)S(1)}, bf16[512,768]{1,0:T(8,128)(2,1...) custom-call(bf16[512,768]{1,0:T(8,128)(2,1)S(1)} %get-tuple-element.319.da_ref, ...), custom_call_target="tpu_custom_call" | custom-call | flops 40000000000 | bytes 1000000 | tf_op jit(solution)/shard_map/self_back/pallas_call | solution.py:819
  202.2 3.8 %collective-permute-done.44.refs_6_.refs_14_.refs_22_.refs_30_ = bf16[2,4,120,768]{3,2,1,0:T(8,128)(2,1)S(1)} collective-permute-done((bf16[2,4,120,768]{3,2,1,0:T(8,128)(2,1)S(1)}, bf16[2,4,120,768]{3,2,1,0:T(8,128)(2,1)S(1)}, u32[]{:S(2)}, u32[]{:S(2)}) %collective-permute-start.44) | collective-permute-done | bytes 1474592 | tf_op jit(solution)/shard_map/ppermute | solution.py:73
  210.0 3.2 %rows_back.3 = f32[512,768]{1,0:T(8,128)} custom-call(bf16[512,768]{1,0:T(8,128)(2,1)S(1)} %get-tuple-element.356.refs_0_, bf16[512,768]{1,0:T(8,128)(2,1)S(1)} %get-tuple-element.357.refs_1_, bf16[512,768]{1,0:T(8,128)(2,1)S(1)} %get-tuple-element.358.refs_2_, bf16[768,768]{1,0:T(8,128)(2,1)S(1)} %bitcast.172, bf16[768,768]{1,0:T(8,128)(2,1)S(1)} %bitcast.174, ...), custom_call_target="tpu_custom_call" | custom-call | flops 40000000000 | bytes 1000000 | tf_op jit(solution)/shard_map/rows_back/pallas_call | solution.py:842
  213.2 5.9 %collective-permute-done.45.refs_7_.refs_15_.refs_23_.refs_31_ = bf16[1,4,120,768]{3,2,1,0:T(8,128)(2,1)S(1)} collective-permute-done((bf16[1,4,120,768]{3,2,1,0:T(8,128)(2,1)S(1)}, bf16[1,4,120,768]{3,2,1,0:T(8,128)(2,1)S(1)}, u32[]{:S(2)}, u32[]{:S(2)}) %collective-permute-start.45) | collective-permute-done | bytes 737312 | tf_op jit(solution)/shard_map/ppermute | solution.py:73
  227.1 7.1 %collective-permute-done.50.refs_5_.refs_12_.refs_19_.refs_26_ = bf16[2,4,80,768]{3,2,1,0:T(8,128)(2,1)S(1)} collective-permute-done((bf16[2,4,80,768]{3,2,1,0:T(8,128)(2,1)S(1)}, bf16[2,4,80,768]{3,2,1,0:T(8,128)(2,1)S(1)}, u32[]{:S(2)}, u32[]{:S(2)}) %collective-permute-start.50) | collective-permute-done | bytes 983072 | tf_op jit(solution)/shard_map/ppermute | solution.py:73
  239.3 4.6 %collective-permute-done.51.refs_6_.refs_13_.refs_20_.refs_27_ = bf16[1,4,80,768]{3,2,1,0:T(8,128)(2,1)S(1)} collective-permute-done((bf16[1,4,80,768]{3,2,1,0:T(8,128)(2,1)S(1)}, bf16[1,4,80,768]{3,2,1,0:T(8,128)(2,1)S(1)}, u32[]{:S(2)}, u32[]{:S(2)}) %collective-permute-start.51) | collective-permute-done | bytes 491552 | tf_op jit(solution)/shard_map/ppermute | solution.py:73
  249.0 3.1 %collective-permute-done.52.refs_1_ = bf16[80,768]{1,0:T(8,128)(2,1)S(1)} collective-permute-done((bf16[80,768]{1,0:T(8,128)(2,1)S(1)}, bf16[80,768]{1,0:T(8,128)(2,1)S(1)}, u32[]{:S(2)}, u32[]{:S(2)}) %collective-permute-start.52) | collective-permute-done | bytes 122912 | tf_op jit(solution)/shard_map/ppermute | solution.py:73
  (246 shorter events, 127.7 us)
Async XLA Ops:
  21.8 18.1 %collective-permute-start.4 = (bf16[4,104,768]{2,1,0:T(8,128)(2,1)S(1)}, bf16[4,104,768]{2,1,0:T(8,128)(2,1)S(1)}, u32[]{:S(2)}, u32[]{:S(2)}) collective-permute-start(bf16[4,104,768]{2,1,0:T(8,128)(2,1)S(1)} %column.4.refs_0_), channel_id=1, source_target_pairs={{0,8},{1,17},{2,10},{3,19},{4,12},{5,21},{6,14},{7,23},{8,0},{9,25... | collective-permute-start | bytes 1916936 | tf_op jit(solution)/shard_map/ppermute | solution.py:73
  23.3 16.6 %collective-permute-start.3 = (bf16[4,104,768]{2,1,0:T(8,128)(2,1)S(1)}, bf16[4,104,768]{2,1,0:T(8,128)(2,1)S(1)}, u32[]{:S(2)}, u32[]{:S(2)}) collective-permute-start(bf16[4,104,768]{2,1,0:T(8,128)(2,1)S(1)} %column.4.refs_0_), channel_id=1, source_target_pairs={{0,16},{1,9},{2,18},{3,11},{4,20},{5,13},{6,22},{7,15},{8,24},{9,1... | collective-permute-start | bytes 1916936 | tf_op jit(solution)/shard_map/ppermute | solution.py:73
  39.9 23.1 %collective-permute-start.8 = (bf16[4,104,768]{2,1,0:T(8,128)(2,1)S(1)}, bf16[4,104,768]{2,1,0:T(8,128)(2,1)S(1)}, u32[]{:S(2)}, u32[]{:S(2)}) collective-permute-start(bf16[4,104,768]{2,1,0:T(8,128)(2,1)S(1)} %collective-permute-done.3.refs_1_), channel_id=1, source_target_pairs={{0,8},{1,17},{2,10},{3,19},{4,12},{5,21},{6,14},{7,23},{8,0},{9,25... | collective-permute-start | bytes 1916936 | tf_op jit(solution)/shard_map/ppermute | solution.py:73
  41.8 21.2 %collective-permute-start.10 = (bf16[4,96,768]{2,1,0:T(8,128)(2,1)S(1)}, bf16[4,96,768]{2,1,0:T(8,128)(2,1)S(1)}, u32[]{:S(2)}, u32[]{:S(2)}) collective-permute-start(bf16[4,96,768]{2,1,0:T(8,128)(2,1)S(1)} %column.5.refs_0_), channel_id=1, source_target_pairs={{0,8},{1,17},{2,10},{3,19},{4,12},{5,21},{6,14},{7,23},{8,0},{9,25... | collective-permute-start | bytes 1769480 | tf_op jit(solution)/shard_map/ppermute | solution.py:73
  43.4 19.6 %collective-permute-start.9 = (bf16[4,96,768]{2,1,0:T(8,128)(2,1)S(1)}, bf16[4,96,768]{2,1,0:T(8,128)(2,1)S(1)}, u32[]{:S(2)}, u32[]{:S(2)}) collective-permute-start(bf16[4,96,768]{2,1,0:T(8,128)(2,1)S(1)} %column.5.refs_0_), channel_id=1, source_target_pairs={{0,16},{1,9},{2,18},{3,11},{4,20},{5,13},{6,22},{7,15},{8,24},{9,1... | collective-permute-start | bytes 1769480 | tf_op jit(solution)/shard_map/ppermute | solution.py:73
  43.9 14.8 %collective-permute-start.12 = (bf16[24,3072]{1,0:T(8,128)(2,1)S(1)}, bf16[24,3072]{1,0:T(8,128)(2,1)S(1)}, u32[]{:S(2)}, u32[]{:S(2)}) collective-permute-start(bf16[24,3072]{1,0:T(8,128)(2,1)S(1)} %copy-done.8), channel_id=1, source_target_pairs={{0,4},{1,5},{2,6},{3,7},{4,0},{5,1},{6,2},{7,3},{8,12},{9,13},{10,... | collective-permute-start | bytes 442376 | tf_op jit(solution)/shard_map/ppermute | solution.py:73
  65.9 15.8 %collective-permute-start.18 = (bf16[96,768]{1,0:T(8,128)(2,1)S(1)}, bf16[96,768]{1,0:T(8,128)(2,1)S(1)}, u32[]{:S(2)}, u32[]{:S(2)}) collective-permute-start(bf16[96,768]{1,0:T(8,128)(2,1)S(1)} %copy-done.9), channel_id=1, source_target_pairs={{0,4},{1,5},{2,6},{3,7},{4,0},{5,1},{6,2},{7,3},{8,12},{9,13},{10,... | collective-permute-start | bytes 442376 | tf_op jit(solution)/shard_map/ppermute | solution.py:73
  67.4 15.9 %collective-permute-start.15 = (bf16[4,24,3072]{2,1,0:T(8,128)(2,1)S(1)}, bf16[4,24,3072]{2,1,0:T(8,128)(2,1)S(1)}, u32[]{:S(2)}, u32[]{:S(2)}) collective-permute-start(bf16[4,24,3072]{2,1,0:T(8,128)(2,1)S(1)} %column.6.refs_0_), channel_id=1, source_target_pairs={{0,16},{1,9},{2,18},{3,11},{4,20},{5,13},{6,22},{7,15},{8,24},{9,1... | collective-permute-start | bytes 1769480 | tf_op jit(solution)/shard_map/ppermute | solution.py:73
  67.9 14.8 %collective-permute-start.16 = (bf16[4,24,3072]{2,1,0:T(8,128)(2,1)S(1)}, bf16[4,24,3072]{2,1,0:T(8,128)(2,1)S(1)}, u32[]{:S(2)}, u32[]{:S(2)}) collective-permute-start(bf16[4,24,3072]{2,1,0:T(8,128)(2,1)S(1)} %column.6.refs_0_), channel_id=1, source_target_pairs={{0,8},{1,17},{2,10},{3,19},{4,12},{5,21},{6,14},{7,23},{8,0},{9,25... | collective-permute-start | bytes 1769480 | tf_op jit(solution)/shard_map/ppermute | solution.py:73
  70.6 18.4 %collective-permute-start.14 = (bf16[4,96,768]{2,1,0:T(8,128)(2,1)S(1)}, bf16[4,96,768]{2,1,0:T(8,128)(2,1)S(1)}, u32[]{:S(2)}, u32[]{:S(2)}) collective-permute-start(bf16[4,96,768]{2,1,0:T(8,128)(2,1)S(1)} %collective-permute-done.9.refs_1_), channel_id=1, source_target_pairs={{0,8},{1,17},{2,10},{3,19},{4,12},{5,21},{6,14},{7,23},{8,0},{9,25... | collective-permute-start | bytes 1769480 | tf_op jit(solution)/shard_map/ppermute | solution.py:73
  92.2 16.2 %collective-permute-start.22 = (bf16[4,96,768]{2,1,0:T(8,128)(2,1)S(1)}, bf16[4,96,768]{2,1,0:T(8,128)(2,1)S(1)}, u32[]{:S(2)}, u32[]{:S(2)}) collective-permute-start(bf16[4,96,768]{2,1,0:T(8,128)(2,1)S(1)} %column.7.refs_0_), channel_id=1, source_target_pairs={{0,16},{1,9},{2,18},{3,11},{4,20},{5,13},{6,22},{7,15},{8,24},{9,1... | collective-permute-start | bytes 1769480 | tf_op jit(solution)/shard_map/ppermute | solution.py:73
  92.7 14.8 %collective-permute-start.23 = (bf16[4,96,768]{2,1,0:T(8,128)(2,1)S(1)}, bf16[4,96,768]{2,1,0:T(8,128)(2,1)S(1)}, u32[]{:S(2)}, u32[]{:S(2)}) collective-permute-start(bf16[4,96,768]{2,1,0:T(8,128)(2,1)S(1)} %column.7.refs_0_), channel_id=1, source_target_pairs={{0,8},{1,17},{2,10},{3,19},{4,12},{5,21},{6,14},{7,23},{8,0},{9,25... | collective-permute-start | bytes 1769480 | tf_op jit(solution)/shard_map/ppermute | solution.py:73
  93.6 20.2 %collective-permute-start.21 = (bf16[4,24,3072]{2,1,0:T(8,128)(2,1)S(1)}, bf16[4,24,3072]{2,1,0:T(8,128)(2,1)S(1)}, u32[]{:S(2)}, u32[]{:S(2)}) collective-permute-start(bf16[4,24,3072]{2,1,0:T(8,128)(2,1)S(1)} %collective-permute-done.15.refs_1_), channel_id=1, source_target_pairs={{0,8},{1,17},{2,10},{3,19},{4,12},{5,21},{6,14},{7,23},{8,0},{9,25... | collective-permute-start | bytes 1769480 | tf_op jit(solution)/shard_map/ppermute | solution.py:73
  146.4 16.2 %collective-permute-start.32 = (bf16[2,4,96,768]{3,2,1,0:T(8,128)(2,1)S(1)}, bf16[2,4,96,768]{3,2,1,0:T(8,128)(2,1)S(1)}, u32[]{:S(2)}, u32[]{:S(2)}) collective-permute-start(bf16[2,4,96,768]{3,2,1,0:T(8,128)(2,1)S(1)} %leave.7), channel_id=1, source_target_pairs={{0,16},{1,9},{2,18},{3,11},{4,20},{5,13},{6,22},{7,15},{8,24},{9,1... | collective-permute-start | bytes 3538952 | tf_op jit(solution)/shard_map/ppermute | solution.py:73
  160.0 18.4 %collective-permute-start.34 = (bf16[2,4,24,3072]{3,2,1,0:T(8,128)(2,1)S(1)}, bf16[2,4,24,3072]{3,2,1,0:T(8,128)(2,1)S(1)}, u32[]{:S(2)}, u32[]{:S(2)}) collective-permute-start(bf16[2,4,24,3072]{3,2,1,0:T(8,128)(2,1)S(1)} %leave.8), channel_id=1, source_target_pairs={{0,16},{1,9},{2,18},{3,11},{4,20},{5,13},{6,22},{7,15},{8,24},{9,1... | collective-permute-start | bytes 3538952 | tf_op jit(solution)/shard_map/ppermute | solution.py:73
  163.6 30.8 %collective-permute-start.36 = (bf16[2,96,768]{2,1,0:T(8,128)(2,1)S(1)}, bf16[2,96,768]{2,1,0:T(8,128)(2,1)S(1)}, u32[]{:S(2)}, u32[]{:S(2)}) collective-permute-start(bf16[2,96,768]{2,1,0:T(8,128)(2,1)S(1)} %get-tuple-element.324), channel_id=1, source_target_pairs={{0,2},{1,3},{2,4},{3,5},{4,6},{5,7},{6,0},{7,1},{8,10},{9,11},{10,... | collective-permute-start | bytes 884744 | tf_op jit(solution)/shard_map/ppermute | solution.py:73
  165.4 31.2 %collective-permute-start.37 = (bf16[2,96,768]{2,1,0:T(8,128)(2,1)S(1)}, bf16[2,96,768]{2,1,0:T(8,128)(2,1)S(1)}, u32[]{:S(2)}, u32[]{:S(2)}) collective-permute-start(bf16[2,96,768]{2,1,0:T(8,128)(2,1)S(1)} %get-tuple-element.325), channel_id=1, source_target_pairs={{0,4},{1,5},{2,6},{3,7},{4,0},{5,1},{6,2},{7,3},{8,12},{9,13},{10,... | collective-permute-start | bytes 884744 | tf_op jit(solution)/shard_map/ppermute | solution.py:73
  166.3 32.3 %collective-permute-start.38 = (bf16[2,96,768]{2,1,0:T(8,128)(2,1)S(1)}, bf16[2,96,768]{2,1,0:T(8,128)(2,1)S(1)}, u32[]{:S(2)}, u32[]{:S(2)}) collective-permute-start(bf16[2,96,768]{2,1,0:T(8,128)(2,1)S(1)} %get-tuple-element.326), channel_id=1, source_target_pairs={{0,6},{1,7},{2,0},{3,1},{4,2},{5,3},{6,4},{7,5},{8,14},{9,15},{10,... | collective-permute-start | bytes 884744 | tf_op jit(solution)/shard_map/ppermute | solution.py:73
  185.0 21.0 %collective-permute-start.44 = (bf16[2,4,120,768]{3,2,1,0:T(8,128)(2,1)S(1)}, bf16[2,4,120,768]{3,2,1,0:T(8,128)(2,1)S(1)}, u32[]{:S(2)}, u32[]{:S(2)}) collective-permute-start(bf16[2,4,120,768]{3,2,1,0:T(8,128)(2,1)S(1)} %leave.10), channel_id=1, source_target_pairs={{0,16},{1,9},{2,18},{3,11},{4,20},{5,13},{6,22},{7,15},{8,24},{9,1... | collective-permute-start | bytes 4423688 | tf_op jit(solution)/shard_map/ppermute | solution.py:73
  192.7 14.8 %collective-permute-start.41 = (bf16[24,3072]{1,0:T(8,128)(2,1)S(1)}, bf16[24,3072]{1,0:T(8,128)(2,1)S(1)}, u32[]{:S(2)}, u32[]{:S(2)}) collective-permute-start(bf16[24,3072]{1,0:T(8,128)(2,1)S(1)} %get-tuple-element.344), channel_id=1, source_target_pairs={{0,2},{1,3},{2,4},{3,5},{4,6},{5,7},{6,0},{7,1},{8,10},{9,11},{10,... | collective-permute-start | bytes 442376 | tf_op jit(solution)/shard_map/ppermute | solution.py:73
  194.4 14.0 %collective-permute-start.42 = (bf16[24,3072]{1,0:T(8,128)(2,1)S(1)}, bf16[24,3072]{1,0:T(8,128)(2,1)S(1)}, u32[]{:S(2)}, u32[]{:S(2)}) collective-permute-start(bf16[24,3072]{1,0:T(8,128)(2,1)S(1)} %get-tuple-element.345), channel_id=1, source_target_pairs={{0,4},{1,5},{2,6},{3,7},{4,0},{5,1},{6,2},{7,3},{8,12},{9,13},{10,... | collective-permute-start | bytes 442376 | tf_op jit(solution)/shard_map/ppermute | solution.py:73
  220.1 14.2 %collective-permute-start.50 = (bf16[2,4,80,768]{3,2,1,0:T(8,128)(2,1)S(1)}, bf16[2,4,80,768]{3,2,1,0:T(8,128)(2,1)S(1)}, u32[]{:S(2)}, u32[]{:S(2)}) collective-permute-start(bf16[2,4,80,768]{3,2,1,0:T(8,128)(2,1)S(1)} %leave.12), channel_id=1, source_target_pairs={{0,16},{1,9},{2,18},{3,11},{4,20},{5,13},{6,22},{7,15},{8,24},{9,1... | collective-permute-start | bytes 2949128 | tf_op jit(solution)/shard_map/ppermute | solution.py:73
  221.5 14.4 %collective-permute-start.47 = (bf16[120,768]{1,0:T(8,128)(2,1)S(1)}, bf16[120,768]{1,0:T(8,128)(2,1)S(1)}, u32[]{:S(2)}, u32[]{:S(2)}) collective-permute-start(bf16[120,768]{1,0:T(8,128)(2,1)S(1)} %get-tuple-element.365), channel_id=1, source_target_pairs={{0,2},{1,3},{2,4},{3,5},{4,6},{5,7},{6,0},{7,1},{8,10},{9,11},{10,... | collective-permute-start | bytes 552968 | tf_op jit(solution)/shard_map/ppermute | solution.py:73
  222.0 15.4 %collective-permute-start.48 = (bf16[120,768]{1,0:T(8,128)(2,1)S(1)}, bf16[120,768]{1,0:T(8,128)(2,1)S(1)}, u32[]{:S(2)}, u32[]{:S(2)}) collective-permute-start(bf16[120,768]{1,0:T(8,128)(2,1)S(1)} %get-tuple-element.366), channel_id=1, source_target_pairs={{0,4},{1,5},{2,6},{3,7},{4,0},{5,1},{6,2},{7,3},{8,12},{9,13},{10,... | collective-permute-start | bytes 552968 | tf_op jit(solution)/shard_map/ppermute | solution.py:73
  (73 other events, 554.4 us)
